TPU v7x, 32 devices: a whole 2x2x4 slice. The times are simulated.
32 devices in a mesh: member: 2 (over y), lon: 8 (over z, x), lat: 2 (over core).
Axes of the slice: x: 2, y: 2, z: 4, core: 2. Of those that a mesh axis runs over, the one named last changes fastest.
Arguments:
- fields: bfloat16 [1280, 32, 128], P('member', 'lat', 'lon'), parts along dimension 0, may hold values from -6 to 6
- support_rows: int32 [7, 32, 16], replicated, may hold values from -1 to 1
- support_lons: int32 [7, 32, 16], replicated, may hold values from -64 to 64, as said below
- support_weights: float32 [7, 32, 16], replicated, may hold values from -1.5 to 1.5
- mix_weight: bfloat16 [7, 640, 640], replicated, may hold values from -0.09375 to 0.09375
- norm_gain: float32 [640], replicated, may hold values from 0.1 to 1.9
- up_weight: bfloat16 [640, 1280], replicated, may hold values from -0.25 to 0.25
- down_weight: bfloat16 [1280, 640], replicated, may hold values from -0.15625 to 0.15625
Outputs:
- output: bfloat16 [1280, 32, 128], P('member', 'lat', 'lon'), parts along dimension 0
There are 2 independent parts, one for each index of `member`. A program takes and returns all parts, laid end to end along the dimension named above; an argument that names none is the same for every part. Nothing has to cross between parts.
Inputs may be any that keep to these rules, and one draw needn't show every extreme that they name: `support_lons`: at output row i every offset lies within plus or minus min(64, 4 * 32 // min(i + 1, 32 - i)); in every basis filter the first pole row has an entry at -(64) and the last pole row one at 64.
All inputs are finite; a program needn't handle non-finite values.
Results may differ from a plain program's by a relative error of at most 0.0095.
Values may be sent and summed in bfloat16 or wider, within the bound.
No kernel may reach another device: no remote copies, remote signals or barrier semaphores. Data moves between devices by JAX's collectives and lax.ppermute only.
A program may use at most 128 MiB of HBM per device.

v0:
```python
import math

import jax
import jax.numpy as jnp
from jax import lax
from jax.sharding import PartitionSpec as P

full_turn = 2.0 * math.pi
norm_eps = 1e-05


def extended(block, sides, width):
    for axis, dim in sides:
        count = lax.axis_size(axis)
        forward = [(i, i + 1) for i in range(count - 1)]
        backward = [(target, source) for source, target in forward]
        low = lax.ppermute(
            lax.slice_in_dim(block, block.shape[dim] - width, None, axis=dim), axis, forward
        )
        high = lax.ppermute(lax.slice_in_dim(block, 0, width, axis=dim), axis, backward)
        block = jnp.concatenate([low, block, high], axis=dim)
    return block


def transform_tables(lon_total):
    lon_half = lon_total // 2
    column = lax.broadcasted_iota(jnp.int32, (lon_total, lon_total), 1)
    sample = lax.broadcasted_iota(jnp.int32, (lon_total, lon_total), 0)
    cos_freq = jnp.where(column == 1, lon_half, column // 2)
    sin_freq = column // 2
    cos_angle = jnp.mod(sample * cos_freq, lon_total).astype(jnp.float32) * (full_turn / lon_total)
    sin_angle = jnp.mod(sample * sin_freq, lon_total).astype(jnp.float32) * (full_turn / lon_total)
    odd_column = (jnp.mod(column, 2) == 1) & (column != 1)
    forward = jnp.where(odd_column, jnp.sin(sin_angle), jnp.cos(cos_angle))
    column_ids = jnp.arange(lon_total, dtype=jnp.int32)
    weight_col = jnp.where(column_ids <= 1, 1.0, 2.0).astype(jnp.float32) / lon_total
    inverse = forward.T * weight_col[:, None]
    return (forward, inverse)


def partner(spectrum):
    pairs = spectrum.reshape(spectrum.shape[:-1] + (spectrum.shape[-1] // 2, 2))
    swapped = jnp.stack([pairs[..., 1], -pairs[..., 0]], axis=-1)
    return swapped.reshape(spectrum.shape)


def filter_spectra(row_offsets, lon_offsets, weights, columns, lon_total):
    lon_half = lon_total // 2
    cos_freq = jnp.where(columns == 1, lon_half, columns // 2)
    sin_freq = columns // 2
    cos_angle = jnp.mod(lon_offsets[..., None] * cos_freq, lon_total).astype(jnp.float32) * (
        full_turn / lon_total
    )
    sin_angle = jnp.mod(lon_offsets[..., None] * sin_freq, lon_total).astype(jnp.float32) * (
        full_turn / lon_total
    )
    offsets = jnp.array([-1, 0, 1], jnp.int32)
    picked = jnp.where(row_offsets[..., None] == offsets, weights[..., None], 0.0)
    direct = jnp.einsum(
        "kisr,kisn->kirn", picked, jnp.cos(cos_angle), precision=lax.Precision.HIGHEST
    )
    cross_part = jnp.einsum(
        "kisr,kisn->kirn", picked, jnp.sin(sin_angle), precision=lax.Precision.HIGHEST
    )
    return (direct, cross_part)


def spectral_product(spectrum, direct, cross_part, rows_out):
    mirrored = partner(spectrum)
    summed = None
    for position in range(3):
        shifted_spec = spectrum[:, position : position + rows_out]
        shifted_pair = mirrored[:, position : position + rows_out]
        piece = (
            shifted_spec[None] * direct[:, None, :, position]
            + shifted_pair[None] * cross_part[:, None, :, position]
        )
        summed = piece if summed is None else summed + piece
    return summed


def filtered(spectrum, columns, support_rows, support_lons, support_weights, row_start, lon_total):
    lat_rows = spectrum.shape[1]
    padded_rows = jnp.pad(support_rows, ((0, 0), (1, 1), (0, 0)))
    padded_lons = jnp.pad(support_lons, ((0, 0), (1, 1), (0, 0)))
    padded_weights = jnp.pad(support_weights, ((0, 0), (1, 1), (0, 0)))
    widened = jnp.pad(spectrum.astype(jnp.float32), ((0, 0), (2, 2), (0, 0)))
    row_sel = lax.dynamic_slice_in_dim(padded_rows, row_start, lat_rows + 2, 1)
    lon_sel = lax.dynamic_slice_in_dim(padded_lons, row_start, lat_rows + 2, 1)
    weight_sel = lax.dynamic_slice_in_dim(padded_weights, row_start, lat_rows + 2, 1)
    direct, cross_part = filter_spectra(row_sel, lon_sel, weight_sel, columns, lon_total)
    product_all = spectral_product(widened, direct, cross_part, lat_rows + 2)
    edge_terms = jnp.concatenate([product_all[:, :, :1], product_all[:, :, lat_rows + 1 :]], axis=2)
    framed = extended(edge_terms.astype(jnp.bfloat16), (("lat", 2),), 1).astype(edge_terms.dtype)
    from_above = jnp.pad(framed[:, :, 0:1], ((0, 0), (0, 0), (0, lat_rows - 1), (0, 0)))
    from_below = jnp.pad(framed[:, :, 3:4], ((0, 0), (0, 0), (lat_rows - 1, 0), (0, 0)))
    product = product_all[:, :, 1 : lat_rows + 1] + from_above + from_below
    return product.astype(jnp.bfloat16)


def on_device(
    fields,
    support_rows,
    support_lons,
    support_weights,
    mix_weight,
    norm_gain,
    up_weight,
    down_weight,
):
    channels, lat_rows, lon_cols = fields.shape
    moved = lax.all_to_all(fields, "lon", split_axis=0, concat_axis=2, tiled=True)
    local_channels = moved.shape[0]
    lon_total = moved.shape[2]
    forward, inverse = transform_tables(lon_total)
    row_start = lax.axis_index("lat") * lat_rows
    spectrum = jnp.dot(
        moved.reshape(-1, lon_total),
        forward,
        precision=lax.Precision.HIGH,
        preferred_element_type=jnp.float32,
    )
    spectrum = spectrum.reshape(local_channels, lat_rows, lon_total).astype(jnp.bfloat16)
    bands = lax.all_to_all(spectrum, "lon", split_axis=2, concat_axis=0, tiled=True)
    columns = lax.axis_index("lon") * lon_cols + jnp.arange(lon_cols, dtype=jnp.int32)
    product = filtered(
        bands, columns, support_rows, support_lons, support_weights, row_start, lon_total
    )
    mixed_spec = lax.dot_general(
        mix_weight.reshape(-1, channels),
        product.reshape(-1, lat_rows * lon_cols),
        (((0,), (0,)), ((), ())),
        preferred_element_type=jnp.float32,
    )
    mixed_spec = mixed_spec.reshape(channels, lat_rows, lon_cols)
    gathered_spec = lax.all_to_all(
        mixed_spec.astype(jnp.bfloat16), "lon", split_axis=0, concat_axis=2, tiled=True
    ).astype(mixed_spec.dtype)
    spatial = jnp.dot(
        gathered_spec.reshape(-1, lon_total),
        inverse,
        precision=lax.Precision.HIGHEST,
        preferred_element_type=jnp.float32,
    )
    spatial = spatial.reshape(local_channels, lat_rows, lon_total)
    mixed = (
        lax.all_to_all(spatial.astype(jnp.bfloat16), "lon", split_axis=2, concat_axis=0, tiled=True)
        .astype(spatial.dtype)
        .reshape(channels, lat_rows * lon_cols)
    )
    latent = fields.reshape(channels, lat_rows * lon_cols).astype(jnp.float32) + mixed
    row_mean = jnp.mean(latent, axis=0)
    variance = jnp.mean(jnp.square(latent - row_mean), axis=0)
    normed = ((latent - row_mean) * lax.rsqrt(variance + norm_eps) * norm_gain[:, None]).astype(
        jnp.bfloat16
    )
    hidden = jax.nn.gelu(
        lax.dot_general(
            up_weight, normed, (((0,), (0,)), ((), ())), preferred_element_type=jnp.float32
        ),
        approximate=False,
    ).astype(jnp.bfloat16)
    output = latent + lax.dot_general(
        down_weight, hidden, (((0,), (0,)), ((), ())), preferred_element_type=jnp.float32
    )
    return output.astype(jnp.bfloat16).reshape(channels, lat_rows, lon_cols)


def solution(mesh):
    in_specs = (P("member", "lat", "lon"), P(), P(), P(), P(), P(), P(), P())
    out_specs = P("member", "lat", "lon")
    return jax.shard_map(
        on_device, mesh=mesh, in_specs=in_specs, out_specs=out_specs, check_vma=False
    )
```

profile of v0, /device:TPU:0, one launch (start us, length us, event | category | flops | bytes accessed | tf_op | source)
XLA Modules:
  0.0 136.8 jit_solution(329501171711781699)
XLA Ops:
  0.0 3.7 %copy.90 = bf16[640,16,16]{2,1,0:T(8,128)(2,1)} copy(bf16[640,16,16]{0,2,1:T(8,128)(2,1)} %param.9) | data formatting | bytes 655360 | tf_op args[0]
  3.7 5.1 %reshape.133 = bf16[8,2,10240]{2,1,0:T(2,128)(2,1)} reshape(bf16[640,16,16]{2,1,0:T(8,128)(2,1)} %copy.90) | data formatting | bytes 655360
  8.8 7.4 %all-to-all-start = ((bf16[8,2,10240]{2,1,0:T(2,128)(2,1)}), bf16[8,2,10240]{2,1,0:T(2,128)(2,1)S(1)}, u32[]{:S(2)}, u32[]{:S(2)}) async-start(bf16[8,2,10240]{2,1,0:T(2,128)(2,1)} %reshape.133), calls=%async_computation | async-start | bytes 655360 | tf_op jit(solution)/shard_map/all_to_all | solution.py:112
  16.8 5.3 %fusion.26 = f32[7,18,3,16]{3,2,1,0:T(4,128)S(1)} fusion(s32[16]{0:T(128)S(1)} %get-tuple-element.26, s32[7,18,16]{2,1,0:T(8,128)S(1)} %copy.98, f32[7,18,16]{2,1,0:T(8,128)S(1)} %copy.97, s32[7,18,16]{2,1,0:T(8,128)S(1)} %copy.96, s32[3]{0:T(128)S(1)} %copy-done.15), kind=kOutput, calls=%fused_computation.50 | convolution fusion | flops 1624896 | bytes 48460 | tf_op jit(solution)/shard_map/kisr,kisn->kirn/dot_general | solution.py:59
  22.1 4.3 %all-to-all-done = bf16[8,2,10240]{2,1,0:T(2,128)(2,1)S(1)} async-done(((bf16[8,2,10240]{2,1,0:T(2,128)(2,1)}), bf16[8,2,10240]{2,1,0:T(2,128)(2,1)S(1)}, u32[]{:S(2)}, u32[]{:S(2)}) %all-to-all-start) | async-done | bytes 327712 | tf_op jit(solution)/shard_map/all_to_all | solution.py:112
  26.5 2.9 %reshape.134 = bf16[640,16,16]{2,1,0:T(8,128)(2,1)} reshape(bf16[8,2,10240]{2,1,0:T(2,128)(2,1)S(1)} %all-to-all-done) | data formatting | bytes 655360
  29.4 6.3 %copy.130 = bf16[8,80,16,16]{3,0,2,1:T(8,128)(2,1)} copy(bf16[8,80,16,16]{3,2,1,0:T(8,128)(2,1)} %bitcast.142) | data formatting | bytes 655360 | tf_op jit(solution)/shard_map/all_to_all | solution.py:112
  35.7 3.5 %reshape.121 = bf16[1280,128]{1,0:T(8,128)(2,1)S(1)} reshape(bf16[80,16,8,16]{3,2,1,0:T(8,128)(2,1)} %bitcast.143) | data formatting | bytes 655360 | tf_op jit(solution)/shard_map/reshape | solution.py:118
  39.2 0.9 fusion.2
  40.3 1.3 copy.93
  41.6 3.7 %all-to-all-start.1 = ((bf16[80,16,128]{0,1,2:T(8,128)(2,1)}), bf16[80,16,128]{0,1,2:T(8,128)(2,1)S(1)}, u32[]{:S(2)}, u32[]{:S(2)}) async-start(bf16[80,16,128]{0,1,2:T(8,128)(2,1)} %copy.93), calls=%async_computation.1 | async-start | bytes 1048576 | tf_op jit(solution)/shard_map/all_to_all | solution.py:124
  45.7 0.8 copy.124
  46.5 0.8 copy.120
  47.3 5.3 %fusion.31 = f32[7,18,3,16]{3,2,1,0:T(4,128)S(1)} fusion(s32[16]{0:T(128)S(1)} %get-tuple-element.25, s32[7,18,16]{2,1,0:T(8,128)S(1)} %copy.98, f32[7,18,16]{2,1,0:T(8,128)S(1)} %copy.97, s32[7,18,16]{2,1,0:T(8,128)S(1)} %copy.96, s32[3]{0:T(128)S(1)} %copy-done.15), kind=kOutput, calls=%fused_computation.54 | convolution fusion | flops 1624896 | bytes 48460 | tf_op jit(solution)/shard_map/kisr,kisn->kirn/dot_general | solution.py:62
  52.8 0.8 copy.121
  53.7 0.8 copy.123
  54.5 0.8 copy.125
  55.4 4.0 %all-to-all-done.1 = bf16[80,16,128]{0,1,2:T(8,128)(2,1)S(1)} async-done(((bf16[80,16,128]{0,1,2:T(8,128)(2,1)}), bf16[80,16,128]{0,1,2:T(8,128)(2,1)S(1)}, u32[]{:S(2)}, u32[]{:S(2)}) %all-to-all-start.1) | async-done | bytes 327712 | tf_op jit(solution)/shard_map/all_to_all | solution.py:124
  59.3 0.3 copy.95
  59.7 0.4 convert_element_type.115
  60.1 0.5 reshape.122
  60.6 1.5 %fusion.230 = (f32[640,18,16]{0,2,1:T(8,128)}, f32[640,18,16]{0,2,1:T(8,128)}, f32[640,18,16]{0,2,1:T(8,128)}) fusion(f32[640,20,16]{0,2,1:T(8,128)S(1)} %pad_convert_fusion), kind=kLoop, calls=%fused_computation.294 | loop fusion | bytes 4423680 | tf_op jit(solution)/shard_map/slice | solution.py:72
  62.1 0.6 fusion.232
  62.7 0.7 pad_maximum_fusion
  63.5 0.6 reshape.123
  64.3 0.9 copy-done.2
  65.8 2.9 %fusion.228 = (bf16[7,640,18,16]{1,0,3,2:T(8,128)(2,1)S(1)}, f32[7,640,18,16]{1,0,3,2:T(8,128)S(1)}) fusion(f32[7,18,16]{0,2,1:T(8,128)S(1)} %bitcast.155, f32[640,18,16]{0,2,1:T(8,128)S(1)} %get-tuple-element.13, f32[7,18,16]{0,2,1:T(8,128)S(1)} %bitcast.151, f32[640,18,16]{0,2,1:T(8,128)S(1)} %copy-done.3, f32[7,18,16]{0,2,1:T(8,128)S(1)} %bitcast.154, ...), kind=kLoop, calls=%fused_computation.292 | loop fusion | flops 15482880 | bytes 12213504 | tf_op jit(solution)/shard_map/convert.14
  68.7 1.3 collective-permute-start
  70.0 1.3 collective-permute-start.1
  71.3 2.0 %collective-permute-done.1 = bf16[7,640,1,16]{1,0,3,2:T(8,128)(2,1)S(1)} collective-permute-done((bf16[7,640,1,16]{1,0,3,2:T(8,128)(2,1)S(1)}, bf16[7,640,1,16]{1,0,3,2:T(8,128)(2,1)S(1)}, u32[]{:S(2)}, u32[]{:S(2)}) %collective-permute-start.1) | collective-permute-done | bytes 143392 | tf_op jit(solution)/shard_map/ppermute | solution.py:20
  73.4 0.4 fusion.1
  73.8 0.4 copy.128
  74.2 1.3 slice-done
  75.5 0.5 slice-done.1
  76.0 2.0 %convolution_convert_fusion.2 = bf16[256,640]{1,0:T(8,128)(2,1)S(1)} fusion(bf16[4480,256]{0,1:T(8,128)(2,1)S(1)} %bitcast.145, bf16[4480,640]{1,0:T(8,128)(2,1)S(1)} %bitcast.159), kind=kOutput, calls=%fused_computation.45 | convolution fusion | flops 1468170240 | bytes 8355840 | tf_op jit(solution)/shard_map/dot_general | solution.py:129
  78.0 2.7 %copy.111 = bf16[640,16,16]{2,1,0:T(8,128)(2,1)} copy(bf16[640,16,16]{0,2,1:T(8,128)(2,1)S(1)} %bitcast.156) | data formatting | bytes 655360 | tf_op jit(solution)/shard_map/convert_element_type | solution.py:137
  80.7 5.1 %reshape.135 = bf16[8,2,10240]{2,1,0:T(2,128)(2,1)} reshape(bf16[640,16,16]{2,1,0:T(8,128)(2,1)} %copy.111) | data formatting | bytes 655360
  85.8 3.9 %all-to-all-start.2 = ((bf16[8,2,10240]{2,1,0:T(2,128)(2,1)}), bf16[8,2,10240]{2,1,0:T(2,128)(2,1)S(1)}, u32[]{:S(2)}, u32[]{:S(2)}) async-start(bf16[8,2,10240]{2,1,0:T(2,128)(2,1)} %reshape.135), calls=%async_computation.2 | async-start | bytes 655360 | tf_op jit(solution)/shard_map/all_to_all | solution.py:136
  89.7 10.6 %all-to-all-done.2 = bf16[8,2,10240]{2,1,0:T(2,128)(2,1)S(1)} async-done(((bf16[8,2,10240]{2,1,0:T(2,128)(2,1)}), bf16[8,2,10240]{2,1,0:T(2,128)(2,1)S(1)}, u32[]{:S(2)}, u32[]{:S(2)}) %all-to-all-start.2) | async-done | bytes 327712 | tf_op jit(solution)/shard_map/all_to_all | solution.py:136
  100.2 2.9 %reshape.136 = bf16[640,16,16]{2,1,0:T(8,128)(2,1)} reshape(bf16[8,2,10240]{2,1,0:T(2,128)(2,1)S(1)} %all-to-all-done.2) | data formatting | bytes 655360
  103.2 3.0 %copy.113 = bf16[80,16,8,16]{0,3,2,1:T(8,128)(2,1)S(1)} copy(bf16[80,16,8,16]{3,1,0,2:T(8,128)(2,1)} %bitcast.144) | data formatting | bytes 655360 | tf_op jit(solution)/shard_map/all_to_all | solution.py:136
  106.4 1.0 convolution_convert_fusion.1
  107.5 0.6 copy.115
  108.0 18.0 %all_to_all.48 = bf16[80,16,128]{0,1,2:T(8,128)(2,1)S(1)} all-to-all(bf16[80,16,128]{0,1,2:T(8,128)(2,1)S(1)} %copy.115), channel_id=1, replica_groups=mesh['member'=2,'lon'=8,'lat'=2] {'lon'}, dimensions={2} | all-to-all | bytes 655360 | tf_op jit(solution)/shard_map/all_to_all | solution.py:147
  127.0 1.2 reshape.128
  128.2 1.2 fusion.95
  129.4 1.2 multiply_reduce_fusion
  130.9 5.9 %fusion.22 = bf16[640,256]{0,1:T(8,128)(2,1)} fusion(f32[640,256]{0,1:T(8,128)S(1)} %bitcast_add_fusion, bf16[1280,640]{1,0:T(8,128)(2,1)S(1)} %copy-done, bf16[640,1280]{1,0:T(8,128)(2,1)} %param.15, f32[640]{0:T(1024)S(1)} %copy-done.14, f32[256]{0:T(256)S(1)} %rsqrt.11, f32[256]{0:T(256)S(1)} %div.44), kind=kOutput, calls=%fused_computation.43 | convolution fusion | flops 861143040 | bytes 4264448 | tf_op jit(solution)/shard_map/dot_general | solution.py:163
  (64 shorter events, 3.8 us)
Async XLA Ops:
  0.0 130.8 %copy-start = (bf16[1280,640]{1,0:T(8,128)(2,1)S(1)}, bf16[1280,640]{1,0:T(8,128)(2,1)}, u32[]{:S(2)}) copy-start(bf16[1280,640]{1,0:T(8,128)(2,1)} %param.16) | copy-start | bytes 4915204
  3.7 12.5 %copy-start.11 = (s32[7,32,16]{1,2,0:T(8,128)S(1)}, s32[7,32,16]{1,2,0:T(8,128)}, u32[]{:S(2)}) copy-start(s32[7,32,16]{1,2,0:T(8,128)} %param.11) | copy-start | bytes 43012
  3.7 12.5 %copy-start.12 = (s32[7,32,16]{1,2,0:T(8,128)S(1)}, s32[7,32,16]{1,2,0:T(8,128)}, u32[]{:S(2)}) copy-start(s32[7,32,16]{1,2,0:T(8,128)} %param.10) | copy-start | bytes 43012
  3.7 12.9 %copy-start.13 = (f32[7,32,16]{1,2,0:T(8,128)S(1)}, f32[7,32,16]{1,2,0:T(8,128)}, u32[]{:S(2)}) copy-start(f32[7,32,16]{1,2,0:T(8,128)} %param.12) | copy-start | bytes 43012
  8.8 8.0 %copy-start.15 = (s32[3]{0:T(128)S(1)}, s32[3]{0:T(128)}, u32[]{:S(2)}) copy-start(s32[3]{0:T(128)} %constant.173.clone) | copy-start | bytes 40
  8.8 17.7 %all-to-all-start = ((bf16[8,2,10240]{2,1,0:T(2,128)(2,1)}), bf16[8,2,10240]{2,1,0:T(2,128)(2,1)S(1)}, u32[]{:S(2)}, u32[]{:S(2)}) async-start(bf16[8,2,10240]{2,1,0:T(2,128)(2,1)} %reshape.133), calls=%async_computation | async-start | bytes 655360 | tf_op jit(solution)/shard_map/all_to_all | solution.py:112
  41.6 17.7 %all-to-all-start.1 = ((bf16[80,16,128]{0,1,2:T(8,128)(2,1)}), bf16[80,16,128]{0,1,2:T(8,128)(2,1)S(1)}, u32[]{:S(2)}, u32[]{:S(2)}) async-start(bf16[80,16,128]{0,1,2:T(8,128)(2,1)} %copy.93), calls=%async_computation.1 | async-start | bytes 1048576 | tf_op jit(solution)/shard_map/all_to_all | solution.py:124
  64.1 1.1 copy-start.2
  64.1 1.3 copy-start.3
  64.1 1.5 %copy-start.4 = (f32[640,18,16]{0,2,1:T(8,128)S(1)}, f32[640,18,16]{0,2,1:T(8,128)}, u32[]{:S(2)}) copy-start(f32[640,18,16]{0,2,1:T(8,128)} %get-tuple-element.11) | copy-start | bytes 2211844
  64.1 1.5 %copy-start.6 = (f32[7,18,1,16]{0,3,1,2:T(8,128)S(1)}, f32[7,18,1,16]{0,3,1,2:T(8,128)}, u32[]{:S(2)}) copy-start(f32[7,18,1,16]{0,3,1,2:T(8,128)} %copy.124) | copy-start | bytes 24196
  64.1 1.6 %copy-start.7 = (f32[7,18,1,16]{0,3,1,2:T(8,128)S(1)}, f32[7,18,1,16]{0,3,1,2:T(8,128)}, u32[]{:S(2)}) copy-start(f32[7,18,1,16]{0,3,1,2:T(8,128)} %copy.120) | copy-start | bytes 24196
  64.1 1.6 %copy-start.8 = (f32[7,18,1,16]{0,3,1,2:T(8,128)S(1)}, f32[7,18,1,16]{0,3,1,2:T(8,128)}, u32[]{:S(2)}) copy-start(f32[7,18,1,16]{0,3,1,2:T(8,128)} %copy.121) | copy-start | bytes 24196
  64.1 1.7 %copy-start.9 = (f32[7,18,1,16]{0,3,1,2:T(8,128)S(1)}, f32[7,18,1,16]{0,3,1,2:T(8,128)}, u32[]{:S(2)}) copy-start(f32[7,18,1,16]{0,3,1,2:T(8,128)} %copy.123) | copy-start | bytes 24196
  64.1 1.7 %copy-start.10 = (f32[7,18,1,16]{0,3,1,2:T(8,128)S(1)}, f32[7,18,1,16]{0,3,1,2:T(8,128)}, u32[]{:S(2)}) copy-start(f32[7,18,1,16]{0,3,1,2:T(8,128)} %copy.125) | copy-start | bytes 24196
  68.7 2.6 %collective-permute-start = (bf16[7,640,1,16]{1,0,3,2:T(8,128)(2,1)S(1)}, bf16[7,640,1,16]{1,0,3,2:T(8,128)(2,1)S(1)}, u32[]{:S(2)}, u32[]{:S(2)}) collective-permute-start(bf16[7,640,1,16]{1,0,3,2:T(8,128)(2,1)S(1)} %get-tuple-element.7), channel_id=1, source_target_pairs={{0,1},{2,3},{4,5},{6,7},{8,9},{10,11},{12,13},{14,15},{16,17},{18,... | collective-permute-start | bytes 430088 | tf_op jit(solution)/shard_map/ppermute | solution.py:17
  70.0 3.3 %collective-permute-start.1 = (bf16[7,640,1,16]{1,0,3,2:T(8,128)(2,1)S(1)}, bf16[7,640,1,16]{1,0,3,2:T(8,128)(2,1)S(1)}, u32[]{:S(2)}, u32[]{:S(2)}) collective-permute-start(bf16[7,640,1,16]{1,0,3,2:T(8,128)(2,1)S(1)} %get-tuple-element.8), channel_id=1, source_target_pairs={{1,0},{3,2},{5,4},{7,6},{9,8},{11,10},{13,12},{15,14},{17,16},{19,... | collective-permute-start | bytes 430088 | tf_op jit(solution)/shard_map/ppermute | solution.py:20
  73.3 2.2 %slice-start = ((s8[5734400]{0:T(1024)(128)(4,1)}), s8[4194304]{0:T(1024)(128)(4,1)S(1)}, s32[]{:S(2)}) async-start(s8[5734400]{0:T(1024)(128)(4,1)} %bitcast.157), calls=%async_computation.4 | async-start | bytes 8388608
  73.4 2.6 %slice-start.1 = ((s8[5734400]{0:T(1024)(128)(4,1)}), s8[1540096]{0:T(1024)(128)(4,1)S(1)}, s32[]{:S(2)}) async-start(s8[5734400]{0:T(1024)(128)(4,1)} %bitcast.157), calls=%async_computation.5 | async-start | bytes 3080192
  85.8 14.5 %all-to-all-start.2 = ((bf16[8,2,10240]{2,1,0:T(2,128)(2,1)}), bf16[8,2,10240]{2,1,0:T(2,128)(2,1)S(1)}, u32[]{:S(2)}, u32[]{:S(2)}) async-start(bf16[8,2,10240]{2,1,0:T(2,128)(2,1)} %reshape.135), calls=%async_computation.2 | async-start | bytes 655360 | tf_op jit(solution)/shard_map/all_to_all | solution.py:136
  128.2 2.6 %copy-start.1 = (bf16[640,16,16]{0,2,1:T(8,128)(2,1)S(1)}, bf16[640,16,16]{0,2,1:T(8,128)(2,1)}, u32[]{:S(2)}) copy-start(bf16[640,16,16]{0,2,1:T(8,128)(2,1)} %param.9) | copy-start | bytes 983044
  128.2 2.6 %copy-start.5 = (f32[640,256]{0,1:T(8,128)S(1)}, f32[640,256]{0,1:T(8,128)}, u32[]{:S(2)}) copy-start(f32[640,256]{0,1:T(8,128)} %reshape.128) | copy-start | bytes 1966084
  129.4 1.5 %copy-start.14 = (f32[640]{0:T(1024)S(1)}, f32[640]{0:T(1024)}, u32[]{:S(2)}) copy-start(f32[640]{0:T(1024)} %param.14) | copy-start | bytes 7684
where the time goes:
time: 138 us; the launch traced here: 137 us
  local copies, waits for them, and re-layouts  52.1 us (38%)
  waiting for transfers between devices  20.9 us (15%)
  matrix products  20.5 us (15%)
  blocking collectives  18 us (13%)
  starting transfers between devices  17.5 us (13%)
  other arithmetic  7.37 us (5%)
    unnamed x42, local copies, waits for them, and re-layouts  23.4 us
    all_to_all x1, blocking collectives, on_device(): lax.all_to_all(spatial.astype(jnp.bfloat16), 'lon', split_axis=2, concat_...  18 us
    all_to_all x1, waiting for transfers between devices, on_device(): lax.all_to_all(mixed_spec.astype(jnp.bfloat16), 'lon', split_axis=0, conc...  10.6 us
    all_to_all x1, starting transfers between devices, on_device(): lax.all_to_all(fields, 'lon', split_axis=0, concat_axis=2, tiled=True)  7.38 us
    all_to_all x1, local copies, waits for them, and re-layouts, on_device(): lax.all_to_all(fields, 'lon', split_axis=0, concat_axis=2, tiled=True)  6.32 us
    dot_general x1, matrix products, on_device(): lax.dot_general(down_weight, hidden, (((0,), (0,)), ((), ())), preferred_...  5.95 us
    dot_general x1, matrix products, filter_spectra(): jnp.einsum('kisr,kisn->kirn', picked, jnp.sin(sin_angle), precision=lax.P...  5.33 us
    dot_general x1, matrix products, filter_spectra(): jnp.einsum('kisr,kisn->kirn', picked, jnp.cos(cos_angle), precision=lax.P...  5.32 us
  transfers between devices with their start and end apart: 5, of which 4 were waited for; matrix products, arithmetic and copies ran while one was open for 12% of the time, Pallas kernels for 0%

commit v1 on v0

v1 whole, which is shorter than its diff:
```python
import math

import jax
import jax.numpy as jnp
from jax import lax
from jax.sharding import PartitionSpec as P

norm_eps = 1e-05


def reach_of(row, lat_total, lon_total):
    return min(lon_total // 2, 4 * lat_total // min(row + 1, lat_total - row))


def needed_columns(rows, lat_shards, lat_total, lon_total):
    need = [0] * (rows + 2)
    for shard in range(lat_shards // 2):
        for slot in range(rows):
            reach = reach_of(shard * rows + slot, lat_total, lon_total)
            for source in (slot, slot + 1, slot + 2):
                if shard == 0 and source == 0:
                    continue
                need[source] = max(need[source], reach)
    return need


def on_device(
    fields,
    support_rows,
    support_lons,
    support_weights,
    mix_weight,
    norm_gain,
    up_weight,
    down_weight,
):
    channels, rows, cols = fields.shape
    kinds, lat_total, entries = support_rows.shape
    lon_shards = lax.axis_size("lon")
    lat_shards = lax.axis_size("lat")
    lon_total = lon_shards * cols
    need = needed_columns(rows, lat_shards, lat_total, lon_total)
    lat = lax.axis_index("lat")
    south = lat >= lat_shards // 2
    x = jnp.transpose(fields, (1, 2, 0))
    forward = [(i, i + 1) for i in range(lat_shards - 1)]
    backward = [(b, a) for a, b in forward]
    low = lax.ppermute(x[rows - 1 :], "lat", forward)
    high = lax.ppermute(x[:1], "lat", backward)
    x = jnp.concatenate([low, x, high], axis=0)
    x = jnp.where(south, x[::-1], x)
    half = lon_shards // 2
    window = {0: x}
    for dist in range(1, half + 1):
        for sign in (1, -1):
            if dist == half and sign == -1:
                continue
            widths = []
            for slot in range(rows + 2):
                width = max(0, min(cols, need[slot] - (dist - 1) * cols))
                if dist == half and width > 0:
                    width = cols
                widths.append(width)
            picks = [(slot, width) for slot, width in enumerate(widths) if width > 0]
            if not picks:
                continue
            pieces = [
                x[slot, :width] if sign == 1 else x[slot, cols - width :] for slot, width in picks
            ]
            sent = jnp.concatenate(pieces, axis=0)
            got = lax.ppermute(
                sent, "lon", [((i + sign * dist) % lon_shards, i) for i in range(lon_shards)]
            )
            blocks = []
            start = 0
            for slot, width in enumerate(widths):
                piece = got[start : start + width]
                start += width
                gap = jnp.zeros((cols - width, channels), x.dtype)
                blocks.append(
                    jnp.concatenate([piece, gap] if sign == 1 else [gap, piece], axis=0)
                )
            window[(sign * dist) % lon_shards] = jnp.stack(blocks)
    empty = jnp.zeros_like(x)
    wide = jnp.concatenate([window.get(b, empty) for b in range(lon_shards)], axis=1)

    row_start = lat * rows
    row_sel = lax.dynamic_slice_in_dim(support_rows, row_start, rows, 1)
    lon_sel = lax.dynamic_slice_in_dim(support_lons, row_start, rows, 1)
    weight_sel = lax.dynamic_slice_in_dim(support_weights, row_start, rows, 1)
    row_sel = jnp.where(south, -row_sel[:, ::-1], row_sel)
    lon_sel = jnp.where(south, lon_sel[:, ::-1], lon_sel)
    weight_sel = jnp.where(south, weight_sel[:, ::-1], weight_sel)
    place = jnp.arange(lon_total, dtype=jnp.int32)
    column = jnp.arange(cols, dtype=jnp.int32)
    response = None
    for offset in (-1, 0, 1):
        picked = jnp.where(row_sel == offset, weight_sel, 0.0)
        taps = jnp.zeros((rows, kinds, cols, lon_total), jnp.float32)
        for entry in range(entries):
            spot = jnp.mod(
                jnp.transpose(lon_sel[:, :, entry])[:, :, None] + column, lon_total
            )
            taps = taps + jnp.where(
                spot[..., None] == place,
                jnp.transpose(picked[:, :, entry])[:, :, None, None],
                0.0,
            )
        taps = taps.astype(jnp.bfloat16).reshape(rows, kinds * cols, lon_total)
        piece = lax.dot_general(
            taps,
            wide[1 + offset : 1 + offset + rows],
            (((2,), (1,)), ((0,), (0,))),
            preferred_element_type=jnp.float32,
        )
        response = piece if response is None else response + piece
    response = response.astype(jnp.bfloat16).reshape(rows, kinds, cols, channels)
    mixed = None
    for kind in range(kinds):
        piece = jnp.dot(
            response[:, kind].reshape(rows * cols, channels),
            mix_weight[kind],
            preferred_element_type=jnp.float32,
        )
        mixed = piece if mixed is None else mixed + piece
    latent = x[1 : rows + 1].reshape(rows * cols, channels).astype(jnp.float32) + mixed
    mean = jnp.mean(latent, axis=1, keepdims=True)
    variance = jnp.mean(jnp.square(latent - mean), axis=1, keepdims=True)
    normed = ((latent - mean) * lax.rsqrt(variance + norm_eps) * norm_gain).astype(jnp.bfloat16)
    hidden = jax.nn.gelu(
        jnp.dot(normed, up_weight, preferred_element_type=jnp.float32), approximate=False
    ).astype(jnp.bfloat16)
    output = latent + jnp.dot(hidden, down_weight, preferred_element_type=jnp.float32)
    output = output.astype(jnp.bfloat16).reshape(rows, cols, channels)
    output = jnp.where(south, output[::-1], output)
    return jnp.transpose(output, (2, 0, 1))


def solution(mesh):
    in_specs = (P("member", "lat", "lon"), P(), P(), P(), P(), P(), P(), P())
    out_specs = P("member", "lat", "lon")
    return jax.shard_map(
        on_device, mesh=mesh, in_specs=in_specs, out_specs=out_specs, check_vma=False
    )
```

time: 138 us -> 197 us (1.43)
  local copies, waits for them, and re-layouts: 52.1 us -> 121 us
  matrix products: 20.5 us -> 46.4 us
  blocking collectives: 18 us -> 0 us
  waiting for transfers between devices: 20.9 us -> 3.07 us
  other arithmetic: 7.37 us -> 2.78 us
  starting transfers between devices: 17.5 us -> 20.6 us
    broadcast_in_dim x0 -> x96, local copies, waits for them, and re-layouts: none -> 36.5 us  [on_device(): jnp.where(spot[..., None] == place, jnp.transpose(picked[:, :, entry])[:,...]
    unnamed x42 -> x159, local copies, waits for them, and re-layouts: 23.4 us -> 56.5 us
    dot_general x6 -> x11, matrix products: 20.5 us -> 46.4 us  [the longest x3 37.8 us: on_device(): lax.dot_general(taps, wide[1 + offset:1 + offset + rows], (((2,), (1,)),...]
    all_to_all x3 -> x0, waiting for transfers between devices: 18.9 us -> none  [the longest x1 10.6 us: on_device(): lax.all_to_all(mixed_spec.astype(jnp.bfloat16), 'lon', split_axis=0, conc...]
    all_to_all x1 -> x0, blocking collectives: 18 us -> none  [on_device(): lax.all_to_all(spatial.astype(jnp.bfloat16), 'lon', split_axis=2, concat_...]
    ppermute x2 -> x9, starting transfers between devices: 2.59 us -> 20.6 us  [the longest x7 17 us: on_device(): lax.ppermute(sent, 'lon', [((i + sign * dist) % lon_shards, i) for i in r...]
    all_to_all x3 -> x0, starting transfers between devices: 14.9 us -> none  [the longest x1 7.38 us: on_device(): lax.all_to_all(fields, 'lon', split_axis=0, concat_axis=2, tiled=True)]
    concatenate x0 -> x5, local copies, waits for them, and re-layouts: none -> 12.6 us  [the longest x4 12 us: on_device(): sent = jnp.concatenate(pieces, axis=0)]
  transfers between devices with their start and end apart: 5 -> 9, of which waited for: 4 -> 1; matrix products, arithmetic and copies ran while one was open for 12% -> 54% of each run, Pallas kernels for 0% -> 0%
where the time goes in v1:
time: 197 us; the launch traced here: 195 us
  local copies, waits for them, and re-layouts  121 us (61%)
  matrix products  46.4 us (24%)
  starting transfers between devices  20.6 us (10%)
  waiting for transfers between devices  3.07 us (2%)
  other arithmetic  2.78 us (1%)
    unnamed x159, local copies, waits for them, and re-layouts  56.5 us
    dot_general x3, matrix products, on_device(): lax.dot_general(taps, wide[1 + offset:1 + offset + rows], (((2,), (1,)),...  37.8 us
    broadcast_in_dim x96, local copies, waits for them, and re-layouts, on_device(): jnp.where(spot[..., None] == place, jnp.transpose(picked[:, :, entry])[:,...  36.5 us
    ppermute x7, starting transfers between devices, on_device(): lax.ppermute(sent, 'lon', [((i + sign * dist) % lon_shards, i) for i in r...  17 us
    concatenate x4, local copies, waits for them, and re-layouts, on_device(): sent = jnp.concatenate(pieces, axis=0)  12 us
    dot_general x1, matrix products, on_device(): jnp.dot(hidden, down_weight, preferred_element_type=jnp.float32)  5.22 us
    slice x20, local copies, waits for them, and re-layouts, on_device(): piece = got[start:start + width]  4.4 us
    transpose x51, local copies, waits for them, and re-layouts, on_device(): jnp.transpose(picked[:, :, entry])[:, :, None, None]  4 us
  transfers between devices with their start and end apart: 9, of which 1 were waited for; matrix products, arithmetic and copies ran while one was open for 54% of the time, Pallas kernels for 0%

profile of v1, /device:TPU:0, one launch (start us, length us, event | category | flops | bytes accessed | tf_op | source)
XLA Modules:
  0.0 195.2 jit_solution(14977648848823364601)
XLA Ops:
  0.0 0.9 fusion.222
  0.9 2.3 %collective-permute-start = (bf16[1,16,640]{2,1,0:T(8,128)(2,1)S(1)}, bf16[1,16,640]{2,1,0:T(8,128)(2,1)S(1)}, u32[]{:S(2)}, u32[]{:S(2)}) collective-permute-start(bf16[1,16,640]{2,1,0:T(8,128)(2,1)S(1)} %get-tuple-element.47), channel_id=1, source_target_pairs={{0,1},{2,3},{4,5},{6,7},{8,9},{10,11},{12,13},{14,15},{16,17},{18,... | collective-permute-start | bytes 61448 | tf_op jit(solution)/shard_map/ppermute | solution.py:48
  3.2 1.3 collective-permute-start.1
  4.6 0.9 constant_dynamic-slice_fusion
  5.6 0.9 constant_dynamic-slice_fusion.1
  14.0 0.7 broadcast_in_dim.843
  20.9 0.7 broadcast_in_dim.870
  23.1 0.7 broadcast_in_dim.879
  44.8 0.7 broadcast_in_dim.762
  47.1 0.7 broadcast_in_dim.771
  47.9 0.7 broadcast_in_dim.774
  50.9 0.7 broadcast_in_dim.737
  51.7 0.8 constant_dynamic-update-slice_fusion.81
  52.7 5.0 %concatenate.109 = bf16[96,640]{1,0:T(8,128)(2,1)} concatenate(bf16[16,640]{1,0:T(8,128)(2,1)S(1)} %get-tuple-element.46, bf16[16,640]{1,0:T(8,128)(2,1)S(1)} %get-tuple-element.45, bf16[16,640]{1,0:T(8,128)(2,1)S(1)} %get-tuple-element.44, bf16[16,640]{1,0:T(8,128)(2,1)S(1)} %get-tuple-element.43, bf16[16,640]{1,0:T(8,128)(2,1)S(1)} %get-tuple-element.42, ...), dimensions={0} | concatenate | bytes 245760 | tf_op jit(solution)/shard_map/concatenate | solution.py:70
  57.7 4.4 %collective-permute-start.3 = (bf16[96,640]{1,0:T(8,128)(2,1)}, bf16[96,640]{1,0:T(8,128)(2,1)}, u32[]{:S(2)}, u32[]{:S(2)}) collective-permute-start(bf16[96,640]{1,0:T(8,128)(2,1)} %concatenate.109), channel_id=1, source_target_pairs={{4,0},{6,2},{8,4},{10,6},{12,8},{14,10},{0,12},{2,14},{5,1},{7,3},... | collective-permute-start | bytes 368648 | tf_op jit(solution)/shard_map/ppermute | solution.py:71
  62.1 4.9 %concatenate.118 = bf16[96,640]{1,0:T(8,128)(2,1)} concatenate(bf16[16,640]{1,0:T(8,128)(2,1)S(1)} %get-tuple-element.46, bf16[16,640]{1,0:T(8,128)(2,1)S(1)} %get-tuple-element.45, bf16[16,640]{1,0:T(8,128)(2,1)S(1)} %get-tuple-element.44, bf16[16,640]{1,0:T(8,128)(2,1)S(1)} %get-tuple-element.43, bf16[16,640]{1,0:T(8,128)(2,1)S(1)} %get-tuple-element.42, ...), dimensions={0} | concatenate | bytes 245760 | tf_op jit(solution)/shard_map/concatenate | solution.py:70
  67.1 1.0 concatenate.100
  68.1 4.8 %collective-permute-start.2 = (bf16[225,640]{1,0:T(8,128)(2,1)S(1)}, bf16[225,640]{1,0:T(8,128)(2,1)S(1)}, u32[]{:S(2)}, u32[]{:S(2)}) collective-permute-start(bf16[225,640]{1,0:T(8,128)(2,1)S(1)} %concatenate.100), channel_id=1, source_target_pairs={{2,0},{4,2},{6,4},{8,6},{10,8},{12,10},{14,12},{0,14},{3,1},{5,3},... | collective-permute-start | bytes 864008 | tf_op jit(solution)/shard_map/ppermute | solution.py:71
  73.7 3.8 %collective-permute-start.4 = (bf16[58,640]{1,0:T(8,128)(2,1)}, bf16[58,640]{1,0:T(8,128)(2,1)S(1)}, u32[]{:S(2)}, u32[]{:S(2)}) collective-permute-start(bf16[58,640]{1,0:T(8,128)(2,1)} %get-tuple-element.125), channel_id=1, source_target_pairs={{6,0},{8,2},{10,4},{12,6},{14,8},{0,10},{2,12},{4,14},{7,1},{9,3},... | collective-permute-start | bytes 222728 | tf_op jit(solution)/shard_map/ppermute | solution.py:71
  77.5 1.0 concatenate.122
  79.2 3.0 %collective-permute-done.6 = bf16[58,640]{1,0:T(8,128)(2,1)S(1)} collective-permute-done((bf16[58,640]{1,0:T(8,128)(2,1)}, bf16[58,640]{1,0:T(8,128)(2,1)S(1)}, u32[]{:S(2)}, u32[]{:S(2)}) %collective-permute-start.6) | collective-permute-done | bytes 74272 | tf_op jit(solution)/shard_map/ppermute | solution.py:71
  82.2 3.2 %collective-permute-start.5 = (bf16[48,640]{1,0:T(8,128)(2,1)S(1)}, bf16[48,640]{1,0:T(8,128)(2,1)S(1)}, u32[]{:S(2)}, u32[]{:S(2)}) collective-permute-start(bf16[48,640]{1,0:T(8,128)(2,1)S(1)} %pad_maximum_fusion.4), channel_id=1, source_target_pairs={{8,0},{10,2},{12,4},{14,6},{0,8},{2,10},{4,12},{6,14},{9,1},{11,3}... | collective-permute-start | bytes 184328 | tf_op jit(solution)/shard_map/ppermute | solution.py:71
  85.4 0.7 collective-permute-start.8
  86.1 0.7 slice.851
  86.8 0.7 slice.850
  87.5 0.7 slice.849
  88.2 0.7 slice.875
  88.9 0.7 slice.874
  89.7 0.7 slice.873
  101.3 1.3 constant_dynamic-update-slice_fusion.61
  102.6 1.3 constant_dynamic-update-slice_fusion.60
  104.0 1.3 constant_dynamic-update-slice_fusion.59
  105.3 1.3 constant_dynamic-update-slice_fusion.58
  106.6 1.3 constant_dynamic-update-slice_fusion.57
  110.4 0.7 constant_dynamic-update-slice_fusion.52
  119.7 0.7 constant_dynamic-update-slice_fusion.37
  124.7 0.7 constant_dynamic-update-slice_fusion.29
  126.0 1.3 constant_dynamic-update-slice_fusion.27
  127.3 1.3 constant_dynamic-update-slice_fusion.26
  128.7 1.3 constant_dynamic-update-slice_fusion.25
  130.0 1.3 constant_dynamic-update-slice_fusion.24
  131.3 1.3 constant_dynamic-update-slice_fusion.23
  135.1 0.7 constant_dynamic-update-slice_fusion.18
  147.0 14.5 %fusion.2 = f32[16,112,640]{2,1,0:T(8,128)S(1)} fusion(bf16[18,128,640]{2,1,0:T(8,128)(2,1)} %constant_dynamic-update-slice_fusion, f32[16,112]{1,0:T(8,128)} %broadcast_in_dim.831, f32[16,112]{1,0:T(8,128)} %broadcast_in_dim.828, f32[16,112]{1,0:T(8,128)} %broadcast_in_dim.825, f32[16,112]{1,0:T(8,128)} %broadcast_in_dim.822, ...), kind=kOutput, calls=%fused_computation.3 | convolution fusion | flops 304611328 | bytes 7454720 | tf_op jit(solution)/shard_map/dot_general | solution.py:110
  161.8 11.7 %fusion.4 = f32[16,112,640]{2,1,0:T(8,128)S(1)} fusion(bf16[18,128,640]{2,1,0:T(8,128)(2,1)S(1)} %copy-done.2, f32[16,112]{1,0:T(8,128)S(1)} %copy-done.33, s32[16,112]{1,0:T(8,128)S(1)} %get-tuple-element.141, f32[16,112]{1,0:T(8,128)S(1)} %copy-done.32, s32[16,112]{1,0:T(8,128)S(1)} %get-tuple-element.140, f32[16,112]{1,0:T(8,128)S(1)} %copy-done.31, ...), kind=kOutput, calls=%fused_computation.5 | convolution fusion | flops 304611328 | bytes 7471104 | tf_op jit(solution)/shard_map/dot_general | solution.py:110
  173.6 11.7 %add_convert_fusion = bf16[16,112,640]{2,1,0:T(8,128)(2,1)S(1)} fusion(f32[16,112,640]{2,1,0:T(8,128)S(1)} %fusion.4, f32[16,112,640]{2,1,0:T(8,128)S(1)} %fusion.2, bf16[18,128,640]{2,1,0:T(8,128)(2,1)S(1)} %copy-done.2, f32[16,112]{1,0:T(8,128)S(1)} %copy-done.17, f32[16,112]{1,0:T(8,128)S(1)} %copy-done.16, f32[16,112]{1,0:T(8,128)S(1)} %copy-done.15, ...), kind=kOutput, calls=%fused_computation | convolution fusion | flops 308051968 | bytes 14352384 | tf_op jit(solution)/shard_map/dot_general | solution.py:110
  189.2 5.2 %fusion.19 = bf16[256,640]{1,0:T(8,128)(2,1)S(1)} fusion(f32[256,640]{1,0:T(8,128)S(1)} %get-tuple-element.143, bf16[1280,640]{1,0:T(8,128)(2,1)S(1)} %copy-done, bf16[640,1280]{1,0:T(8,128)(2,1)} %param.14, f32[640]{0:T(1024)S(1)} %copy-done.35, f32[256]{0:T(256)S(1)} %add_rsqrt_fusion, f32[256]{0:T(256)S(1)} %broadcast_multiply_fusion), kind=kOutput, calls=%fused_computation.34 | convolution fusion | flops 861143040 | bytes 4264448 | tf_op jit(solution)/shard_map/dot_general | solution.py:133
  194.4 0.8 fusion.164
  (392 shorter events, 85.9 us)
Async XLA Ops:
  0.0 189.2 %copy-start = (bf16[1280,640]{1,0:T(8,128)(2,1)S(1)}, bf16[1280,640]{1,0:T(8,128)(2,1)}, u32[]{:S(2)}) copy-start(bf16[1280,640]{1,0:T(8,128)(2,1)} %param.15) | copy-start | bytes 4915204
  0.9 50.7 %collective-permute-start = (bf16[1,16,640]{2,1,0:T(8,128)(2,1)S(1)}, bf16[1,16,640]{2,1,0:T(8,128)(2,1)S(1)}, u32[]{:S(2)}, u32[]{:S(2)}) collective-permute-start(bf16[1,16,640]{2,1,0:T(8,128)(2,1)S(1)} %get-tuple-element.47), channel_id=1, source_target_pairs={{0,1},{2,3},{4,5},{6,7},{8,9},{10,11},{12,13},{14,15},{16,17},{18,... | collective-permute-start | bytes 61448 | tf_op jit(solution)/shard_map/ppermute | solution.py:48
  3.2 48.4 %collective-permute-start.1 = (bf16[1,16,640]{2,1,0:T(8,128)(2,1)S(1)}, bf16[1,16,640]{2,1,0:T(8,128)(2,1)S(1)}, u32[]{:S(2)}, u32[]{:S(2)}) collective-permute-start(bf16[1,16,640]{2,1,0:T(8,128)(2,1)S(1)} %get-tuple-element.48), channel_id=1, source_target_pairs={{1,0},{3,2},{5,4},{7,6},{9,8},{11,10},{13,12},{15,14},{17,16},{19,... | collective-permute-start | bytes 61448 | tf_op jit(solution)/shard_map/ppermute | solution.py:49
  20.8 30.8 %copy-start.1 = (bf16[640,16,16]{0,2,1:T(8,128)(2,1)S(1)}, bf16[640,16,16]{0,2,1:T(8,128)(2,1)}, u32[]{:S(2)}) copy-start(bf16[640,16,16]{0,2,1:T(8,128)(2,1)} %param.8) | copy-start | bytes 983044
  57.7 28.4 %collective-permute-start.3 = (bf16[96,640]{1,0:T(8,128)(2,1)}, bf16[96,640]{1,0:T(8,128)(2,1)}, u32[]{:S(2)}, u32[]{:S(2)}) collective-permute-start(bf16[96,640]{1,0:T(8,128)(2,1)} %concatenate.109), channel_id=1, source_target_pairs={{4,0},{6,2},{8,4},{10,6},{12,8},{14,10},{0,12},{2,14},{5,1},{7,3},... | collective-permute-start | bytes 368648 | tf_op jit(solution)/shard_map/ppermute | solution.py:71
  67.1 21.2 %collective-permute-start.7 = (bf16[96,640]{1,0:T(8,128)(2,1)}, bf16[96,640]{1,0:T(8,128)(2,1)}, u32[]{:S(2)}, u32[]{:S(2)}) collective-permute-start(bf16[96,640]{1,0:T(8,128)(2,1)} %concatenate.118), channel_id=1, source_target_pairs={{12,0},{14,2},{0,4},{2,6},{4,8},{6,10},{8,12},{10,14},{13,1},{15,3... | collective-permute-start | bytes 368648 | tf_op jit(solution)/shard_map/ppermute | solution.py:71
  68.1 22.3 %collective-permute-start.2 = (bf16[225,640]{1,0:T(8,128)(2,1)S(1)}, bf16[225,640]{1,0:T(8,128)(2,1)S(1)}, u32[]{:S(2)}, u32[]{:S(2)}) collective-permute-start(bf16[225,640]{1,0:T(8,128)(2,1)S(1)} %concatenate.100), channel_id=1, source_target_pairs={{2,0},{4,2},{6,4},{8,6},{10,8},{12,10},{14,12},{0,14},{3,1},{5,3},... | collective-permute-start | bytes 864008 | tf_op jit(solution)/shard_map/ppermute | solution.py:71
  73.6 8.6 %collective-permute-start.6 = (bf16[58,640]{1,0:T(8,128)(2,1)}, bf16[58,640]{1,0:T(8,128)(2,1)S(1)}, u32[]{:S(2)}, u32[]{:S(2)}) collective-permute-start(bf16[58,640]{1,0:T(8,128)(2,1)} %get-tuple-element.124), channel_id=1, source_target_pairs={{10,0},{12,2},{14,4},{0,6},{2,8},{4,10},{6,12},{8,14},{11,1},{13,3... | collective-permute-start | bytes 222728 | tf_op jit(solution)/shard_map/ppermute | solution.py:71
  73.7 11.7 %collective-permute-start.4 = (bf16[58,640]{1,0:T(8,128)(2,1)}, bf16[58,640]{1,0:T(8,128)(2,1)S(1)}, u32[]{:S(2)}, u32[]{:S(2)}) collective-permute-start(bf16[58,640]{1,0:T(8,128)(2,1)} %get-tuple-element.125), channel_id=1, source_target_pairs={{6,0},{8,2},{10,4},{12,6},{14,8},{0,10},{2,12},{4,14},{7,1},{9,3},... | collective-permute-start | bytes 222728 | tf_op jit(solution)/shard_map/ppermute | solution.py:71
  82.2 34.4 %collective-permute-start.5 = (bf16[48,640]{1,0:T(8,128)(2,1)S(1)}, bf16[48,640]{1,0:T(8,128)(2,1)S(1)}, u32[]{:S(2)}, u32[]{:S(2)}) collective-permute-start(bf16[48,640]{1,0:T(8,128)(2,1)S(1)} %pad_maximum_fusion.4), channel_id=1, source_target_pairs={{8,0},{10,2},{12,4},{14,6},{0,8},{2,10},{4,12},{6,14},{9,1},{11,3}... | collective-permute-start | bytes 184328 | tf_op jit(solution)/shard_map/ppermute | solution.py:71
  85.4 51.0 %collective-permute-start.8 = (bf16[225,640]{1,0:T(8,128)(2,1)S(1)}, bf16[225,640]{1,0:T(8,128)(2,1)S(1)}, u32[]{:S(2)}, u32[]{:S(2)}) collective-permute-start(bf16[225,640]{1,0:T(8,128)(2,1)S(1)} %concatenate.122), channel_id=1, source_target_pairs={{14,0},{0,2},{2,4},{4,6},{6,8},{8,10},{10,12},{12,14},{15,1},{1,3}... | collective-permute-start | bytes 864008 | tf_op jit(solution)/shard_map/ppermute | solution.py:71
  146.8 14.6 %copy-start.2 = (bf16[18,128,640]{2,1,0:T(8,128)(2,1)S(1)}, bf16[18,128,640]{2,1,0:T(8,128)(2,1)}, u32[]{:S(2)}) copy-start(bf16[18,128,640]{2,1,0:T(8,128)(2,1)} %constant_dynamic-update-slice_fusion) | copy-start | bytes 8847364
  146.8 14.7 %copy-start.19 = (f32[16,112]{1,0:T(8,128)S(1)}, f32[16,112]{1,0:T(8,128)}, u32[]{:S(2)}) copy-start(f32[16,112]{1,0:T(8,128)} %broadcast_in_dim.741) | copy-start | bytes 21508
  146.8 14.7 %copy-start.20 = (f32[16,112]{1,0:T(8,128)S(1)}, f32[16,112]{1,0:T(8,128)}, u32[]{:S(2)}) copy-start(f32[16,112]{1,0:T(8,128)} %broadcast_in_dim.744) | copy-start | bytes 21508
  146.8 14.7 %copy-start.21 = (f32[16,112]{1,0:T(8,128)S(1)}, f32[16,112]{1,0:T(8,128)}, u32[]{:S(2)}) copy-start(f32[16,112]{1,0:T(8,128)} %broadcast_in_dim.747) | copy-start | bytes 21508
  146.8 14.7 %copy-start.22 = (f32[16,112]{1,0:T(8,128)S(1)}, f32[16,112]{1,0:T(8,128)}, u32[]{:S(2)}) copy-start(f32[16,112]{1,0:T(8,128)} %broadcast_in_dim.750) | copy-start | bytes 21508
  146.8 14.7 %copy-start.23 = (f32[16,112]{1,0:T(8,128)S(1)}, f32[16,112]{1,0:T(8,128)}, u32[]{:S(2)}) copy-start(f32[16,112]{1,0:T(8,128)} %broadcast_in_dim.753) | copy-start | bytes 21508
  146.8 14.7 %copy-start.24 = (f32[16,112]{1,0:T(8,128)S(1)}, f32[16,112]{1,0:T(8,128)}, u32[]{:S(2)}) copy-start(f32[16,112]{1,0:T(8,128)} %broadcast_in_dim.756) | copy-start | bytes 21508
  146.9 14.7 %copy-start.25 = (f32[16,112]{1,0:T(8,128)S(1)}, f32[16,112]{1,0:T(8,128)}, u32[]{:S(2)}) copy-start(f32[16,112]{1,0:T(8,128)} %broadcast_in_dim.759) | copy-start | bytes 21508
  146.9 14.7 %copy-start.26 = (f32[16,112]{1,0:T(8,128)S(1)}, f32[16,112]{1,0:T(8,128)}, u32[]{:S(2)}) copy-start(f32[16,112]{1,0:T(8,128)} %broadcast_in_dim.762) | copy-start | bytes 21508
  146.9 14.7 %copy-start.27 = (f32[16,112]{1,0:T(8,128)S(1)}, f32[16,112]{1,0:T(8,128)}, u32[]{:S(2)}) copy-start(f32[16,112]{1,0:T(8,128)} %broadcast_in_dim.765) | copy-start | bytes 21508
  146.9 14.7 %copy-start.28 = (f32[16,112]{1,0:T(8,128)S(1)}, f32[16,112]{1,0:T(8,128)}, u32[]{:S(2)}) copy-start(f32[16,112]{1,0:T(8,128)} %broadcast_in_dim.768) | copy-start | bytes 21508
  146.9 14.7 %copy-start.29 = (f32[16,112]{1,0:T(8,128)S(1)}, f32[16,112]{1,0:T(8,128)}, u32[]{:S(2)}) copy-start(f32[16,112]{1,0:T(8,128)} %broadcast_in_dim.771) | copy-start | bytes 21508
  146.9 14.7 %copy-start.30 = (f32[16,112]{1,0:T(8,128)S(1)}, f32[16,112]{1,0:T(8,128)}, u32[]{:S(2)}) copy-start(f32[16,112]{1,0:T(8,128)} %broadcast_in_dim.774) | copy-start | bytes 21508
  146.9 14.7 %copy-start.31 = (f32[16,112]{1,0:T(8,128)S(1)}, f32[16,112]{1,0:T(8,128)}, u32[]{:S(2)}) copy-start(f32[16,112]{1,0:T(8,128)} %broadcast_in_dim.777) | copy-start | bytes 21508
  146.9 14.7 %copy-start.32 = (f32[16,112]{1,0:T(8,128)S(1)}, f32[16,112]{1,0:T(8,128)}, u32[]{:S(2)}) copy-start(f32[16,112]{1,0:T(8,128)} %broadcast_in_dim.780) | copy-start | bytes 21508
  146.9 14.7 %copy-start.33 = (f32[16,112]{1,0:T(8,128)S(1)}, f32[16,112]{1,0:T(8,128)}, u32[]{:S(2)}) copy-start(f32[16,112]{1,0:T(8,128)} %broadcast_in_dim.783) | copy-start | bytes 21508
  146.9 14.7 %copy-start.34 = (f32[16,112]{1,0:T(8,128)S(1)}, f32[16,112]{1,0:T(8,128)}, u32[]{:S(2)}) copy-start(f32[16,112]{1,0:T(8,128)} %broadcast_in_dim.737) | copy-start | bytes 21508
  161.6 11.8 %copy-start.3 = (f32[16,112]{1,0:T(8,128)S(1)}, f32[16,112]{1,0:T(8,128)}, u32[]{:S(2)}) copy-start(f32[16,112]{1,0:T(8,128)} %broadcast_in_dim.837) | copy-start | bytes 21508
  161.6 11.8 %copy-start.4 = (f32[16,112]{1,0:T(8,128)S(1)}, f32[16,112]{1,0:T(8,128)}, u32[]{:S(2)}) copy-start(f32[16,112]{1,0:T(8,128)} %broadcast_in_dim.840) | copy-start | bytes 21508
  161.6 11.8 %copy-start.5 = (f32[16,112]{1,0:T(8,128)S(1)}, f32[16,112]{1,0:T(8,128)}, u32[]{:S(2)}) copy-start(f32[16,112]{1,0:T(8,128)} %broadcast_in_dim.843) | copy-start | bytes 21508
  161.7 11.8 %copy-start.6 = (f32[16,112]{1,0:T(8,128)S(1)}, f32[16,112]{1,0:T(8,128)}, u32[]{:S(2)}) copy-start(f32[16,112]{1,0:T(8,128)} %broadcast_in_dim.846) | copy-start | bytes 21508
  161.7 11.8 %copy-start.7 = (f32[16,112]{1,0:T(8,128)S(1)}, f32[16,112]{1,0:T(8,128)}, u32[]{:S(2)}) copy-start(f32[16,112]{1,0:T(8,128)} %broadcast_in_dim.849) | copy-start | bytes 21508
  161.7 11.8 %copy-start.8 = (f32[16,112]{1,0:T(8,128)S(1)}, f32[16,112]{1,0:T(8,128)}, u32[]{:S(2)}) copy-start(f32[16,112]{1,0:T(8,128)} %broadcast_in_dim.852) | copy-start | bytes 21508
  161.7 11.8 %copy-start.9 = (f32[16,112]{1,0:T(8,128)S(1)}, f32[16,112]{1,0:T(8,128)}, u32[]{:S(2)}) copy-start(f32[16,112]{1,0:T(8,128)} %broadcast_in_dim.855) | copy-start | bytes 21508
  161.7 11.8 %copy-start.10 = (f32[16,112]{1,0:T(8,128)S(1)}, f32[16,112]{1,0:T(8,128)}, u32[]{:S(2)}) copy-start(f32[16,112]{1,0:T(8,128)} %broadcast_in_dim.858) | copy-start | bytes 21508
  161.7 11.8 %copy-start.11 = (f32[16,112]{1,0:T(8,128)S(1)}, f32[16,112]{1,0:T(8,128)}, u32[]{:S(2)}) copy-start(f32[16,112]{1,0:T(8,128)} %broadcast_in_dim.861) | copy-start | bytes 21508
  161.7 11.8 %copy-start.12 = (f32[16,112]{1,0:T(8,128)S(1)}, f32[16,112]{1,0:T(8,128)}, u32[]{:S(2)}) copy-start(f32[16,112]{1,0:T(8,128)} %broadcast_in_dim.864) | copy-start | bytes 21508
  161.7 11.8 %copy-start.13 = (f32[16,112]{1,0:T(8,128)S(1)}, f32[16,112]{1,0:T(8,128)}, u32[]{:S(2)}) copy-start(f32[16,112]{1,0:T(8,128)} %broadcast_in_dim.867) | copy-start | bytes 21508
  161.7 11.8 %copy-start.14 = (f32[16,112]{1,0:T(8,128)S(1)}, f32[16,112]{1,0:T(8,128)}, u32[]{:S(2)}) copy-start(f32[16,112]{1,0:T(8,128)} %broadcast_in_dim.870) | copy-start | bytes 21508
  161.7 11.8 %copy-start.15 = (f32[16,112]{1,0:T(8,128)S(1)}, f32[16,112]{1,0:T(8,128)}, u32[]{:S(2)}) copy-start(f32[16,112]{1,0:T(8,128)} %broadcast_in_dim.873) | copy-start | bytes 21508
  161.8 11.8 %copy-start.16 = (f32[16,112]{1,0:T(8,128)S(1)}, f32[16,112]{1,0:T(8,128)}, u32[]{:S(2)}) copy-start(f32[16,112]{1,0:T(8,128)} %broadcast_in_dim.876) | copy-start | bytes 21508
  161.8 11.8 %copy-start.17 = (f32[16,112]{1,0:T(8,128)S(1)}, f32[16,112]{1,0:T(8,128)}, u32[]{:S(2)}) copy-start(f32[16,112]{1,0:T(8,128)} %broadcast_in_dim.879) | copy-start | bytes 21508
  161.8 11.8 %copy-start.18 = (f32[16,112]{1,0:T(8,128)S(1)}, f32[16,112]{1,0:T(8,128)}, u32[]{:S(2)}) copy-start(f32[16,112]{1,0:T(8,128)} %broadcast_in_dim.834) | copy-start | bytes 21508
  161.8 23.8 %slice-start = ((s8[5734400]{0:T(1024)(128)(4,1)}), s8[4194304]{0:T(1024)(128)(4,1)S(1)}, s32[]{:S(2)}) async-start(s8[5734400]{0:T(1024)(128)(4,1)} %bitcast.564), calls=%async_computation | async-start | bytes 8388608
  173.6 11.9 %slice-start.1 = ((s8[5734400]{0:T(1024)(128)(4,1)}), s8[1540096]{0:T(1024)(128)(4,1)S(1)}, s32[]{:S(2)}) async-start(s8[5734400]{0:T(1024)(128)(4,1)} %bitcast.564), calls=%async_computation.1 | async-start | bytes 3080192
  187.9 1.3 copy-start.35

commit v2 on v1

v2 whole, which is shorter than its diff:
```python
import functools

import jax
import jax.numpy as jnp
from jax import lax
from jax.experimental import pallas as pl
from jax.experimental.pallas import tpu as pltpu
from jax.sharding import PartitionSpec as P

norm_eps = 1e-05
lanes = 128
vmem = pl.BlockSpec(memory_space=pltpu.VMEM)


class Plan:
    def __init__(self, rows, cols, lat_shards, lon_shards):
        self.rows, self.cols = rows, cols
        self.lat_shards, self.lon_shards = lat_shards, lon_shards
        lat_total, lon_total = rows * lat_shards, cols * lon_shards
        self.lon_total = lon_total
        self.half = lon_shards // 2
        self.outer = lat_shards > 2
        reach = [0] * rows
        need = [0] * (rows + 2)
        for shard in range(lat_shards // 2):
            for slot in range(rows):
                row = shard * rows + slot
                span = min(lon_total // 2, 4 * lat_total // min(row + 1, lat_total - row))
                reach[slot] = max(reach[slot], span)
                for source in (slot, slot + 1, slot + 2):
                    need[source] = max(need[source], span)
        if not self.outer:
            need[0] = 0
        self.blocks = [min(self.half, -(-span // cols)) for span in reach]
        self.moves = []
        for dist in range(1, self.half + 1):
            for sign in (1, -1):
                if dist == self.half and sign == -1:
                    continue
                picks, start = [], 0
                for slot in range(rows + 2):
                    width = max(0, min(cols, need[slot] - (dist - 1) * cols))
                    if width > 0:
                        width = cols if dist == self.half else width
                        picks.append((slot, start, width))
                        start += width
                if picks:
                    self.moves.append((dist, sign, picks, start))

    def span(self, slot):
        blocks = self.blocks[slot]
        if blocks == self.half:
            return 0, self.lon_total
        return (self.half - 1 - blocks) * self.cols, (2 * blocks + 1) * self.cols

    def sources(self, slot):
        return [s for s in (slot, slot + 1, slot + 2) if s > 0 or self.outer]


def is_south(plan):
    return lax.axis_index("lat") >= plan.lat_shards // 2


def row_of(plan, south, slot):
    return jnp.where(south, plan.rows - slot, slot - 1)


def load_slot(plan, south, slot, x_ref, low_ref, high_ref):
    if slot == 0:
        return jnp.where(south, high_ref[0], low_ref[0])
    if slot == plan.rows + 1:
        return jnp.where(south, low_ref[0], high_ref[0])
    return x_ref[row_of(plan, south, slot)]


def pack_body(plan, moves, halo, *refs):
    low_ref, high_ref = refs[1:3] if halo else (None, None)
    outs = refs[3:] if halo else refs[1:]
    south = is_south(plan)
    for (_, sign, picks, _), out in zip(moves, outs):
        for slot, start, width in picks:
            block = load_slot(plan, south, slot, refs[0], low_ref, high_ref)
            block = block[:width] if sign == 1 else block[plan.cols - width :]
            out[start : start + width] = block


def pack(plan, moves, x, low, high):
    halo = low is not None
    args = (x, low, high) if halo else (x,)
    return pl.pallas_call(
        functools.partial(pack_body, plan, moves, halo),
        out_shape=[jax.ShapeDtypeStruct((m[3], x.shape[2]), x.dtype) for m in moves],
        in_specs=[vmem] * len(args),
        out_specs=[vmem] * len(moves),
        name="pack_columns",
    )(*args)


def taps_body(plan, kinds, entries, support_ref, out):
    south = is_south(plan)
    row_start = lax.axis_index("lat") * plan.rows
    width = out.shape[2]
    spot = lax.broadcasted_iota(jnp.int32, (kinds, width), 1).astype(jnp.float32)
    index = 0
    for slot in range(plan.rows):
        center = (plan.half - 1) * plan.cols - plan.span(slot)[0]
        tile = support_ref[row_start + row_of(plan, south, slot + 1)]
        lift = jnp.where(south, -tile[0], tile[0])
        place = tile[1] + center
        place = jnp.where(place < 0, place + plan.lon_total, place)
        for source in plan.sources(slot):
            weight = jnp.where(lift == (source - slot - 1), tile[2], 0.0)
            taps = jnp.zeros((kinds, width), jnp.float32)
            for entry in range(entries):
                hit = place[:, entry : entry + 1] == spot
                taps = taps + jnp.where(hit, weight[:, entry : entry + 1], 0.0)
            for kind in range(kinds):
                spread = jnp.broadcast_to(taps[kind : kind + 1], (plan.cols, width))
                spread = pltpu.roll(spread, 0, 1, stride=1, stride_axis=0)
                out[index, kind * plan.cols : (kind + 1) * plan.cols] = spread.astype(jnp.bfloat16)
            index += 1


def make_taps(plan, support):
    kinds, entries = support.shape[2:]
    count = sum(len(plan.sources(slot)) for slot in range(plan.rows))
    width = -(-plan.lon_total // lanes) * lanes
    return pl.pallas_call(
        functools.partial(taps_body, plan, kinds, entries),
        out_shape=jax.ShapeDtypeStruct((count, kinds * plan.cols, width), jnp.bfloat16),
        in_specs=[vmem],
        out_specs=vmem,
        name="filter_taps",
    )(support)


def compute_body(plan, kinds, *refs):
    x_ref, low_ref, high_ref = refs[:3]
    used = 3 + len(plan.moves)
    got_refs = refs[3:used]
    taps_ref, mix_ref, gain_ref, up_ref, down_ref, out_ref, win, response = refs[used:]
    rows, cols = plan.rows, plan.cols
    south = is_south(plan)
    middle = (plan.half - 1) * cols
    for slot in range(0 if plan.outer else 1, rows + 2):
        win[slot, middle : middle + cols] = load_slot(plan, south, slot, x_ref, low_ref, high_ref)
    for (dist, sign, picks, _), got in zip(plan.moves, got_refs):
        place = middle + sign * dist * cols
        for slot, start, width in picks:
            block = got[start : start + width]
            if width < cols:
                gap = jnp.zeros((cols - width, block.shape[1]), block.dtype)
                block = jnp.concatenate([block, gap] if sign == 1 else [gap, block], axis=0)
            win[slot, place : place + cols] = block
    index = 0
    for slot in range(rows):
        first, count = plan.span(slot)
        total = None
        for source in plan.sources(slot):
            piece = jnp.dot(
                taps_ref[index, :, :count],
                win[source, first : first + count],
                preferred_element_type=jnp.float32,
            )
            total = piece if total is None else total + piece
            index += 1
        total = total.astype(jnp.bfloat16)
        for kind in range(kinds):
            response[kind, slot * cols : (slot + 1) * cols] = total[kind * cols : (kind + 1) * cols]
    mixed = jnp.dot(response[0], mix_ref[0], preferred_element_type=jnp.float32)
    for kind in range(1, kinds):
        mixed = mixed + jnp.dot(response[kind], mix_ref[kind], preferred_element_type=jnp.float32)
    own = win[1 : rows + 1, middle : middle + cols].reshape(rows * cols, -1)
    latent = own.astype(jnp.float32) + mixed
    mean = jnp.mean(latent, axis=1, keepdims=True)
    variance = jnp.mean(jnp.square(latent - mean), axis=1, keepdims=True)
    normed = (latent - mean) * lax.rsqrt(variance + norm_eps) * gain_ref[...]
    hidden = jnp.dot(normed.astype(jnp.bfloat16), up_ref[...], preferred_element_type=jnp.float32)
    hidden = (0.5 * hidden * (1.0 + lax.erf(hidden * 0.5**0.5))).astype(jnp.bfloat16)
    output = latent + jnp.dot(hidden, down_ref[...], preferred_element_type=jnp.float32)
    output = output.astype(jnp.bfloat16)
    for slot in range(rows):
        out_ref[row_of(plan, south, slot + 1)] = output[slot * cols : (slot + 1) * cols]


def on_device(
    fields,
    support_rows,
    support_lons,
    support_weights,
    mix_weight,
    norm_gain,
    up_weight,
    down_weight,
):
    channels, rows, cols = fields.shape
    kinds = support_rows.shape[0]
    lon_shards = lax.axis_size("lon")
    lat_shards = lax.axis_size("lat")
    plan = Plan(rows, cols, lat_shards, lon_shards)
    x = jnp.transpose(fields, (1, 2, 0))
    forward = [(i, i + 1) for i in range(lat_shards - 1)]
    low = lax.ppermute(x[rows - 1 :], "lat", forward)
    high = lax.ppermute(x[:1], "lat", [(b, a) for a, b in forward])

    edge = (0, rows + 1)
    inside = [m for m in plan.moves if all(slot not in edge for slot, _, _ in m[2])]
    across = [m for m in plan.moves if m not in inside]
    sent = {}
    if inside:
        sent.update(zip([m[:2] for m in inside], pack(plan, inside, x, None, None)))
    sent.update(zip([m[:2] for m in across], pack(plan, across, x, low, high)))
    got = [
        lax.ppermute(
            sent[dist, sign],
            "lon",
            [((i + sign * dist) % lon_shards, i) for i in range(lon_shards)],
        )
        for dist, sign, _, _ in plan.moves
    ]
    support = jnp.stack(
        [
            support_rows.astype(jnp.float32),
            support_lons.astype(jnp.float32),
            support_weights,
        ]
    ).transpose(2, 0, 1, 3)
    taps = make_taps(plan, support)
    args = (x, low, high, *got, taps, mix_weight, norm_gain[None], up_weight, down_weight)
    output = pl.pallas_call(
        functools.partial(compute_body, plan, kinds),
        out_shape=jax.ShapeDtypeStruct((rows, cols, channels), jnp.bfloat16),
        in_specs=[vmem] * len(args),
        out_specs=vmem,
        scratch_shapes=[
            pltpu.VMEM((rows + 2, plan.lon_total, channels), jnp.bfloat16),
            pltpu.VMEM((kinds, rows * cols, channels), jnp.bfloat16),
        ],
        compiler_params=pltpu.CompilerParams(vmem_limit_bytes=40 * 2**20),
        name="filter_mix_mlp",
    )(*args)
    return jnp.transpose(output, (2, 0, 1))


def solution(mesh):
    in_specs = (P("member", "lat", "lon"), P(), P(), P(), P(), P(), P(), P())
    out_specs = P("member", "lat", "lon")
    return jax.shard_map(
        on_device, mesh=mesh, in_specs=in_specs, out_specs=out_specs, check_vma=False
    )
```

time: 197 us -> 50.8 us (0.26)
  the two profiles are of different devices: /device:TPU:0 before, /device:TPU:16 now
where the time goes in v2:
time: 50.8 us; the launch traced here: 50.3 us
  starting transfers between devices  21.3 us (42%)
  Pallas kernels  17.6 us (35%)
  local copies, waits for them, and re-layouts  7.69 us (15%)
  waiting for transfers between devices  1.84 us (4%)
  other arithmetic  1.69 us (3%)
    ppermute x7, starting transfers between devices, on_device(): lax.ppermute(sent[dist, sign], 'lon', [((i + sign * dist) % lon_shards, i...  18.1 us
    pallas_call x1, Pallas kernels, make_taps(): pl.pallas_call(functools.partial(taps_body, plan, kinds, entries), out_sh...  7.38 us
    pallas_call x1, Pallas kernels, on_device(): pl.pallas_call(functools.partial(compute_body, plan, kinds), out_shape=ja...  6.57 us
    unnamed x20, local copies, waits for them, and re-layouts  6 us
    pallas_call x2, Pallas kernels, pack(): pl.pallas_call(functools.partial(pack_body, plan, moves, halo), out_shape...  3.69 us
    ppermute x1, starting transfers between devices, on_device(): low = lax.ppermute(x[rows - 1:], 'lat', forward)  1.87 us
    ppermute x7, waiting for transfers between devices, on_device(): lax.ppermute(sent[dist, sign], 'lon', [((i + sign * dist) % lon_shards, i...  1.83 us
    another operation x2, other arithmetic, on_device(): jnp.stack([support_rows.astype(jnp.float32), support_lons.astype(jnp.floa...  1.69 us
  transfers between devices with their start and end apart: 9, of which 1 were waited for; matrix products, arithmetic and copies ran while one was open for 7% of the time, Pallas kernels for 18%

profile of v2, /device:TPU:16, one launch (start us, length us, event | category | flops | bytes accessed | tf_op | source)
XLA Modules:
  0.0 50.3 jit_solution(178240590658473518)
XLA Ops:
  0.0 1.8 %pack_columns.3 = (bf16[96,640]{1,0:T(8,128)(2,1)}, bf16[96,640]{1,0:T(8,128)(2,1)}, bf16[58,640]{1,0:T(8,128)(2,1)}, bf16[58,640]{1,0:T(8,128)(2,1)}, bf16[48,640]{1,0:T(8,128)(2,1)}) custom-call(bf16[16,16,640]{2,1,0:T(8,128)(2,1)} %bitcast.8), custom_call_target="tpu_custom_call" | custom-call | tf_op jit(solution)/shard_map/pack_columns/pallas_call | solution.py:90
  1.8 0.0 collective-permute-start.8
  1.8 0.8 %fusion = (bf16[1,16,640]{2,1,0:T(8,128)(2,1)S(1)}, bf16[1,16,640]{2,1,0:T(8,128)(2,1)S(1)}) fusion(bf16[16,16,640]{2,1,0:T(8,128)(2,1)} %bitcast.9), kind=kLoop, calls=%fused_computation.3 | loop fusion | bytes 81920 | tf_op jit(solution)/shard_map/slice | solution.py:204
  2.5 0.0 copy-start.9
  2.5 0.0 copy-start.2
  2.5 0.0 copy-start.3
  2.6 1.9 %collective-permute-start = (bf16[1,16,640]{2,1,0:T(8,128)(2,1)S(1)}, bf16[1,16,640]{2,1,0:T(8,128)(2,1)S(1)}, u32[]{:S(2)}, u32[]{:S(2)}) collective-permute-start(bf16[1,16,640]{2,1,0:T(8,128)(2,1)S(1)} %get-tuple-element.20), channel_id=1, source_target_pairs={{0,1},{2,3},{4,5},{6,7},{8,9},{10,11},{12,13},{14,15},{16,17},{18,... | collective-permute-start | bytes 61448 | tf_op jit(solution)/shard_map/ppermute | solution.py:203
  4.4 1.3 %collective-permute-start.1 = (bf16[1,16,640]{2,1,0:T(8,128)(2,1)S(1)}, bf16[1,16,640]{2,1,0:T(8,128)(2,1)S(1)}, u32[]{:S(2)}, u32[]{:S(2)}) collective-permute-start(bf16[1,16,640]{2,1,0:T(8,128)(2,1)S(1)} %get-tuple-element.19), channel_id=1, source_target_pairs={{1,0},{3,2},{5,4},{7,6},{9,8},{11,10},{13,12},{15,14},{17,16},{19,... | collective-permute-start | bytes 61448 | tf_op jit(solution)/shard_map/ppermute | solution.py:204
  5.7 2.8 %collective-permute-start.4 = (bf16[96,640]{1,0:T(8,128)(2,1)}, bf16[96,640]{1,0:T(8,128)(2,1)S(1)}, u32[]{:S(2)}, u32[]{:S(2)}) collective-permute-start(bf16[96,640]{1,0:T(8,128)(2,1)} %get-tuple-element.14), channel_id=1, source_target_pairs={{4,0},{6,2},{8,4},{10,6},{12,8},{14,10},{0,12},{2,14},{5,1},{7,3},... | collective-permute-start | bytes 368648 | tf_op jit(solution)/shard_map/ppermute | solution.py:214
  8.5 0.0 collective-permute-start.5
  8.6 0.0 collective-permute-done.refs_1_
  8.6 0.0 copy-start.5
  8.6 2.8 %collective-permute-start.6 = (bf16[58,640]{1,0:T(8,128)(2,1)}, bf16[58,640]{1,0:T(8,128)(2,1)S(1)}, u32[]{:S(2)}, u32[]{:S(2)}) collective-permute-start(bf16[58,640]{1,0:T(8,128)(2,1)} %get-tuple-element.16), channel_id=1, source_target_pairs={{6,0},{8,2},{10,4},{12,6},{14,8},{0,10},{2,12},{4,14},{7,1},{9,3},... | collective-permute-start | bytes 222728 | tf_op jit(solution)/shard_map/ppermute | solution.py:214
  11.4 0.0 collective-permute-done.1.refs_2_
  11.4 0.0 copy-done.5
  11.4 0.0 copy-start.7
  11.4 0.6 %copy-done.7 = bf16[1,16,640]{2,1,0:T(8,128)(2,1)} copy-done((bf16[1,16,640]{2,1,0:T(8,128)(2,1)}, bf16[1,16,640]{2,1,0:T(8,128)(2,1)S(1)}, u32[]{:S(2)}) %copy-start.7) | copy-done | bytes 20504
  12.0 1.9 %pack_columns.2 = (bf16[225,640]{1,0:T(8,128)(2,1)}, bf16[225,640]{1,0:T(8,128)(2,1)}) custom-call(bf16[16,16,640]{2,1,0:T(8,128)(2,1)} %bitcast.10, bf16[1,16,640]{2,1,0:T(8,128)(2,1)} %copy-done.5, bf16[1,16,640]{2,1,0:T(8,128)(2,1)} %copy-done.7), custom_call_target="tpu_custom_call" | custom-call | tf_op jit(solution)/shard_map/pack_columns/pallas_call | solution.py:90
  13.9 0.0 copy-start.6
  13.9 0.0 copy-start.8
  13.9 0.7 %collective-permute-start.2 = (bf16[225,640]{1,0:T(8,128)(2,1)}, bf16[225,640]{1,0:T(8,128)(2,1)S(1)}, u32[]{:S(2)}, u32[]{:S(2)}) collective-permute-start(bf16[225,640]{1,0:T(8,128)(2,1)} %get-tuple-element.12), channel_id=1, source_target_pairs={{2,0},{4,2},{6,4},{8,6},{10,8},{12,10},{14,12},{0,14},{3,1},{5,3},... | collective-permute-start | bytes 864008 | tf_op jit(solution)/shard_map/ppermute | solution.py:214
  14.6 0.0 collective-permute-done.8.refs_9_
  14.6 1.3 %collective-permute-start.3 = (bf16[225,640]{1,0:T(8,128)(2,1)}, bf16[225,640]{1,0:T(8,128)(2,1)S(1)}, u32[]{:S(2)}, u32[]{:S(2)}) collective-permute-start(bf16[225,640]{1,0:T(8,128)(2,1)} %get-tuple-element.13), channel_id=1, source_target_pairs={{14,0},{0,2},{2,4},{4,6},{6,8},{8,10},{10,12},{12,14},{15,1},{1,3}... | collective-permute-start | bytes 864008 | tf_op jit(solution)/shard_map/ppermute | solution.py:214
  15.9 0.9 %convert_bitcast_fusion = (f32[1,7,32,16]{2,3,1,0:T(8,128)S(1)}, f32[1,7,32,16]{2,3,1,0:T(8,128)S(1)}) fusion(s32[7,32,16]{1,2,0:T(8,128)} %param.10, s32[7,32,16]{1,2,0:T(8,128)} %param.9), kind=kLoop, calls=%fused_computation.1 | loop fusion | flops 7168 | bytes 57344 | tf_op jit(solution)/shard_map/stack | solution.py:221
  16.8 1.8 %collective-permute-done.6.refs_7_ = bf16[58,640]{1,0:T(8,128)(2,1)S(1)} collective-permute-done((bf16[58,640]{1,0:T(8,128)(2,1)}, bf16[58,640]{1,0:T(8,128)(2,1)S(1)}, u32[]{:S(2)}, u32[]{:S(2)}) %collective-permute-start.6) | collective-permute-done | bytes 74272 | tf_op jit(solution)/shard_map/ppermute | solution.py:214
  18.6 10.5 %collective-permute-start.7 = (bf16[58,640]{1,0:T(8,128)(2,1)}, bf16[58,640]{1,0:T(8,128)(2,1)S(1)}, u32[]{:S(2)}, u32[]{:S(2)}) collective-permute-start(bf16[58,640]{1,0:T(8,128)(2,1)} %get-tuple-element.17), channel_id=1, source_target_pairs={{10,0},{12,2},{14,4},{0,6},{2,8},{4,10},{6,12},{8,14},{11,1},{13,3... | collective-permute-start | bytes 222728 | tf_op jit(solution)/shard_map/ppermute | solution.py:214
  29.1 0.8 %pad_maximum_fusion = f32[3,7,32,16]{2,3,1,0:T(8,128)S(1)} fusion(f32[1,7,32,16]{2,3,1,0:T(8,128)} %bitcast.13, f32[1,7,32,16]{2,3,1,0:T(8,128)S(1)} %get-tuple-element.21, f32[1,7,32,16]{2,3,1,0:T(8,128)S(1)} %get-tuple-element.22), kind=kLoop, calls=%fused_computation | loop fusion | flops 21504 | bytes 86016 | tf_op jit(solution)/shard_map/stack | solution.py:221
  29.9 0.9 %copy.12 = f32[3,7,32,16]{3,1,0,2:T(8,128)} copy(f32[3,7,32,16]{2,3,1,0:T(8,128)S(1)} %pad_maximum_fusion) | data formatting | bytes 86016 | tf_op jit(solution)/shard_map/stack | solution.py:221
  30.9 7.4 %filter_taps.1.refs_10_ = bf16[47,112,128]{2,1,0:T(8,128)(2,1)} custom-call(f32[32,3,7,16]{3,2,1,0:T(8,128)} %bitcast.12), custom_call_target="tpu_custom_call" | custom-call | tf_op jit(solution)/shard_map/filter_taps/pallas_call | solution.py:128
  38.2 0.0 copy-done.9
  38.3 0.0 collective-permute-done.7.refs_8_
  38.3 0.0 collective-permute-done.4.refs_5_
  38.3 0.0 collective-permute-done.5.refs_6_
  38.3 0.0 collective-permute-done.2.refs_3_
  38.3 0.0 collective-permute-done.3.refs_4_
  38.3 0.0 copy-done.2
  38.3 0.0 copy-done.3
  38.3 0.0 copy-done.6
  38.3 0.0 copy-done.8
  38.3 0.0 copy-start
  38.4 2.6 %copy-done = bf16[7,640,640]{2,1,0:T(8,128)(2,1)S(1)} copy-done((bf16[7,640,640]{2,1,0:T(8,128)(2,1)S(1)}, bf16[7,640,640]{2,1,0:T(8,128)(2,1)}, u32[]{:S(2)}) %copy-start) | copy-done | bytes 5734424
  41.0 0.0 copy-start.1
  41.0 1.3 %copy-done.1 = bf16[47,112,128]{2,1,0:T(8,128)(2,1)S(1)} copy-done((bf16[47,112,128]{2,1,0:T(8,128)(2,1)S(1)}, bf16[47,112,128]{2,1,0:T(8,128)(2,1)}, u32[]{:S(2)}) %copy-start.1) | copy-done | bytes 1347608
  42.3 0.0 copy-start.4
  42.3 1.4 %copy-done.4 = bf16[1280,640]{1,0:T(8,128)(2,1)S(1)} copy-done((bf16[1280,640]{1,0:T(8,128)(2,1)S(1)}, bf16[1280,640]{1,0:T(8,128)(2,1)}, u32[]{:S(2)}) %copy-start.4) | copy-done | bytes 1638424
  43.7 6.6 %filter_mix_mlp.1 = bf16[16,16,640]{2,1,0:T(8,128)(2,1)} custom-call(bf16[16,16,640]{2,1,0:T(8,128)(2,1)S(1)} %bitcast.11, bf16[1,16,640]{2,1,0:T(8,128)(2,1)S(1)} %copy-done.6, bf16[1,16,640]{2,1,0:T(8,128)(2,1)S(1)} %copy-done.8, bf16[225,640]{1,0:T(8,128)(2,1)S(1)} %collective-permute-done.2.refs_3_, bf16[225,640]{1,0:T(8,128)(2,1)S(1)} %collective-permute-done.3.refs_4_, ...), custom_call_target="tpu_custom_call" | custom-call | tf_op jit(solution)/shard_map/filter_mix_mlp/pallas_call | solution.py:230
  (1 shorter events, 0.0 us)
Async XLA Ops:
  1.8 12.8 %collective-permute-start.8 = (bf16[48,640]{1,0:T(8,128)(2,1)}, bf16[48,640]{1,0:T(8,128)(2,1)S(1)}, u32[]{:S(2)}, u32[]{:S(2)}) collective-permute-start(bf16[48,640]{1,0:T(8,128)(2,1)} %get-tuple-element.18), channel_id=1, source_target_pairs={{8,0},{10,2},{12,4},{14,6},{0,8},{2,10},{4,12},{6,14},{9,1},{11,3}... | collective-permute-start | bytes 184328 | tf_op jit(solution)/shard_map/ppermute | solution.py:214
  2.5 35.7 %copy-start.9 = (f32[640]{0:T(1024)S(1)}, f32[640]{0:T(1024)}, u32[]{:S(2)}) copy-start(f32[640]{0:T(1024)} %param.13) | copy-start | bytes 7684
  2.5 35.8 %copy-start.2 = (bf16[640,16,16]{0,2,1:T(8,128)(2,1)S(1)}, bf16[640,16,16]{0,2,1:T(8,128)(2,1)}, u32[]{:S(2)}) copy-start(bf16[640,16,16]{0,2,1:T(8,128)(2,1)} %param.8) | copy-start | bytes 983044
  2.5 35.8 %copy-start.3 = (bf16[640,1280]{1,0:T(8,128)(2,1)S(1)}, bf16[640,1280]{1,0:T(8,128)(2,1)}, u32[]{:S(2)}) copy-start(bf16[640,1280]{1,0:T(8,128)(2,1)} %refs_13_.1) | copy-start | bytes 4915204
  2.6 6.0 %collective-permute-start = (bf16[1,16,640]{2,1,0:T(8,128)(2,1)S(1)}, bf16[1,16,640]{2,1,0:T(8,128)(2,1)S(1)}, u32[]{:S(2)}, u32[]{:S(2)}) collective-permute-start(bf16[1,16,640]{2,1,0:T(8,128)(2,1)S(1)} %get-tuple-element.20), channel_id=1, source_target_pairs={{0,1},{2,3},{4,5},{6,7},{8,9},{10,11},{12,13},{14,15},{16,17},{18,... | collective-permute-start | bytes 61448 | tf_op jit(solution)/shard_map/ppermute | solution.py:203
  4.4 7.0 %collective-permute-start.1 = (bf16[1,16,640]{2,1,0:T(8,128)(2,1)S(1)}, bf16[1,16,640]{2,1,0:T(8,128)(2,1)S(1)}, u32[]{:S(2)}, u32[]{:S(2)}) collective-permute-start(bf16[1,16,640]{2,1,0:T(8,128)(2,1)S(1)} %get-tuple-element.19), channel_id=1, source_target_pairs={{1,0},{3,2},{5,4},{7,6},{9,8},{11,10},{13,12},{15,14},{17,16},{19,... | collective-permute-start | bytes 61448 | tf_op jit(solution)/shard_map/ppermute | solution.py:204
  5.7 32.5 %collective-permute-start.4 = (bf16[96,640]{1,0:T(8,128)(2,1)}, bf16[96,640]{1,0:T(8,128)(2,1)S(1)}, u32[]{:S(2)}, u32[]{:S(2)}) collective-permute-start(bf16[96,640]{1,0:T(8,128)(2,1)} %get-tuple-element.14), channel_id=1, source_target_pairs={{4,0},{6,2},{8,4},{10,6},{12,8},{14,10},{0,12},{2,14},{5,1},{7,3},... | collective-permute-start | bytes 368648 | tf_op jit(solution)/shard_map/ppermute | solution.py:214
  8.5 29.7 %collective-permute-start.5 = (bf16[96,640]{1,0:T(8,128)(2,1)}, bf16[96,640]{1,0:T(8,128)(2,1)S(1)}, u32[]{:S(2)}, u32[]{:S(2)}) collective-permute-start(bf16[96,640]{1,0:T(8,128)(2,1)} %get-tuple-element.15), channel_id=1, source_target_pairs={{12,0},{14,2},{0,4},{2,6},{4,8},{6,10},{8,12},{10,14},{13,1},{15,3... | collective-permute-start | bytes 368648 | tf_op jit(solution)/shard_map/ppermute | solution.py:214
  8.6 2.8 %copy-start.5 = (bf16[1,16,640]{2,1,0:T(8,128)(2,1)}, bf16[1,16,640]{2,1,0:T(8,128)(2,1)S(1)}, u32[]{:S(2)}) copy-start(bf16[1,16,640]{2,1,0:T(8,128)(2,1)S(1)} %collective-permute-done.refs_1_) | copy-start | bytes 61444
  8.6 10.1 %collective-permute-start.6 = (bf16[58,640]{1,0:T(8,128)(2,1)}, bf16[58,640]{1,0:T(8,128)(2,1)S(1)}, u32[]{:S(2)}, u32[]{:S(2)}) collective-permute-start(bf16[58,640]{1,0:T(8,128)(2,1)} %get-tuple-element.16), channel_id=1, source_target_pairs={{6,0},{8,2},{10,4},{12,6},{14,8},{0,10},{2,12},{4,14},{7,1},{9,3},... | collective-permute-start | bytes 222728 | tf_op jit(solution)/shard_map/ppermute | solution.py:214
  11.4 0.6 %copy-start.7 = (bf16[1,16,640]{2,1,0:T(8,128)(2,1)}, bf16[1,16,640]{2,1,0:T(8,128)(2,1)S(1)}, u32[]{:S(2)}) copy-start(bf16[1,16,640]{2,1,0:T(8,128)(2,1)S(1)} %collective-permute-done.1.refs_2_) | copy-start | bytes 61444
  13.9 24.4 %copy-start.6 = (bf16[1,16,640]{2,1,0:T(8,128)(2,1)S(1)}, bf16[1,16,640]{2,1,0:T(8,128)(2,1)}, u32[]{:S(2)}) copy-start(bf16[1,16,640]{2,1,0:T(8,128)(2,1)} %copy-done.5) | copy-start | bytes 61444
  13.9 24.4 %copy-start.8 = (bf16[1,16,640]{2,1,0:T(8,128)(2,1)S(1)}, bf16[1,16,640]{2,1,0:T(8,128)(2,1)}, u32[]{:S(2)}) copy-start(bf16[1,16,640]{2,1,0:T(8,128)(2,1)} %copy-done.7) | copy-start | bytes 61444
  13.9 24.4 %collective-permute-start.2 = (bf16[225,640]{1,0:T(8,128)(2,1)}, bf16[225,640]{1,0:T(8,128)(2,1)S(1)}, u32[]{:S(2)}, u32[]{:S(2)}) collective-permute-start(bf16[225,640]{1,0:T(8,128)(2,1)} %get-tuple-element.12), channel_id=1, source_target_pairs={{2,0},{4,2},{6,4},{8,6},{10,8},{12,10},{14,12},{0,14},{3,1},{5,3},... | collective-permute-start | bytes 864008 | tf_op jit(solution)/shard_map/ppermute | solution.py:214
  14.6 23.7 %collective-permute-start.3 = (bf16[225,640]{1,0:T(8,128)(2,1)}, bf16[225,640]{1,0:T(8,128)(2,1)S(1)}, u32[]{:S(2)}, u32[]{:S(2)}) collective-permute-start(bf16[225,640]{1,0:T(8,128)(2,1)} %get-tuple-element.13), channel_id=1, source_target_pairs={{14,0},{0,2},{2,4},{4,6},{6,8},{8,10},{10,12},{12,14},{15,1},{1,3}... | collective-permute-start | bytes 864008 | tf_op jit(solution)/shard_map/ppermute | solution.py:214
  18.6 19.6 %collective-permute-start.7 = (bf16[58,640]{1,0:T(8,128)(2,1)}, bf16[58,640]{1,0:T(8,128)(2,1)S(1)}, u32[]{:S(2)}, u32[]{:S(2)}) collective-permute-start(bf16[58,640]{1,0:T(8,128)(2,1)} %get-tuple-element.17), channel_id=1, source_target_pairs={{10,0},{12,2},{14,4},{0,6},{2,8},{4,10},{6,12},{8,14},{11,1},{13,3... | collective-permute-start | bytes 222728 | tf_op jit(solution)/shard_map/ppermute | solution.py:214
  38.3 2.6 %copy-start = (bf16[7,640,640]{2,1,0:T(8,128)(2,1)S(1)}, bf16[7,640,640]{2,1,0:T(8,128)(2,1)}, u32[]{:S(2)}) copy-start(bf16[7,640,640]{2,1,0:T(8,128)(2,1)} %refs_11_.1) | copy-start | bytes 17203204
  41.0 1.3 %copy-start.1 = (bf16[47,112,128]{2,1,0:T(8,128)(2,1)S(1)}, bf16[47,112,128]{2,1,0:T(8,128)(2,1)}, u32[]{:S(2)}) copy-start(bf16[47,112,128]{2,1,0:T(8,128)(2,1)} %filter_taps.1.refs_10_) | copy-start | bytes 4042756
  42.3 1.4 %copy-start.4 = (bf16[1280,640]{1,0:T(8,128)(2,1)S(1)}, bf16[1280,640]{1,0:T(8,128)(2,1)}, u32[]{:S(2)}) copy-start(bf16[1280,640]{1,0:T(8,128)(2,1)} %refs_14_.1) | copy-start | bytes 4915204

commit v3 on v2

v3 whole, which is shorter than its diff:
```python
import functools

import jax
import jax.numpy as jnp
from jax import lax
from jax.experimental import pallas as pl
from jax.experimental.pallas import tpu as pltpu
from jax.sharding import PartitionSpec as P

norm_eps = 1e-05
lanes = 128
mib = 2**20
vmem = pl.BlockSpec(memory_space=pltpu.VMEM)
anywhere = pl.BlockSpec(memory_space=pl.ANY)


class Plan:
    def __init__(self, rows, cols, lat_shards, lon_shards):
        self.rows, self.cols = rows, cols
        self.lat_shards, self.lon_shards = lat_shards, lon_shards
        lat_total, lon_total = rows * lat_shards, cols * lon_shards
        self.lon_total = lon_total
        self.half = half = lon_shards // 2
        self.outer = lat_shards > 2
        reach = [0] * rows
        need = [0] * (rows + 2)
        for shard in range(lat_shards // 2):
            for slot in range(rows):
                row = shard * rows + slot
                span = min(lon_total // 2, 4 * lat_total // min(row + 1, lat_total - row))
                reach[slot] = max(reach[slot], span)
                for source in (slot, slot + 1, slot + 2):
                    if shard > 0 or source > 0:
                        need[source] = max(need[source], span)
        self.blocks = [min(half, -(-span // cols)) for span in reach]
        self.moves = {}
        for dist in range(1, half + 1):
            for sign in (1, -1):
                picks, start = [], 0
                for slot in range(1, rows + 1):
                    if dist >= half - 1:
                        width = cols if need[slot] > (half - 2) * cols else 0
                    else:
                        width = max(0, min(cols, need[slot] - (dist - 1) * cols))
                    if width > 0:
                        picks.append((slot, start, width))
                        start += width
                if picks and (dist < half or sign == 1):
                    self.moves[dist, sign] = picks
        self.margin = max(need[0], need[rows + 1])
        self.margin_blocks = -(-self.margin // cols)

    def payload(self, move):
        _, start, width = self.moves[move][-1]
        return start + width

    def span(self, slot):
        blocks = self.blocks[slot]
        if blocks == self.half:
            return 0, self.lon_total
        return (self.half - 1 - blocks) * self.cols, (2 * blocks + 1) * self.cols

    def sources(self, slot):
        return [s for s in (slot, slot + 1, slot + 2) if s > 0 or self.outer]


def is_south(plan):
    return lax.axis_index("lat") >= plan.lat_shards // 2


def row_of(plan, south, slot):
    return jnp.where(south, plan.rows - slot, slot - 1)


def pack_body(plan, moves, x_ref, *outs):
    south = is_south(plan)
    for move, out in zip(moves, outs):
        for slot, start, width in plan.moves[move]:
            block = x_ref[row_of(plan, south, slot)]
            block = block[:width] if move[1] == 1 else block[plan.cols - width :]
            out[start : start + width] = block


def pack(plan, moves, x):
    return pl.pallas_call(
        functools.partial(pack_body, plan, moves),
        out_shape=[jax.ShapeDtypeStruct((plan.payload(m), x.shape[2]), x.dtype) for m in moves],
        in_specs=[vmem],
        out_specs=[vmem] * len(moves),
        compiler_params=pltpu.CompilerParams(vmem_limit_bytes=8 * mib),
        name="pack_columns",
    )(x)


def strip_of(plan, slot, south, x_ref, got):
    parts = [x_ref[row_of(plan, south, slot)]]
    for dist in range(1, plan.margin_blocks + 1):
        width = min(plan.cols, plan.margin - (dist - 1) * plan.cols)
        for sign in (1, -1):
            (pick,) = [p for p in plan.moves[dist, sign] if p[0] == slot]
            _, start, held = pick
            if sign == 1:
                parts.append(got[dist, sign][start : start + width])
            else:
                parts.insert(0, got[dist, sign][start + held - width : start + held])
    return jnp.concatenate(parts, axis=0)


def strip_body(plan, moves, x_ref, *refs):
    got = dict(zip(moves, refs))
    outs = refs[len(moves) :]
    south = is_south(plan)
    inner = strip_of(plan, plan.rows, south, x_ref, got)
    if not plan.outer:
        outs[0][...] = inner
        return
    outer = strip_of(plan, 1, south, x_ref, got)
    outs[0][...] = jnp.where(south, outer, inner)
    outs[1][...] = jnp.where(south, inner, outer)


def edge_rows(plan, x, got):
    moves = [m for m in plan.moves if m[0] <= plan.margin_blocks]
    count = 2 if plan.outer else 1
    size = plan.cols + 2 * plan.margin
    strips = pl.pallas_call(
        functools.partial(strip_body, plan, moves),
        out_shape=[jax.ShapeDtypeStruct((size, x.shape[2]), x.dtype)] * count,
        in_specs=[vmem] * (1 + len(moves)),
        out_specs=[vmem] * count,
        compiler_params=pltpu.CompilerParams(vmem_limit_bytes=8 * mib),
        name="pack_edge_row",
    )(x, *[got[m] for m in moves])
    if not plan.outer:
        return [lax.ppermute(strips[0], "lat", [(0, 1), (1, 0)])]
    forward = [(i, i + 1) for i in range(plan.lat_shards - 1)]
    low = lax.ppermute(strips[0], "lat", forward)
    high = lax.ppermute(strips[1], "lat", [(b, a) for a, b in forward])
    return [low, high]


def taps_body(plan, entries, lift_ref, place_ref, weight_ref, out):
    size, lat_total = lift_ref.shape
    cols, width = plan.cols, out.shape[2]
    south = is_south(plan)
    row_start = lax.axis_index("lat") * plan.rows
    source_row = lax.broadcasted_iota(jnp.int32, (lat_total, width), 0)
    spot = lax.broadcasted_iota(jnp.int32, (size, width), 1)
    early = lax.broadcasted_iota(jnp.int32, (size, width), 0) // entries * cols
    kinds_rows = size // entries * cols
    basis_row = lax.broadcasted_iota(jnp.int32, (kinds_rows, size), 0) // cols
    basis_col = lax.broadcasted_iota(jnp.int32, (kinds_rows, size), 1) // entries
    gather = jnp.where(basis_row == basis_col, 1.0, 0.0).astype(jnp.bfloat16)
    tables = [ref[...].astype(jnp.bfloat16) for ref in (lift_ref, place_ref, weight_ref)]
    index = 0
    for slot in range(plan.rows):
        center = (plan.half - 1) * cols - plan.span(slot)[0]
        here = source_row == row_start + row_of(plan, south, slot + 1)
        here = jnp.where(here, 1.0, 0.0).astype(jnp.bfloat16)
        lift, place, weight = [
            jnp.dot(table, here, preferred_element_type=jnp.float32) for table in tables
        ]
        lift = jnp.where(south, -lift, lift)
        want = spot + early - center
        gap = want - place.astype(jnp.int32)
        hit = lax.rem(gap + 4 * width, width) == 0
        weight = jnp.where(hit, weight, 0.0)
        for source in plan.sources(slot):
            part = jnp.where(lift == float(source - slot - 1), weight, 0.0).astype(jnp.bfloat16)
            taps = jnp.dot(gather, part, preferred_element_type=jnp.float32)
            taps = pltpu.roll(taps, 0, 1, stride=1, stride_axis=0)
            out[index] = taps.astype(jnp.bfloat16)
            index += 1


def make_taps(plan, support):
    kinds, _, entries = support[0].shape
    count = sum(len(plan.sources(slot)) for slot in range(plan.rows))
    width = -(-plan.lon_total // lanes) * lanes
    tables = [s.transpose(0, 2, 1).reshape(kinds * entries, -1) for s in support]
    return pl.pallas_call(
        functools.partial(taps_body, plan, entries),
        out_shape=jax.ShapeDtypeStruct((count, kinds * plan.cols, width), jnp.bfloat16),
        in_specs=[vmem] * 3,
        out_specs=vmem,
        compiler_params=pltpu.CompilerParams(vmem_limit_bytes=8 * mib),
        cost_estimate=pl.CostEstimate(flops=3 * 10**9, bytes_accessed=10**7, transcendentals=0),
        name="filter_taps",
    )(*tables)


def fill_window(plan, sources, south, x_ref, got, edges, win):
    rows, cols = plan.rows, plan.cols
    middle = (plan.half - 1) * cols
    for slot in sources:
        if slot in (0, rows + 1):
            strip = edges[0][...]
            if plan.outer:
                first, last = (edges[1], edges[0]) if slot == 0 else (edges[0], edges[1])
                strip = jnp.where(south, first[...], last[...])
            gap = plan.margin_blocks * cols - plan.margin
            if gap > 0:
                gap = jnp.zeros((gap, strip.shape[1]), strip.dtype)
                strip = jnp.concatenate([gap, strip, gap], axis=0)
            start = middle - plan.margin_blocks * cols
            win[slot - sources[0], start : start + strip.shape[0]] = strip
        else:
            win[slot - sources[0], middle : middle + cols] = x_ref[row_of(plan, south, slot)]
    for (dist, sign), ref in got.items():
        place = middle + sign * dist * cols
        for slot, start, width in plan.moves[dist, sign]:
            if slot not in sources:
                continue
            block = ref[start : start + width]
            if width < cols:
                gap = jnp.zeros((cols - width, block.shape[1]), block.dtype)
                block = jnp.concatenate([block, gap] if sign == 1 else [gap, block], axis=0)
            win[slot - sources[0], place : place + cols] = block


def compute_body(plan, slots, moves, edge_count, chained, *refs):
    x_ref = refs[0]
    got = dict(zip(moves, refs[1:]))
    used = 1 + len(moves)
    edges = refs[used : used + edge_count]
    used += edge_count
    taps_ref, mix_ref, gain_ref, up_ref, down_ref = refs[used : used + 5]
    used += 5 + chained
    out_ref, win, response, result, sem = refs[used:]
    rows, cols = plan.rows, plan.cols
    kinds = mix_ref.shape[0]
    south = is_south(plan)
    middle = (plan.half - 1) * cols
    sources = sorted({s for slot in slots for s in plan.sources(slot)})
    fill_window(plan, sources, south, x_ref, got, edges, win)
    for order, slot in enumerate(slots):
        first, count = plan.span(slot)
        index = sum(len(plan.sources(s)) for s in range(slot))
        total = None
        for source in plan.sources(slot):
            piece = jnp.dot(
                taps_ref[index, :, :count],
                win[source - sources[0], first : first + count],
                preferred_element_type=jnp.float32,
            )
            total = piece if total is None else total + piece
            index += 1
        total = total.astype(jnp.bfloat16)
        for kind in range(kinds):
            place = slice(order * cols, (order + 1) * cols)
            response[kind, place] = total[kind * cols : (kind + 1) * cols]
    mixed = jnp.dot(response[0], mix_ref[0], preferred_element_type=jnp.float32)
    for kind in range(1, kinds):
        mixed = mixed + jnp.dot(response[kind], mix_ref[kind], preferred_element_type=jnp.float32)
    start = slots[0] + 1 - sources[0]
    own = win[start : start + len(slots), middle : middle + cols]
    latent = own.reshape(len(slots) * cols, -1).astype(jnp.float32) + mixed
    mean = jnp.mean(latent, axis=1, keepdims=True)
    variance = jnp.mean(jnp.square(latent - mean), axis=1, keepdims=True)
    normed = (latent - mean) * lax.rsqrt(variance + norm_eps) * gain_ref[...]
    hidden = jnp.dot(normed.astype(jnp.bfloat16), up_ref[...], preferred_element_type=jnp.float32)
    hidden = (0.5 * hidden * (1.0 + lax.erf(hidden * 0.5**0.5))).astype(jnp.bfloat16)
    output = latent + jnp.dot(hidden, down_ref[...], preferred_element_type=jnp.float32)
    output = output.astype(jnp.bfloat16)
    for order in range(len(slots)):
        spot = jnp.where(south, len(slots) - 1 - order, order)
        result[spot] = output[order * cols : (order + 1) * cols]
    first_row = jnp.where(south, rows - 1 - slots[-1], slots[0])
    copy = pltpu.make_async_copy(result, out_ref.at[pl.ds(first_row, len(slots))], sem)
    copy.start()
    copy.wait()


def compute(plan, slots, x, got, edges, taps, weights, chain):
    sources = sorted({s for slot in slots for s in plan.sources(slot)})
    moves = [m for m, picks in plan.moves.items() if any(p[0] in sources for p in picks)]
    reach = max(plan.blocks[slot] for slot in slots)
    moves = [m for m in moves if m[0] <= reach]
    edges = edges if set(sources) & {0, plan.rows + 1} else []
    args = [x, *[got[m] for m in moves], *edges, taps, *weights]
    specs = [vmem] * len(args)
    if chain is not None:
        args.append(chain)
        specs.append(anywhere)
    channels = x.shape[2]
    kinds = weights[0].shape[0]
    return pl.pallas_call(
        functools.partial(compute_body, plan, slots, moves, len(edges), chain is not None),
        out_shape=jax.ShapeDtypeStruct(x.shape, x.dtype),
        in_specs=specs,
        out_specs=anywhere,
        scratch_shapes=[
            pltpu.VMEM((len(sources), plan.lon_total, channels), x.dtype),
            pltpu.VMEM((kinds, len(slots) * plan.cols, channels), x.dtype),
            pltpu.VMEM((len(slots), plan.cols, channels), x.dtype),
            pltpu.SemaphoreType.DMA,
        ],
        input_output_aliases={} if chain is None else {len(args) - 1: 0},
        compiler_params=pltpu.CompilerParams(vmem_limit_bytes=24 * mib),
        cost_estimate=pl.CostEstimate(flops=10**6, bytes_accessed=10**5, transcendentals=0),
        name="filter_mix_mlp",
    )(*args)


def on_device(
    fields,
    support_rows,
    support_lons,
    support_weights,
    mix_weight,
    norm_gain,
    up_weight,
    down_weight,
):
    channels, rows, cols = fields.shape
    count = lax.axis_size("lon")
    plan = Plan(rows, cols, lax.axis_size("lat"), count)
    half = plan.half
    x = jnp.transpose(fields, (1, 2, 0))

    direct = [m for m in plan.moves if m[0] < half - 1 or m[0] == half]
    sent = dict(zip(direct, pack(plan, direct, x)))

    def shifted(value, step):
        return lax.ppermute(value, "lon", [((i + step) % count, i) for i in range(count)])

    got = {m: shifted(sent[m], m[0] * m[1]) for m in direct}
    taps = make_taps(plan, (support_rows, support_lons, support_weights))
    first = [m for m in got if m[0] <= plan.margin_blocks or m[0] == half]
    joined, taps = lax.optimization_barrier(([got[m] for m in first], taps))
    got.update(zip(first, joined))
    if (half - 1, 1) in plan.moves and half > 2:
        got[half - 1, 1] = shifted(got[half, 1], -1)
        got[half - 1, -1] = shifted(got[half, 1], 1)
    edges = edge_rows(plan, x, got)
    weights = (mix_weight, norm_gain[None], up_weight, down_weight)
    near = [slot for slot in range(rows) if plan.blocks[slot] <= 1]
    far = [slot for slot in range(rows) if plan.blocks[slot] > 1]
    output = None
    for slots in (near, far):
        if slots:
            output = compute(plan, slots, x, got, edges, taps, weights, output)
    return jnp.transpose(output, (2, 0, 1))


def solution(mesh):
    in_specs = (P("member", "lat", "lon"), P(), P(), P(), P(), P(), P(), P())
    out_specs = P("member", "lat", "lon")
    return jax.shard_map(
        on_device, mesh=mesh, in_specs=in_specs, out_specs=out_specs, check_vma=False
    )
```

time: 50.8 us -> 36.5 us (0.72)
  the two profiles are of different devices: /device:TPU:16 before, /device:TPU:0 now
where the time goes in v3:
time: 36.5 us; the launch traced here: 36.3 us
  starting transfers between devices  13.6 us (37%)
  Pallas kernels  12.2 us (33%)
  waiting for transfers between devices  6.59 us (18%)
  local copies, waits for them, and re-layouts  3.85 us (11%)
    ppermute x7, starting transfers between devices, shifted(): lax.ppermute(value, 'lon', [((i + step) % count, i) for i in range(count)])  13.5 us
    pallas_call x2, Pallas kernels, compute(): pl.pallas_call(functools.partial(compute_body, plan, slots, moves, len(ed...  8.11 us
    ppermute x7, waiting for transfers between devices, shifted(): lax.ppermute(value, 'lon', [((i + step) % count, i) for i in range(count)])  5.41 us
    pallas_call x1, Pallas kernels, make_taps(): pl.pallas_call(functools.partial(taps_body, plan, entries), out_shape=jax...  3.95 us
    unnamed x20, local copies, waits for them, and re-layouts  3.84 us
    ppermute x1, waiting for transfers between devices, edge_rows(): return [lax.ppermute(strips[0], 'lat', [(0, 1), (1, 0)])]  1.18 us
  transfers between devices with their start and end apart: 8, of which 4 were waited for; matrix products, arithmetic and copies ran while one was open for 0% of the time, Pallas kernels for 23%

profile of v3, /device:TPU:0, one launch (start us, length us, event | category | flops | bytes accessed | tf_op | source)
XLA Modules:
  0.0 36.3 jit_solution(11676100835289140377)
XLA Ops:
  0.0 0.0 copy-start.2
  0.0 1.0 %copy-done.2 = bf16[640,16,16]{0,2,1:T(8,128)(2,1)S(1)} copy-done((bf16[640,16,16]{0,2,1:T(8,128)(2,1)S(1)}, bf16[640,16,16]{0,2,1:T(8,128)(2,1)}, u32[]{:S(2)}) %copy-start.2) | copy-done | bytes 327704
  1.0 0.1 pack_columns.1
  1.1 4.1 %collective-permute-start.2 = (bf16[64,640]{1,0:T(8,128)(2,1)S(1)}, bf16[64,640]{1,0:T(8,128)(2,1)S(1)}, u32[]{:S(2)}, u32[]{:S(2)}) collective-permute-start(bf16[64,640]{1,0:T(8,128)(2,1)S(1)} %get-tuple-element.16), channel_id=1, source_target_pairs={{8,0},{10,2},{12,4},{14,6},{0,8},{2,10},{4,12},{6,14},{9,1},{11,3}... | collective-permute-start | bytes 245768 | tf_op jit(solution)/shard_map/ppermute | solution.py:325
  5.2 1.3 %collective-permute-start.3 = (bf16[96,640]{1,0:T(8,128)(2,1)S(1)}, bf16[96,640]{1,0:T(8,128)(2,1)S(1)}, u32[]{:S(2)}, u32[]{:S(2)}) collective-permute-start(bf16[96,640]{1,0:T(8,128)(2,1)S(1)} %get-tuple-element.19), channel_id=1, source_target_pairs={{4,0},{6,2},{8,4},{10,6},{12,8},{14,10},{0,12},{2,14},{5,1},{7,3},... | collective-permute-start | bytes 368648 | tf_op jit(solution)/shard_map/ppermute | solution.py:325
  6.6 0.7 %collective-permute-start.4 = (bf16[96,640]{1,0:T(8,128)(2,1)S(1)}, bf16[96,640]{1,0:T(8,128)(2,1)S(1)}, u32[]{:S(2)}, u32[]{:S(2)}) collective-permute-start(bf16[96,640]{1,0:T(8,128)(2,1)S(1)} %get-tuple-element.20), channel_id=1, source_target_pairs={{12,0},{14,2},{0,4},{2,6},{4,8},{6,10},{8,12},{10,14},{13,1},{15,3... | collective-permute-start | bytes 368648 | tf_op jit(solution)/shard_map/ppermute | solution.py:325
  7.2 4.1 %collective-permute-start = (bf16[217,640]{1,0:T(8,128)(2,1)S(1)}, bf16[217,640]{1,0:T(8,128)(2,1)S(1)}, u32[]{:S(2)}, u32[]{:S(2)}) collective-permute-start(bf16[217,640]{1,0:T(8,128)(2,1)S(1)} %get-tuple-element.14), channel_id=1, source_target_pairs={{2,0},{4,2},{6,4},{8,6},{10,8},{12,10},{14,12},{0,14},{3,1},{5,3},... | collective-permute-start | bytes 833288 | tf_op jit(solution)/shard_map/ppermute | solution.py:325
  11.3 0.0 collective-permute-start.1
  11.3 0.0 slice-start
  11.3 0.0 copy-start.4
  11.3 1.0 %copy-done.4 = s32[7,32,16]{1,2,0:T(8,128)S(1)} copy-done((s32[7,32,16]{1,2,0:T(8,128)S(1)}, s32[7,32,16]{1,2,0:T(8,128)}, u32[]{:S(2)}) %copy-start.4) | copy-done | bytes 14360
  12.3 0.0 copy-start.5
  12.3 1.1 %copy-done.5 = s32[7,32,16]{1,2,0:T(8,128)S(1)} copy-done((s32[7,32,16]{1,2,0:T(8,128)S(1)}, s32[7,32,16]{1,2,0:T(8,128)}, u32[]{:S(2)}) %copy-start.5) | copy-done | bytes 14360
  13.3 0.0 copy-start.6
  13.3 0.8 %copy-done.6 = f32[7,32,16]{1,2,0:T(8,128)S(1)} copy-done((f32[7,32,16]{1,2,0:T(8,128)S(1)}, f32[7,32,16]{1,2,0:T(8,128)}, u32[]{:S(2)}) %copy-start.6) | copy-done | bytes 14360
  14.2 0.0 copy-start.3
  14.2 0.0 copy-start.7
  14.2 0.0 slice-start.1
  14.2 0.0 copy-start
  14.2 0.0 copy-start.1
  14.2 3.9 %filter_taps.1.refs_4_.refs_8_ = bf16[47,112,128]{2,1,0:T(8,128)(2,1)S(1)} custom-call(s32[112,32]{1,0:T(8,128)S(1)} %bitcast.17, s32[112,32]{1,0:T(8,128)S(1)} %bitcast.18, f32[112,32]{1,0:T(8,128)S(1)} %bitcast.19), custom_call_target="tpu_custom_call" | custom-call | flops 3000000000 | bytes 10000000 | tf_op jit(solution)/shard_map/filter_taps/pallas_call | solution.py:181
  18.1 0.0 collective-permute-done.2.refs_7_
  18.1 0.4 %collective-permute-done.refs_0_.refs_1_ = bf16[217,640]{1,0:T(8,128)(2,1)S(1)} collective-permute-done((bf16[217,640]{1,0:T(8,128)(2,1)S(1)}, bf16[217,640]{1,0:T(8,128)(2,1)S(1)}, u32[]{:S(2)}, u32[]{:S(2)}) %collective-permute-start) | collective-permute-done | bytes 277792 | tf_op jit(solution)/shard_map/ppermute | solution.py:325
  18.6 3.6 %collective-permute-done.1.refs_1_.refs_2_ = bf16[217,640]{1,0:T(8,128)(2,1)S(1)} collective-permute-done((bf16[217,640]{1,0:T(8,128)(2,1)S(1)}, bf16[217,640]{1,0:T(8,128)(2,1)S(1)}, u32[]{:S(2)}, u32[]{:S(2)}) %collective-permute-start.1) | collective-permute-done | bytes 277792 | tf_op jit(solution)/shard_map/ppermute | solution.py:325
  22.2 3.3 %collective-permute-start.6 = (bf16[64,640]{1,0:T(8,128)(2,1)S(1)}, bf16[64,640]{1,0:T(8,128)(2,1)S(1)}, u32[]{:S(2)}, u32[]{:S(2)}) collective-permute-start(bf16[64,640]{1,0:T(8,128)(2,1)S(1)} %collective-permute-done.2.refs_7_), channel_id=1, source_target_pairs={{2,0},{4,2},{6,4},{8,6},{10,8},{12,10},{14,12},{0,14},{3,1},{5,3},... | collective-permute-start | bytes 245768 | tf_op jit(solution)/shard_map/ppermute | solution.py:325
  25.4 0.0 collective-permute-start.5
  25.5 0.0 copy-done.3
  25.5 0.1 collective-permute-start.7
  25.6 0.0 copy-done.7
  25.6 1.2 %collective-permute-done.7.refs_3_ = bf16[32,640]{1,0:T(8,128)(2,1)S(1)} collective-permute-done((bf16[32,640]{1,0:T(8,128)(2,1)S(1)}, bf16[32,640]{1,0:T(8,128)(2,1)S(1)}, u32[]{:S(2)}, u32[]{:S(2)}) %collective-permute-start.7) | collective-permute-done | bytes 40992 | tf_op jit(solution)/shard_map/ppermute | solution.py:135
  26.8 0.0 slice-done
  26.8 0.0 slice-done.1
  26.8 0.0 copy-done
  26.8 0.0 copy-done.1
  26.8 4.4 %filter_mix_mlp.2.refs_13_ = bf16[16,16,640]{2,1,0:T(8,128)(2,1)} custom-call(bf16[16,16,640]{2,1,0:T(8,128)(2,1)S(1)} %bitcast.15, bf16[217,640]{1,0:T(8,128)(2,1)S(1)} %collective-permute-done.refs_0_.refs_1_, bf16[217,640]{1,0:T(8,128)(2,1)S(1)} %collective-permute-done.1.refs_1_.refs_2_, bf16[32,640]{1,0:T(8,128)(2,1)S(1)} %collective-permute-done.7.refs_3_, ...), custom_call_target="tpu_custom_call" | custom-call | flops 1000000 | bytes 100000 | tf_op jit(solution)/shard_map/filter_mix_mlp/pallas_call | solution.py:287
  31.2 0.0 collective-permute-done.3.refs_3_
  31.2 0.0 collective-permute-done.4.refs_4_
  31.2 0.0 collective-permute-done.6.refs_6_
  31.2 1.4 %collective-permute-done.5.refs_5_ = bf16[64,640]{1,0:T(8,128)(2,1)S(1)} collective-permute-done((bf16[64,640]{1,0:T(8,128)(2,1)S(1)}, bf16[64,640]{1,0:T(8,128)(2,1)S(1)}, u32[]{:S(2)}, u32[]{:S(2)}) %collective-permute-start.5) | collective-permute-done | bytes 81952 | tf_op jit(solution)/shard_map/ppermute | solution.py:325
  32.6 3.7 %filter_mix_mlp.3 = bf16[16,16,640]{2,1,0:T(8,128)(2,1)} custom-call(bf16[16,16,640]{2,1,0:T(8,128)(2,1)S(1)} %bitcast.16, bf16[217,640]{1,0:T(8,128)(2,1)S(1)} %collective-permute-done.refs_0_.refs_1_, bf16[217,640]{1,0:T(8,128)(2,1)S(1)} %collective-permute-done.1.refs_1_.refs_2_, ...), custom_call_target="tpu_custom_call", output_to_operand_aliasing={{}: (13, {})} | custom-call | flops 1000000 | bytes 100000 | tf_op jit(solution)/shard_map/filter_mix_mlp/pallas_call | solution.py:287
  (3 shorter events, 0.0 us)
Async XLA Ops:
  0.0 1.0 %copy-start.2 = (bf16[640,16,16]{0,2,1:T(8,128)(2,1)S(1)}, bf16[640,16,16]{0,2,1:T(8,128)(2,1)}, u32[]{:S(2)}) copy-start(bf16[640,16,16]{0,2,1:T(8,128)(2,1)} %param.8) | copy-start | bytes 983044
  1.1 17.0 %collective-permute-start.2 = (bf16[64,640]{1,0:T(8,128)(2,1)S(1)}, bf16[64,640]{1,0:T(8,128)(2,1)S(1)}, u32[]{:S(2)}, u32[]{:S(2)}) collective-permute-start(bf16[64,640]{1,0:T(8,128)(2,1)S(1)} %get-tuple-element.16), channel_id=1, source_target_pairs={{8,0},{10,2},{12,4},{14,6},{0,8},{2,10},{4,12},{6,14},{9,1},{11,3}... | collective-permute-start | bytes 245768 | tf_op jit(solution)/shard_map/ppermute | solution.py:325
  5.2 26.0 %collective-permute-start.3 = (bf16[96,640]{1,0:T(8,128)(2,1)S(1)}, bf16[96,640]{1,0:T(8,128)(2,1)S(1)}, u32[]{:S(2)}, u32[]{:S(2)}) collective-permute-start(bf16[96,640]{1,0:T(8,128)(2,1)S(1)} %get-tuple-element.19), channel_id=1, source_target_pairs={{4,0},{6,2},{8,4},{10,6},{12,8},{14,10},{0,12},{2,14},{5,1},{7,3},... | collective-permute-start | bytes 368648 | tf_op jit(solution)/shard_map/ppermute | solution.py:325
  6.6 24.6 %collective-permute-start.4 = (bf16[96,640]{1,0:T(8,128)(2,1)S(1)}, bf16[96,640]{1,0:T(8,128)(2,1)S(1)}, u32[]{:S(2)}, u32[]{:S(2)}) collective-permute-start(bf16[96,640]{1,0:T(8,128)(2,1)S(1)} %get-tuple-element.20), channel_id=1, source_target_pairs={{12,0},{14,2},{0,4},{2,6},{4,8},{6,10},{8,12},{10,14},{13,1},{15,3... | collective-permute-start | bytes 368648 | tf_op jit(solution)/shard_map/ppermute | solution.py:325
  7.2 11.3 %collective-permute-start = (bf16[217,640]{1,0:T(8,128)(2,1)S(1)}, bf16[217,640]{1,0:T(8,128)(2,1)S(1)}, u32[]{:S(2)}, u32[]{:S(2)}) collective-permute-start(bf16[217,640]{1,0:T(8,128)(2,1)S(1)} %get-tuple-element.14), channel_id=1, source_target_pairs={{2,0},{4,2},{6,4},{8,6},{10,8},{12,10},{14,12},{0,14},{3,1},{5,3},... | collective-permute-start | bytes 833288 | tf_op jit(solution)/shard_map/ppermute | solution.py:325
  11.3 10.8 %collective-permute-start.1 = (bf16[217,640]{1,0:T(8,128)(2,1)S(1)}, bf16[217,640]{1,0:T(8,128)(2,1)S(1)}, u32[]{:S(2)}, u32[]{:S(2)}) collective-permute-start(bf16[217,640]{1,0:T(8,128)(2,1)S(1)} %get-tuple-element.15), channel_id=1, source_target_pairs={{14,0},{0,2},{2,4},{4,6},{6,8},{8,10},{10,12},{12,14},{15,1},{1,3}... | collective-permute-start | bytes 833288 | tf_op jit(solution)/shard_map/ppermute | solution.py:325
  11.3 15.5 %slice-start = ((s8[5734400]{0:T(1024)(128)(4,1)}), s8[4194304]{0:T(1024)(128)(4,1)S(1)}, s32[]{:S(2)}) async-start(s8[5734400]{0:T(1024)(128)(4,1)} %bitcast.11), calls=%async_computation | async-start | bytes 8388608
  11.3 1.0 %copy-start.4 = (s32[7,32,16]{1,2,0:T(8,128)S(1)}, s32[7,32,16]{1,2,0:T(8,128)}, u32[]{:S(2)}) copy-start(s32[7,32,16]{1,2,0:T(8,128)} %param.9) | copy-start | bytes 43012
  12.3 1.1 %copy-start.5 = (s32[7,32,16]{1,2,0:T(8,128)S(1)}, s32[7,32,16]{1,2,0:T(8,128)}, u32[]{:S(2)}) copy-start(s32[7,32,16]{1,2,0:T(8,128)} %param.10) | copy-start | bytes 43012
  13.3 0.8 %copy-start.6 = (f32[7,32,16]{1,2,0:T(8,128)S(1)}, f32[7,32,16]{1,2,0:T(8,128)}, u32[]{:S(2)}) copy-start(f32[7,32,16]{1,2,0:T(8,128)} %param.11) | copy-start | bytes 43012
  14.2 11.3 %copy-start.3 = (bf16[640,16,16]{0,2,1:T(8,128)(2,1)S(1)}, bf16[640,16,16]{0,2,1:T(8,128)(2,1)}, u32[]{:S(2)}) copy-start(bf16[640,16,16]{0,2,1:T(8,128)(2,1)} %param.8) | copy-start | bytes 983044
  14.2 11.4 %copy-start.7 = (f32[640]{0:T(1024)S(1)}, f32[640]{0:T(1024)}, u32[]{:S(2)}) copy-start(f32[640]{0:T(1024)} %param.13) | copy-start | bytes 7684
  14.2 12.6 %slice-start.1 = ((s8[5734400]{0:T(1024)(128)(4,1)}), s8[1540096]{0:T(1024)(128)(4,1)S(1)}, s32[]{:S(2)}) async-start(s8[5734400]{0:T(1024)(128)(4,1)} %bitcast.11), calls=%async_computation.1 | async-start | bytes 3080192
  14.2 12.6 %copy-start = (bf16[640,1280]{1,0:T(8,128)(2,1)S(1)}, bf16[640,1280]{1,0:T(8,128)(2,1)}, u32[]{:S(2)}) copy-start(bf16[640,1280]{1,0:T(8,128)(2,1)} %refs_11_.1) | copy-start | bytes 4915204
  14.2 12.6 %copy-start.1 = (bf16[1280,640]{1,0:T(8,128)(2,1)S(1)}, bf16[1280,640]{1,0:T(8,128)(2,1)}, u32[]{:S(2)}) copy-start(bf16[1280,640]{1,0:T(8,128)(2,1)} %refs_12_.1) | copy-start | bytes 4915204
  22.2 9.0 %collective-permute-start.6 = (bf16[64,640]{1,0:T(8,128)(2,1)S(1)}, bf16[64,640]{1,0:T(8,128)(2,1)S(1)}, u32[]{:S(2)}, u32[]{:S(2)}) collective-permute-start(bf16[64,640]{1,0:T(8,128)(2,1)S(1)} %collective-permute-done.2.refs_7_), channel_id=1, source_target_pairs={{2,0},{4,2},{6,4},{8,6},{10,8},{12,10},{14,12},{0,14},{3,1},{5,3},... | collective-permute-start | bytes 245768 | tf_op jit(solution)/shard_map/ppermute | solution.py:325
  25.4 7.1 %collective-permute-start.5 = (bf16[64,640]{1,0:T(8,128)(2,1)S(1)}, bf16[64,640]{1,0:T(8,128)(2,1)S(1)}, u32[]{:S(2)}, u32[]{:S(2)}) collective-permute-start(bf16[64,640]{1,0:T(8,128)(2,1)S(1)} %collective-permute-done.2.refs_7_), channel_id=1, source_target_pairs={{14,0},{0,2},{2,4},{4,6},{6,8},{8,10},{10,12},{12,14},{15,1},{1,3}... | collective-permute-start | bytes 245768 | tf_op jit(solution)/shard_map/ppermute | solution.py:325
  25.5 1.3 %collective-permute-start.7 = (bf16[32,640]{1,0:T(8,128)(2,1)S(1)}, bf16[32,640]{1,0:T(8,128)(2,1)S(1)}, u32[]{:S(2)}, u32[]{:S(2)}) collective-permute-start(bf16[32,640]{1,0:T(8,128)(2,1)S(1)} %pack_edge_row.1), channel_id=1, source_target_pairs={{0,1},{1,0},{2,3},{3,2},{4,5},{5,4},{6,7},{7,6},{8,9},{9,8},{10,11... | collective-permute-start | bytes 122888 | tf_op jit(solution)/shard_map/ppermute | solution.py:135

commit v4 on v3

--- a/solution.py
+++ b/solution.py
@@ -60,6 +60,9 @@
             return 0, self.lon_total
         return (self.half - 1 - blocks) * self.cols, (2 * blocks + 1) * self.cols
 
+    def taps_width(self, slot):
+        return -(-len(self.sources(slot)) * self.span(slot)[1] // lanes) * lanes
+
     def sources(self, slot):
         return [s for s in (slot, slot + 1, slot + 2) if s > 0 or self.outer]
 
@@ -144,7 +147,7 @@
     cols, width = plan.cols, out.shape[2]
     south = is_south(plan)
     row_start = lax.axis_index("lat") * plan.rows
-    source_row = lax.broadcasted_iota(jnp.int32, (lat_total, width), 0)
+    source_row = lax.broadcasted_iota(jnp.int32, (lat_total, lanes), 0)
     spot = lax.broadcasted_iota(jnp.int32, (size, width), 1)
     early = lax.broadcasted_iota(jnp.int32, (size, width), 0) // entries * cols
     kinds_rows = size // entries * cols
@@ -152,35 +155,41 @@
     basis_col = lax.broadcasted_iota(jnp.int32, (kinds_rows, size), 1) // entries
     gather = jnp.where(basis_row == basis_col, 1.0, 0.0).astype(jnp.bfloat16)
     tables = [ref[...].astype(jnp.bfloat16) for ref in (lift_ref, place_ref, weight_ref)]
-    index = 0
     for slot in range(plan.rows):
-        center = (plan.half - 1) * cols - plan.span(slot)[0]
+        first, count = plan.span(slot)
+        center = (plan.half - 1) * cols - first
         here = source_row == row_start + row_of(plan, south, slot + 1)
         here = jnp.where(here, 1.0, 0.0).astype(jnp.bfloat16)
         lift, place, weight = [
             jnp.dot(table, here, preferred_element_type=jnp.float32) for table in tables
         ]
-        lift = jnp.where(south, -lift, lift)
-        want = spot + early - center
-        gap = want - place.astype(jnp.int32)
-        hit = lax.rem(gap + 4 * width, width) == 0
-        weight = jnp.where(hit, weight, 0.0)
-        for source in plan.sources(slot):
-            part = jnp.where(lift == float(source - slot - 1), weight, 0.0).astype(jnp.bfloat16)
+        lift = jnp.where(south, -lift, lift).astype(jnp.int32)
+        place = place.astype(jnp.int32) + center
+        sources = plan.sources(slot)
+        if count == plan.lon_total:
+            pieces = [(source - slot - 1, order * count) for order, source in enumerate(sources)]
+            size = count
+        else:
+            place = place + (lift + slot + 1 - sources[0]) * count
+            pieces, size = [(None, 0)], plan.taps_width(slot)
+        for offset, start in pieces:
+            gap = spot[:, :size] + early[:, :size] - place[:, :1]
+            hit = lax.rem(gap + 4 * size, size) == 0
+            if offset is not None:
+                hit = hit & (lift[:, :1] == offset)
+            part = jnp.where(hit, weight[:, :1], 0.0).astype(jnp.bfloat16)
             taps = jnp.dot(gather, part, preferred_element_type=jnp.float32)
             taps = pltpu.roll(taps, 0, 1, stride=1, stride_axis=0)
-            out[index] = taps.astype(jnp.bfloat16)
-            index += 1
+            out[slot, :, start : start + size] = taps.astype(jnp.bfloat16)
 
 
 def make_taps(plan, support):
     kinds, _, entries = support[0].shape
-    count = sum(len(plan.sources(slot)) for slot in range(plan.rows))
-    width = -(-plan.lon_total // lanes) * lanes
+    width = max(plan.taps_width(slot) for slot in range(plan.rows))
     tables = [s.transpose(0, 2, 1).reshape(kinds * entries, -1) for s in support]
     return pl.pallas_call(
         functools.partial(taps_body, plan, entries),
-        out_shape=jax.ShapeDtypeStruct((count, kinds * plan.cols, width), jnp.bfloat16),
+        out_shape=jax.ShapeDtypeStruct((plan.rows, kinds * plan.cols, width), jnp.bfloat16),
         in_specs=[vmem] * 3,
         out_specs=vmem,
         compiler_params=pltpu.CompilerParams(vmem_limit_bytes=8 * mib),
@@ -203,9 +212,9 @@
                 gap = jnp.zeros((gap, strip.shape[1]), strip.dtype)
                 strip = jnp.concatenate([gap, strip, gap], axis=0)
             start = middle - plan.margin_blocks * cols
-            win[slot - sources[0], start : start + strip.shape[0]] = strip
+            win[sources.index(slot), start : start + strip.shape[0]] = strip
         else:
-            win[slot - sources[0], middle : middle + cols] = x_ref[row_of(plan, south, slot)]
+            win[sources.index(slot), middle : middle + cols] = x_ref[row_of(plan, south, slot)]
     for (dist, sign), ref in got.items():
         place = middle + sign * dist * cols
         for slot, start, width in plan.moves[dist, sign]:
@@ -215,7 +224,7 @@
             if width < cols:
                 gap = jnp.zeros((cols - width, block.shape[1]), block.dtype)
                 block = jnp.concatenate([block, gap] if sign == 1 else [gap, block], axis=0)
-            win[slot - sources[0], place : place + cols] = block
+            win[sources.index(slot), place : place + cols] = block
 
 
 def compute_body(plan, slots, moves, edge_count, chained, *refs):
@@ -235,16 +244,12 @@
     fill_window(plan, sources, south, x_ref, got, edges, win)
     for order, slot in enumerate(slots):
         first, count = plan.span(slot)
-        index = sum(len(plan.sources(s)) for s in range(slot))
-        total = None
-        for source in plan.sources(slot):
-            piece = jnp.dot(
-                taps_ref[index, :, :count],
-                win[source - sources[0], first : first + count],
-                preferred_element_type=jnp.float32,
-            )
-            total = piece if total is None else total + piece
-            index += 1
+        found = [win[sources.index(s), first : first + count] for s in plan.sources(slot)]
+        total = jnp.dot(
+            taps_ref[slot, :, : count * len(found)],
+            jnp.concatenate(found, axis=0),
+            preferred_element_type=jnp.float32,
+        )
         total = total.astype(jnp.bfloat16)
         for kind in range(kinds):
             place = slice(order * cols, (order + 1) * cols)
@@ -252,9 +257,8 @@
     mixed = jnp.dot(response[0], mix_ref[0], preferred_element_type=jnp.float32)
     for kind in range(1, kinds):
         mixed = mixed + jnp.dot(response[kind], mix_ref[kind], preferred_element_type=jnp.float32)
-    start = slots[0] + 1 - sources[0]
-    own = win[start : start + len(slots), middle : middle + cols]
-    latent = own.reshape(len(slots) * cols, -1).astype(jnp.float32) + mixed
+    own = [win[sources.index(slot + 1), middle : middle + cols] for slot in slots]
+    latent = jnp.concatenate(own, axis=0).astype(jnp.float32) + mixed
     mean = jnp.mean(latent, axis=1, keepdims=True)
     variance = jnp.mean(jnp.square(latent - mean), axis=1, keepdims=True)
     normed = (latent - mean) * lax.rsqrt(variance + norm_eps) * gain_ref[...]
@@ -262,13 +266,30 @@
     hidden = (0.5 * hidden * (1.0 + lax.erf(hidden * 0.5**0.5))).astype(jnp.bfloat16)
     output = latent + jnp.dot(hidden, down_ref[...], preferred_element_type=jnp.float32)
     output = output.astype(jnp.bfloat16)
-    for order in range(len(slots)):
-        spot = jnp.where(south, len(slots) - 1 - order, order)
-        result[spot] = output[order * cols : (order + 1) * cols]
-    first_row = jnp.where(south, rows - 1 - slots[-1], slots[0])
-    copy = pltpu.make_async_copy(result, out_ref.at[pl.ds(first_row, len(slots))], sem)
-    copy.start()
-    copy.wait()
+    copies = []
+    for number, (offset, run) in enumerate(runs_of(slots)):
+        size = len(run)
+        for order in range(size):
+            spot = offset + jnp.where(south, size - 1 - order, order)
+            place = (offset + order) * cols
+            result[spot] = output[place : place + cols]
+        first_row = jnp.where(south, rows - 1 - run[-1], run[0])
+        source = result.at[pl.ds(offset, size)]
+        target = out_ref.at[pl.ds(first_row, size)]
+        copies.append(pltpu.make_async_copy(source, target, sem.at[number]))
+        copies[-1].start()
+    for copy in copies:
+        copy.wait()
+
+
+def runs_of(slots):
+    runs = []
+    for position, slot in enumerate(slots):
+        if runs and runs[-1][1][-1] + 1 == slot:
+            runs[-1][1].append(slot)
+        else:
+            runs.append((position, [slot]))
+    return runs
 
 
 def compute(plan, slots, x, got, edges, taps, weights, chain):
@@ -293,7 +314,7 @@
             pltpu.VMEM((len(sources), plan.lon_total, channels), x.dtype),
             pltpu.VMEM((kinds, len(slots) * plan.cols, channels), x.dtype),
             pltpu.VMEM((len(slots), plan.cols, channels), x.dtype),
-            pltpu.SemaphoreType.DMA,
+            pltpu.SemaphoreType.DMA((len(runs_of(slots)),)),
         ],
         input_output_aliases={} if chain is None else {len(args) - 1: 0},
         compiler_params=pltpu.CompilerParams(vmem_limit_bytes=24 * mib),
@@ -319,23 +340,31 @@
     x = jnp.transpose(fields, (1, 2, 0))
 
     direct = [m for m in plan.moves if m[0] < half - 1 or m[0] == half]
-    sent = dict(zip(direct, pack(plan, direct, x)))
+    close = [m for m in direct if m[0] == 1]
+    wide = [m for m in direct if m[0] > 1]
+    sent = dict(zip(close, pack(plan, close, x)))
+    later, sent[1, 1], sent[1, -1] = lax.optimization_barrier((x, sent[1, 1], sent[1, -1]))
+    sent.update(zip(wide, pack(plan, wide, later)))
 
     def shifted(value, step):
         return lax.ppermute(value, "lon", [((i + step) % count, i) for i in range(count)])
 
     got = {m: shifted(sent[m], m[0] * m[1]) for m in direct}
+    forward = (half - 1, 1) in plan.moves and half > 2
+    if forward:
+        got[half - 1, 1] = shifted(got[half, 1], -1)
     taps = make_taps(plan, (support_rows, support_lons, support_weights))
-    first = [m for m in got if m[0] <= plan.margin_blocks or m[0] == half]
+    if forward:
+        opposite, taps = lax.optimization_barrier((got[half, 1], taps))
+        got[half - 1, -1] = shifted(opposite, 1)
+    first = [m for m in got if m[0] <= plan.margin_blocks]
     joined, taps = lax.optimization_barrier(([got[m] for m in first], taps))
     got.update(zip(first, joined))
-    if (half - 1, 1) in plan.moves and half > 2:
-        got[half - 1, 1] = shifted(got[half, 1], -1)
-        got[half - 1, -1] = shifted(got[half, 1], 1)
     edges = edge_rows(plan, x, got)
     weights = (mix_weight, norm_gain[None], up_weight, down_weight)
-    near = [slot for slot in range(rows) if plan.blocks[slot] <= 1]
-    far = [slot for slot in range(rows) if plan.blocks[slot] > 1]
+    inner = range(1 if plan.outer else 0, rows - 1)
+    near = [slot for slot in inner if plan.blocks[slot] <= 1]
+    far = [slot for slot in range(rows) if slot not in near]
     output = None
     for slots in (near, far):
         if slots:

time: 36.5 us -> 31.4 us (0.86)
  waiting for transfers between devices: 6.59 us -> 1.26 us
  starting transfers between devices: 13.6 us -> 14.5 us
  Pallas kernels: 12.2 us -> 11.5 us
    ppermute x7, waiting for transfers between devices: 5.41 us -> 1.26 us  [shifted(): lax.ppermute(value, 'lon', [((i + step) % count, i) for i in range(count)])]
    pallas_call x2, Pallas kernels: 8.11 us -> 6.73 us  [compute(): pl.pallas_call(functools.partial(compute_body, plan, slots, moves, len(ed...]
    ppermute x1, waiting for transfers between devices: 1.18 us -> 0.01 us  [edge_rows(): return [lax.ppermute(strips[0], 'lat', [(0, 1), (1, 0)])]]
    ppermute x7, starting transfers between devices: 13.5 us -> 14.4 us  [shifted(): lax.ppermute(value, 'lon', [((i + step) % count, i) for i in range(count)])]
    pallas_call x1, Pallas kernels: 3.95 us -> 4.62 us  [make_taps(): pl.pallas_call(functools.partial(taps_body, plan, entries), out_shape=jax...]
  transfers between devices with their start and end apart: 8 -> 8, of which waited for: 4 -> 1; matrix products, arithmetic and copies ran while one was open for 0% -> 0% of each run, Pallas kernels for 23% -> 25%
where the time goes in v4:
time: 31.4 us; the launch traced here: 31.2 us
  starting transfers between devices  14.5 us (46%)
  Pallas kernels  11.5 us (37%)
  local copies, waits for them, and re-layouts  3.85 us (12%)
  waiting for transfers between devices  1.26 us (4%)
    ppermute x7, starting transfers between devices, shifted(): lax.ppermute(value, 'lon', [((i + step) % count, i) for i in range(count)])  14.4 us
    pallas_call x2, Pallas kernels, compute(): pl.pallas_call(functools.partial(compute_body, plan, slots, moves, len(ed...  6.73 us
    pallas_call x1, Pallas kernels, make_taps(): pl.pallas_call(functools.partial(taps_body, plan, entries), out_shape=jax...  4.62 us
    unnamed x20, local copies, waits for them, and re-layouts  3.84 us
    ppermute x7, waiting for transfers between devices, shifted(): lax.ppermute(value, 'lon', [((i + step) % count, i) for i in range(count)])  1.26 us
  transfers between devices with their start and end apart: 8, of which 1 were waited for; matrix products, arithmetic and copies ran while one was open for 0% of the time, Pallas kernels for 25%

profile of v4, /device:TPU:0, one launch (start us, length us, event | category | flops | bytes accessed | tf_op | source)
XLA Modules:
  0.0 31.2 jit_solution(9563868334823026055)
XLA Ops:
  0.0 0.0 copy-start
  0.0 1.0 %copy-done = bf16[640,16,16]{0,2,1:T(8,128)(2,1)S(1)} copy-done((bf16[640,16,16]{0,2,1:T(8,128)(2,1)S(1)}, bf16[640,16,16]{0,2,1:T(8,128)(2,1)}, u32[]{:S(2)}) %copy-start) | copy-done | bytes 327704
  1.0 0.1 pack_columns.2
  1.1 6.0 %collective-permute-start = (bf16[217,640]{1,0:T(8,128)(2,1)S(1)}, bf16[217,640]{1,0:T(8,128)(2,1)S(1)}, u32[]{:S(2)}, u32[]{:S(2)}) collective-permute-start(bf16[217,640]{1,0:T(8,128)(2,1)S(1)} %get-tuple-element.20), channel_id=1, source_target_pairs={{2,0},{4,2},{6,4},{8,6},{10,8},{12,10},{14,12},{0,14},{3,1},{5,3},... | collective-permute-start | bytes 833288 | tf_op jit(solution)/shard_map/ppermute | solution.py:350
  7.1 0.0 collective-permute-start.1
  7.1 0.1 collective-permute-start.2
  7.3 1.3 %collective-permute-start.3 = (bf16[96,640]{1,0:T(8,128)(2,1)S(1)}, bf16[96,640]{1,0:T(8,128)(2,1)S(1)}, u32[]{:S(2)}, u32[]{:S(2)}) collective-permute-start(bf16[96,640]{1,0:T(8,128)(2,1)S(1)} %get-tuple-element.27), channel_id=1, source_target_pairs={{4,0},{6,2},{8,4},{10,6},{12,8},{14,10},{0,12},{2,14},{5,1},{7,3},... | collective-permute-start | bytes 368648 | tf_op jit(solution)/shard_map/ppermute | solution.py:350
  8.6 0.7 %collective-permute-start.4 = (bf16[96,640]{1,0:T(8,128)(2,1)S(1)}, bf16[96,640]{1,0:T(8,128)(2,1)S(1)}, u32[]{:S(2)}, u32[]{:S(2)}) collective-permute-start(bf16[96,640]{1,0:T(8,128)(2,1)S(1)} %get-tuple-element.28), channel_id=1, source_target_pairs={{12,0},{14,2},{0,4},{2,6},{4,8},{6,10},{8,12},{10,14},{13,1},{15,3... | collective-permute-start | bytes 368648 | tf_op jit(solution)/shard_map/ppermute | solution.py:350
  9.3 0.0 slice-start
  9.3 0.0 copy-start.4
  9.3 1.0 %copy-done.4 = s32[7,32,16]{1,2,0:T(8,128)S(1)} copy-done((s32[7,32,16]{1,2,0:T(8,128)S(1)}, s32[7,32,16]{1,2,0:T(8,128)}, u32[]{:S(2)}) %copy-start.4) | copy-done | bytes 14360
  10.3 0.0 copy-start.5
  10.3 1.1 %copy-done.5 = s32[7,32,16]{1,2,0:T(8,128)S(1)} copy-done((s32[7,32,16]{1,2,0:T(8,128)S(1)}, s32[7,32,16]{1,2,0:T(8,128)}, u32[]{:S(2)}) %copy-start.5) | copy-done | bytes 14360
  11.3 0.0 copy-start.6
  11.3 0.8 %copy-done.6 = f32[7,32,16]{1,2,0:T(8,128)S(1)} copy-done((f32[7,32,16]{1,2,0:T(8,128)S(1)}, f32[7,32,16]{1,2,0:T(8,128)}, u32[]{:S(2)}) %copy-start.6) | copy-done | bytes 14360
  12.2 0.0 copy-start.1
  12.2 0.0 copy-start.7
  12.2 0.0 slice-start.1
  12.2 0.0 copy-start.2
  12.2 0.0 copy-start.3
  12.2 4.6 %filter_taps.1.refs_3_.refs_9_ = bf16[16,112,384]{2,1,0:T(8,128)(2,1)S(1)} custom-call(s32[112,32]{1,0:T(8,128)S(1)} %bitcast.18, s32[112,32]{1,0:T(8,128)S(1)} %bitcast.19, f32[112,32]{1,0:T(8,128)S(1)} %bitcast.20), custom_call_target="tpu_custom_call" | custom-call | flops 3000000000 | bytes 10000000 | tf_op jit(solution)/shard_map/filter_taps/pallas_call | solution.py:190
  16.8 1.2 %collective-permute-done.2.refs_7_ = bf16[64,640]{1,0:T(8,128)(2,1)S(1)} collective-permute-done((bf16[64,640]{1,0:T(8,128)(2,1)S(1)}, bf16[64,640]{1,0:T(8,128)(2,1)S(1)}, u32[]{:S(2)}, u32[]{:S(2)}) %collective-permute-start.2) | collective-permute-done | bytes 81952 | tf_op jit(solution)/shard_map/ppermute | solution.py:350
  18.1 2.6 %collective-permute-start.5 = (bf16[64,640]{1,0:T(8,128)(2,1)S(1)}, bf16[64,640]{1,0:T(8,128)(2,1)S(1)}, u32[]{:S(2)}, u32[]{:S(2)}) collective-permute-start(bf16[64,640]{1,0:T(8,128)(2,1)S(1)} %collective-permute-done.2.refs_7_), channel_id=1, source_target_pairs={{14,0},{0,2},{2,4},{4,6},{6,8},{8,10},{10,12},{12,14},{15,1},{1,3}... | collective-permute-start | bytes 245768 | tf_op jit(solution)/shard_map/ppermute | solution.py:350
  20.6 0.0 collective-permute-done.refs_0_.refs_1_
  20.6 3.6 %collective-permute-start.6 = (bf16[64,640]{1,0:T(8,128)(2,1)S(1)}, bf16[64,640]{1,0:T(8,128)(2,1)S(1)}, u32[]{:S(2)}, u32[]{:S(2)}) collective-permute-start(bf16[64,640]{1,0:T(8,128)(2,1)S(1)} %collective-permute-done.2.refs_7_), channel_id=1, source_target_pairs={{2,0},{4,2},{6,4},{8,6},{10,8},{12,10},{14,12},{0,14},{3,1},{5,3},... | collective-permute-start | bytes 245768 | tf_op jit(solution)/shard_map/ppermute | solution.py:350
  24.2 0.0 collective-permute-done.1.refs_1_.refs_2_
  24.2 0.0 copy-done.1
  24.3 0.1 collective-permute-start.7
  24.4 0.0 copy-done.7
  24.4 0.0 slice-done
  24.4 0.0 slice-done.1
  24.4 0.0 copy-done.2
  24.4 0.0 copy-done.3
  24.4 3.3 %filter_mix_mlp.2.refs_14_ = bf16[16,16,640]{2,1,0:T(8,128)(2,1)} custom-call(bf16[16,16,640]{2,1,0:T(8,128)(2,1)S(1)} %bitcast.16, bf16[217,640]{1,0:T(8,128)(2,1)S(1)} %collective-permute-done.refs_0_.refs_1_, bf16[217,640]{1,0:T(8,128)(2,1)S(1)} %collective-permute-done.1.refs_1_.refs_2_, bf16[16,112,384]{2,1,0:T(8,128)(2,1)S(1)} %filter_taps.1.refs_3_.refs_9_, ...), custom_call_target="tpu_custom_call" | custom-call | flops 1000000 | bytes 100000 | tf_op jit(solution)/shard_map/filter_mix_mlp/pallas_call | solution.py:308
  27.7 0.0 collective-permute-done.3.refs_3_
  27.7 0.0 collective-permute-done.4.refs_4_
  27.7 0.0 collective-permute-done.5.refs_5_
  27.7 0.0 collective-permute-done.6.refs_6_
  27.7 0.0 collective-permute-done.7.refs_8_
  27.8 3.5 %filter_mix_mlp.3 = bf16[16,16,640]{2,1,0:T(8,128)(2,1)} custom-call(bf16[16,16,640]{2,1,0:T(8,128)(2,1)S(1)} %bitcast.17, bf16[217,640]{1,0:T(8,128)(2,1)S(1)} %collective-permute-done.refs_0_.refs_1_, bf16[217,640]{1,0:T(8,128)(2,1)S(1)} %collective-permute-done.1.refs_1_.refs_2_, ...), custom_call_target="tpu_custom_call", output_to_operand_aliasing={{}: (14, {})} | custom-call | flops 1000000 | bytes 100000 | tf_op jit(solution)/shard_map/filter_mix_mlp/pallas_call | solution.py:308
  (4 shorter events, 0.1 us)
Async XLA Ops:
  0.0 1.0 %copy-start = (bf16[640,16,16]{0,2,1:T(8,128)(2,1)S(1)}, bf16[640,16,16]{0,2,1:T(8,128)(2,1)}, u32[]{:S(2)}) copy-start(bf16[640,16,16]{0,2,1:T(8,128)(2,1)} %param.8) | copy-start | bytes 983044
  1.1 19.6 %collective-permute-start = (bf16[217,640]{1,0:T(8,128)(2,1)S(1)}, bf16[217,640]{1,0:T(8,128)(2,1)S(1)}, u32[]{:S(2)}, u32[]{:S(2)}) collective-permute-start(bf16[217,640]{1,0:T(8,128)(2,1)S(1)} %get-tuple-element.20), channel_id=1, source_target_pairs={{2,0},{4,2},{6,4},{8,6},{10,8},{12,10},{14,12},{0,14},{3,1},{5,3},... | collective-permute-start | bytes 833288 | tf_op jit(solution)/shard_map/ppermute | solution.py:350
  7.1 17.2 %collective-permute-start.1 = (bf16[217,640]{1,0:T(8,128)(2,1)S(1)}, bf16[217,640]{1,0:T(8,128)(2,1)S(1)}, u32[]{:S(2)}, u32[]{:S(2)}) collective-permute-start(bf16[217,640]{1,0:T(8,128)(2,1)S(1)} %get-tuple-element.21), channel_id=1, source_target_pairs={{14,0},{0,2},{2,4},{4,6},{6,8},{8,10},{10,12},{12,14},{15,1},{1,3}... | collective-permute-start | bytes 833288 | tf_op jit(solution)/shard_map/ppermute | solution.py:350
  7.1 10.9 %collective-permute-start.2 = (bf16[64,640]{1,0:T(8,128)(2,1)S(1)}, bf16[64,640]{1,0:T(8,128)(2,1)S(1)}, u32[]{:S(2)}, u32[]{:S(2)}) collective-permute-start(bf16[64,640]{1,0:T(8,128)(2,1)S(1)} %get-tuple-element.23), channel_id=1, source_target_pairs={{8,0},{10,2},{12,4},{14,6},{0,8},{2,10},{4,12},{6,14},{9,1},{11,3}... | collective-permute-start | bytes 245768 | tf_op jit(solution)/shard_map/ppermute | solution.py:350
  7.3 20.4 %collective-permute-start.3 = (bf16[96,640]{1,0:T(8,128)(2,1)S(1)}, bf16[96,640]{1,0:T(8,128)(2,1)S(1)}, u32[]{:S(2)}, u32[]{:S(2)}) collective-permute-start(bf16[96,640]{1,0:T(8,128)(2,1)S(1)} %get-tuple-element.27), channel_id=1, source_target_pairs={{4,0},{6,2},{8,4},{10,6},{12,8},{14,10},{0,12},{2,14},{5,1},{7,3},... | collective-permute-start | bytes 368648 | tf_op jit(solution)/shard_map/ppermute | solution.py:350
  8.6 19.1 %collective-permute-start.4 = (bf16[96,640]{1,0:T(8,128)(2,1)S(1)}, bf16[96,640]{1,0:T(8,128)(2,1)S(1)}, u32[]{:S(2)}, u32[]{:S(2)}) collective-permute-start(bf16[96,640]{1,0:T(8,128)(2,1)S(1)} %get-tuple-element.28), channel_id=1, source_target_pairs={{12,0},{14,2},{0,4},{2,6},{4,8},{6,10},{8,12},{10,14},{13,1},{15,3... | collective-permute-start | bytes 368648 | tf_op jit(solution)/shard_map/ppermute | solution.py:350
  9.3 15.1 %slice-start = ((s8[5734400]{0:T(1024)(128)(4,1)}), s8[4194304]{0:T(1024)(128)(4,1)S(1)}, s32[]{:S(2)}) async-start(s8[5734400]{0:T(1024)(128)(4,1)} %bitcast.11), calls=%async_computation | async-start | bytes 8388608
  9.3 1.0 %copy-start.4 = (s32[7,32,16]{1,2,0:T(8,128)S(1)}, s32[7,32,16]{1,2,0:T(8,128)}, u32[]{:S(2)}) copy-start(s32[7,32,16]{1,2,0:T(8,128)} %param.9) | copy-start | bytes 43012
  10.3 1.1 %copy-start.5 = (s32[7,32,16]{1,2,0:T(8,128)S(1)}, s32[7,32,16]{1,2,0:T(8,128)}, u32[]{:S(2)}) copy-start(s32[7,32,16]{1,2,0:T(8,128)} %param.10) | copy-start | bytes 43012
  11.3 0.8 %copy-start.6 = (f32[7,32,16]{1,2,0:T(8,128)S(1)}, f32[7,32,16]{1,2,0:T(8,128)}, u32[]{:S(2)}) copy-start(f32[7,32,16]{1,2,0:T(8,128)} %param.11) | copy-start | bytes 43012
  12.2 12.1 %copy-start.1 = (bf16[640,16,16]{0,2,1:T(8,128)(2,1)S(1)}, bf16[640,16,16]{0,2,1:T(8,128)(2,1)}, u32[]{:S(2)}) copy-start(bf16[640,16,16]{0,2,1:T(8,128)(2,1)} %param.8) | copy-start | bytes 983044
  12.2 12.2 %copy-start.7 = (f32[640]{0:T(1024)S(1)}, f32[640]{0:T(1024)}, u32[]{:S(2)}) copy-start(f32[640]{0:T(1024)} %param.13) | copy-start | bytes 7684
  12.2 12.2 %slice-start.1 = ((s8[5734400]{0:T(1024)(128)(4,1)}), s8[1540096]{0:T(1024)(128)(4,1)S(1)}, s32[]{:S(2)}) async-start(s8[5734400]{0:T(1024)(128)(4,1)} %bitcast.11), calls=%async_computation.1 | async-start | bytes 3080192
  12.2 12.2 %copy-start.2 = (bf16[640,1280]{1,0:T(8,128)(2,1)S(1)}, bf16[640,1280]{1,0:T(8,128)(2,1)}, u32[]{:S(2)}) copy-start(bf16[640,1280]{1,0:T(8,128)(2,1)} %refs_12_.1) | copy-start | bytes 4915204
  12.2 12.2 %copy-start.3 = (bf16[1280,640]{1,0:T(8,128)(2,1)S(1)}, bf16[1280,640]{1,0:T(8,128)(2,1)}, u32[]{:S(2)}) copy-start(bf16[1280,640]{1,0:T(8,128)(2,1)} %refs_13_.1) | copy-start | bytes 4915204
  18.1 9.7 %collective-permute-start.5 = (bf16[64,640]{1,0:T(8,128)(2,1)S(1)}, bf16[64,640]{1,0:T(8,128)(2,1)S(1)}, u32[]{:S(2)}, u32[]{:S(2)}) collective-permute-start(bf16[64,640]{1,0:T(8,128)(2,1)S(1)} %collective-permute-done.2.refs_7_), channel_id=1, source_target_pairs={{14,0},{0,2},{2,4},{4,6},{6,8},{8,10},{10,12},{12,14},{15,1},{1,3}... | collective-permute-start | bytes 245768 | tf_op jit(solution)/shard_map/ppermute | solution.py:350
  20.6 7.1 %collective-permute-start.6 = (bf16[64,640]{1,0:T(8,128)(2,1)S(1)}, bf16[64,640]{1,0:T(8,128)(2,1)S(1)}, u32[]{:S(2)}, u32[]{:S(2)}) collective-permute-start(bf16[64,640]{1,0:T(8,128)(2,1)S(1)} %collective-permute-done.2.refs_7_), channel_id=1, source_target_pairs={{2,0},{4,2},{6,4},{8,6},{10,8},{12,10},{14,12},{0,14},{3,1},{5,3},... | collective-permute-start | bytes 245768 | tf_op jit(solution)/shard_map/ppermute | solution.py:350
  24.3 3.5 %collective-permute-start.7 = (bf16[32,640]{1,0:T(8,128)(2,1)S(1)}, bf16[32,640]{1,0:T(8,128)(2,1)S(1)}, u32[]{:S(2)}, u32[]{:S(2)}) collective-permute-start(bf16[32,640]{1,0:T(8,128)(2,1)S(1)} %pack_edge_row.1), channel_id=1, source_target_pairs={{0,1},{1,0},{2,3},{3,2},{4,5},{5,4},{6,7},{7,6},{8,9},{9,8},{10,11... | collective-permute-start | bytes 122888 | tf_op jit(solution)/shard_map/ppermute | solution.py:138

commit v5 on v4

--- a/solution.py
+++ b/solution.py
@@ -63,6 +63,10 @@
     def taps_width(self, slot):
         return -(-len(self.sources(slot)) * self.span(slot)[1] // lanes) * lanes
 
+    def taps_size(self, slot):
+        count = self.span(slot)[1]
+        return count if count == self.lon_total else self.taps_width(slot)
+
     def sources(self, slot):
         return [s for s in (slot, slot + 1, slot + 2) if s > 0 or self.outer]
 
@@ -142,19 +146,31 @@
     return [low, high]
 
 
-def taps_body(plan, entries, lift_ref, place_ref, weight_ref, out):
-    size, lat_total = lift_ref.shape
+def taps_body(plan, entries, lift_hbm, place_hbm, weight_hbm, out, *scratch):
+    held, sem = scratch[:3], scratch[3]
+    copies = [
+        pltpu.make_async_copy(source, target, sem.at[order])
+        for order, (source, target) in enumerate(zip((lift_hbm, place_hbm, weight_hbm), held))
+    ]
+    for copy in copies:
+        copy.start()
+    size, lat_total = lift_hbm.shape
     cols, width = plan.cols, out.shape[2]
     south = is_south(plan)
     row_start = lax.axis_index("lat") * plan.rows
     source_row = lax.broadcasted_iota(jnp.int32, (lat_total, lanes), 0)
-    spot = lax.broadcasted_iota(jnp.int32, (size, width), 1)
-    early = lax.broadcasted_iota(jnp.int32, (size, width), 0) // entries * cols
-    kinds_rows = size // entries * cols
-    basis_row = lax.broadcasted_iota(jnp.int32, (kinds_rows, size), 0) // cols
-    basis_col = lax.broadcasted_iota(jnp.int32, (kinds_rows, size), 1) // entries
+    spots = {}
+    for span in {plan.taps_size(slot) for slot in range(plan.rows)}:
+        spot = lax.broadcasted_iota(jnp.int32, (size, span), 1)
+        early = lax.broadcasted_iota(jnp.int32, (size, span), 0) // entries * cols
+        spots[span] = lax.rem(spot + early, span)
+    tall = size // entries * cols
+    basis_row = lax.broadcasted_iota(jnp.int32, (tall, size), 0) // cols
+    basis_col = lax.broadcasted_iota(jnp.int32, (tall, size), 1) // entries
     gather = jnp.where(basis_row == basis_col, 1.0, 0.0).astype(jnp.bfloat16)
-    tables = [ref[...].astype(jnp.bfloat16) for ref in (lift_ref, place_ref, weight_ref)]
+    for copy in copies:
+        copy.wait()
+    tables = [ref[...].astype(jnp.bfloat16) for ref in held]
     for slot in range(plan.rows):
         first, count = plan.span(slot)
         center = (plan.half - 1) * cols - first
@@ -166,32 +182,38 @@
         lift = jnp.where(south, -lift, lift).astype(jnp.int32)
         place = place.astype(jnp.int32) + center
         sources = plan.sources(slot)
+        span = plan.taps_size(slot)
         if count == plan.lon_total:
+            place = jnp.where(place < 0, place + count, place)
             pieces = [(source - slot - 1, order * count) for order, source in enumerate(sources)]
-            size = count
         else:
             place = place + (lift + slot + 1 - sources[0]) * count
-            pieces, size = [(None, 0)], plan.taps_width(slot)
+            pieces = [(None, 0)]
+        place, weight, lift = [
+            jnp.concatenate([v] * (span // lanes), axis=1) for v in (place, weight, lift)
+        ]
+        part = jnp.where(spots[span] == place, weight, 0.0)
         for offset, start in pieces:
-            gap = spot[:, :size] + early[:, :size] - place[:, :1]
-            hit = lax.rem(gap + 4 * size, size) == 0
-            if offset is not None:
-                hit = hit & (lift[:, :1] == offset)
-            part = jnp.where(hit, weight[:, :1], 0.0).astype(jnp.bfloat16)
-            taps = jnp.dot(gather, part, preferred_element_type=jnp.float32)
+            chosen = part if offset is None else jnp.where(lift == offset, part, 0.0)
+            taps = jnp.dot(
+                gather, chosen.astype(jnp.bfloat16), preferred_element_type=jnp.float32
+            )
             taps = pltpu.roll(taps, 0, 1, stride=1, stride_axis=0)
-            out[slot, :, start : start + size] = taps.astype(jnp.bfloat16)
+            out[slot, :, start : start + span] = taps.astype(jnp.bfloat16)
 
 
 def make_taps(plan, support):
     kinds, _, entries = support[0].shape
     width = max(plan.taps_width(slot) for slot in range(plan.rows))
     tables = [s.transpose(0, 2, 1).reshape(kinds * entries, -1) for s in support]
+    scratch = [pltpu.VMEM(t.shape, t.dtype) for t in tables]
+    tables = [pltpu.with_memory_space_constraint(t, pltpu.HBM) for t in tables]
     return pl.pallas_call(
         functools.partial(taps_body, plan, entries),
         out_shape=jax.ShapeDtypeStruct((plan.rows, kinds * plan.cols, width), jnp.bfloat16),
-        in_specs=[vmem] * 3,
+        in_specs=[pl.BlockSpec(memory_space=pltpu.HBM)] * 3,
         out_specs=vmem,
+        scratch_shapes=scratch + [pltpu.SemaphoreType.DMA((3,))],
         compiler_params=pltpu.CompilerParams(vmem_limit_bytes=8 * mib),
         cost_estimate=pl.CostEstimate(flops=3 * 10**9, bytes_accessed=10**7, transcendentals=0),
         name="filter_taps",
@@ -237,7 +259,8 @@
     used += 5 + chained
     out_ref, win, response, result, sem = refs[used:]
     rows, cols = plan.rows, plan.cols
-    kinds = mix_ref.shape[0]
+    channels = x_ref.shape[2]
+    kinds = mix_ref.shape[0] // channels
     south = is_south(plan)
     middle = (plan.half - 1) * cols
     sources = sorted({s for slot in slots for s in plan.sources(slot)})
@@ -253,10 +276,9 @@
         total = total.astype(jnp.bfloat16)
         for kind in range(kinds):
             place = slice(order * cols, (order + 1) * cols)
-            response[kind, place] = total[kind * cols : (kind + 1) * cols]
-    mixed = jnp.dot(response[0], mix_ref[0], preferred_element_type=jnp.float32)
-    for kind in range(1, kinds):
-        mixed = mixed + jnp.dot(response[kind], mix_ref[kind], preferred_element_type=jnp.float32)
+            depth = slice(kind * channels, (kind + 1) * channels)
+            response[place, depth] = total[kind * cols : (kind + 1) * cols]
+    mixed = jnp.dot(response[...], mix_ref[...], preferred_element_type=jnp.float32)
     own = [win[sources.index(slot + 1), middle : middle + cols] for slot in slots]
     latent = jnp.concatenate(own, axis=0).astype(jnp.float32) + mixed
     mean = jnp.mean(latent, axis=1, keepdims=True)
@@ -304,7 +326,7 @@
         args.append(chain)
         specs.append(anywhere)
     channels = x.shape[2]
-    kinds = weights[0].shape[0]
+    depth = weights[0].shape[0]
     return pl.pallas_call(
         functools.partial(compute_body, plan, slots, moves, len(edges), chain is not None),
         out_shape=jax.ShapeDtypeStruct(x.shape, x.dtype),
@@ -312,7 +334,7 @@
         out_specs=anywhere,
         scratch_shapes=[
             pltpu.VMEM((len(sources), plan.lon_total, channels), x.dtype),
-            pltpu.VMEM((kinds, len(slots) * plan.cols, channels), x.dtype),
+            pltpu.VMEM((len(slots) * plan.cols, depth), x.dtype),
             pltpu.VMEM((len(slots), plan.cols, channels), x.dtype),
             pltpu.SemaphoreType.DMA((len(runs_of(slots)),)),
         ],
@@ -361,7 +383,7 @@
     joined, taps = lax.optimization_barrier(([got[m] for m in first], taps))
     got.update(zip(first, joined))
     edges = edge_rows(plan, x, got)
-    weights = (mix_weight, norm_gain[None], up_weight, down_weight)
+    weights = (mix_weight.reshape(-1, channels), norm_gain[None], up_weight, down_weight)
     inner = range(1 if plan.outer else 0, rows - 1)
     near = [slot for slot in inner if plan.blocks[slot] <= 1]
     far = [slot for slot in range(rows) if slot not in near]

time: 31.4 us -> 31 us (0.987)
  waiting for transfers between devices: 1.26 us -> 4.46 us
  local copies, waits for them, and re-layouts: 3.85 us -> 1 us
  Pallas kernels: 11.5 us -> 10.7 us
    ppermute x7, waiting for transfers between devices: 1.26 us -> 4.45 us  [shifted(): lax.ppermute(value, 'lon', [((i + step) % count, i) for i in range(count)])]
    unnamed x20 -> x14, local copies, waits for them, and re-layouts: 3.84 us -> 1 us
    pallas_call x2, Pallas kernels: 6.73 us -> 6.34 us  [compute(): pl.pallas_call(functools.partial(compute_body, plan, slots, moves, len(ed...]
    pallas_call x1, Pallas kernels: 4.62 us -> 4.26 us  [make_taps(): pl.pallas_call(functools.partial(taps_body, plan, entries), out_shape=jax...]
  transfers between devices with their start and end apart: 8 -> 8, of which waited for: 1 -> 1; matrix products, arithmetic and copies ran while one was open for 0% -> 0% of each run, Pallas kernels for 25% -> 24%
where the time goes in v5:
time: 31 us; the launch traced here: 30.8 us
  starting transfers between devices  14.5 us (47%)
  Pallas kernels  10.7 us (35%)
  waiting for transfers between devices  4.46 us (14%)
  local copies, waits for them, and re-layouts  1 us (3%)
    ppermute x7, starting transfers between devices, shifted(): lax.ppermute(value, 'lon', [((i + step) % count, i) for i in range(count)])  14.4 us
    pallas_call x2, Pallas kernels, compute(): pl.pallas_call(functools.partial(compute_body, plan, slots, moves, len(ed...  6.34 us
    ppermute x7, waiting for transfers between devices, shifted(): lax.ppermute(value, 'lon', [((i + step) % count, i) for i in range(count)])  4.45 us
    pallas_call x1, Pallas kernels, make_taps(): pl.pallas_call(functools.partial(taps_body, plan, entries), out_shape=jax...  4.26 us
    unnamed x14, local copies, waits for them, and re-layouts  1 us
  transfers between devices with their start and end apart: 8, of which 1 were waited for; matrix products, arithmetic and copies ran while one was open for 0% of the time, Pallas kernels for 24%

profile of v5, /device:TPU:0, one launch (start us, length us, event | category | flops | bytes accessed | tf_op | source)
XLA Modules:
  0.0 30.8 jit_solution(1858442752611776619)
XLA Ops:
  0.0 0.0 copy-start
  0.0 1.0 %copy-done = bf16[640,16,16]{0,2,1:T(8,128)(2,1)S(1)} copy-done((bf16[640,16,16]{0,2,1:T(8,128)(2,1)S(1)}, bf16[640,16,16]{0,2,1:T(8,128)(2,1)}, u32[]{:S(2)}) %copy-start) | copy-done | bytes 327704
  1.0 0.1 pack_columns.2
  1.1 6.0 %collective-permute-start = (bf16[217,640]{1,0:T(8,128)(2,1)S(1)}, bf16[217,640]{1,0:T(8,128)(2,1)S(1)}, u32[]{:S(2)}, u32[]{:S(2)}) collective-permute-start(bf16[217,640]{1,0:T(8,128)(2,1)S(1)} %get-tuple-element.20), channel_id=1, source_target_pairs={{2,0},{4,2},{6,4},{8,6},{10,8},{12,10},{14,12},{0,14},{3,1},{5,3},... | collective-permute-start | bytes 833288 | tf_op jit(solution)/shard_map/ppermute | solution.py:372
  7.1 0.0 collective-permute-start.1
  7.1 0.1 collective-permute-start.2
  7.3 1.3 %collective-permute-start.3 = (bf16[96,640]{1,0:T(8,128)(2,1)S(1)}, bf16[96,640]{1,0:T(8,128)(2,1)S(1)}, u32[]{:S(2)}, u32[]{:S(2)}) collective-permute-start(bf16[96,640]{1,0:T(8,128)(2,1)S(1)} %get-tuple-element.27), channel_id=1, source_target_pairs={{4,0},{6,2},{8,4},{10,6},{12,8},{14,10},{0,12},{2,14},{5,1},{7,3},... | collective-permute-start | bytes 368648 | tf_op jit(solution)/shard_map/ppermute | solution.py:372
  8.6 0.7 %collective-permute-start.4 = (bf16[96,640]{1,0:T(8,128)(2,1)S(1)}, bf16[96,640]{1,0:T(8,128)(2,1)S(1)}, u32[]{:S(2)}, u32[]{:S(2)}) collective-permute-start(bf16[96,640]{1,0:T(8,128)(2,1)S(1)} %get-tuple-element.28), channel_id=1, source_target_pairs={{12,0},{14,2},{0,4},{2,6},{4,8},{6,10},{8,12},{10,14},{13,1},{15,3... | collective-permute-start | bytes 368648 | tf_op jit(solution)/shard_map/ppermute | solution.py:372
  9.3 0.0 slice-start
  9.3 0.0 copy-start.1
  9.3 0.0 copy-start.4
  9.3 0.0 slice-start.1
  9.3 0.0 copy-start.2
  9.3 0.0 copy-start.3
  9.3 4.3 %filter_taps.1.refs_3_.refs_9_ = bf16[16,112,384]{2,1,0:T(8,128)(2,1)S(1)} custom-call(s32[112,32]{1,0:T(8,128)} %bitcast.21, s32[112,32]{1,0:T(8,128)} %bitcast.22, f32[112,32]{1,0:T(8,128)} %bitcast.23), custom_call_target="tpu_custom_call" | custom-call | flops 3000000000 | bytes 10000000 | tf_op jit(solution)/shard_map/filter_taps/pallas_call | solution.py:211
  13.6 4.4 %collective-permute-done.2.refs_7_ = bf16[64,640]{1,0:T(8,128)(2,1)S(1)} collective-permute-done((bf16[64,640]{1,0:T(8,128)(2,1)S(1)}, bf16[64,640]{1,0:T(8,128)(2,1)S(1)}, u32[]{:S(2)}, u32[]{:S(2)}) %collective-permute-start.2) | collective-permute-done | bytes 81952 | tf_op jit(solution)/shard_map/ppermute | solution.py:372
  18.1 0.0 collective-permute-start.5
  18.1 0.0 collective-permute-done.refs_0_.refs_1_
  18.1 6.2 %collective-permute-start.6 = (bf16[64,640]{1,0:T(8,128)(2,1)S(1)}, bf16[64,640]{1,0:T(8,128)(2,1)S(1)}, u32[]{:S(2)}, u32[]{:S(2)}) collective-permute-start(bf16[64,640]{1,0:T(8,128)(2,1)S(1)} %collective-permute-done.2.refs_7_), channel_id=1, source_target_pairs={{2,0},{4,2},{6,4},{8,6},{10,8},{12,10},{14,12},{0,14},{3,1},{5,3},... | collective-permute-start | bytes 245768 | tf_op jit(solution)/shard_map/ppermute | solution.py:372
  24.2 0.0 collective-permute-done.1.refs_1_.refs_2_
  24.2 0.0 copy-done.1
  24.3 0.1 collective-permute-start.7
  24.4 0.0 copy-done.4
  24.4 0.0 slice-done
  24.4 0.0 slice-done.1
  24.4 0.0 copy-done.2
  24.4 0.0 copy-done.3
  24.4 3.1 %filter_mix_mlp.2.refs_14_ = bf16[16,16,640]{2,1,0:T(8,128)(2,1)} custom-call(bf16[16,16,640]{2,1,0:T(8,128)(2,1)S(1)} %bitcast.19, bf16[217,640]{1,0:T(8,128)(2,1)S(1)} %collective-permute-done.refs_0_.refs_1_, bf16[217,640]{1,0:T(8,128)(2,1)S(1)} %collective-permute-done.1.refs_1_.refs_2_, bf16[16,112,384]{2,1,0:T(8,128)(2,1)S(1)} %filter_taps.1.refs_3_.refs_9_, ...), custom_call_target="tpu_custom_call" | custom-call | flops 1000000 | bytes 100000 | tf_op jit(solution)/shard_map/filter_mix_mlp/pallas_call | solution.py:330
  27.5 0.0 collective-permute-done.3.refs_3_
  27.5 0.0 collective-permute-done.4.refs_4_
  27.5 0.0 collective-permute-done.5.refs_5_
  27.6 0.0 collective-permute-done.6.refs_6_
  27.6 0.0 collective-permute-done.7.refs_8_
  27.6 3.2 %filter_mix_mlp.3 = bf16[16,16,640]{2,1,0:T(8,128)(2,1)} custom-call(bf16[16,16,640]{2,1,0:T(8,128)(2,1)S(1)} %bitcast.20, bf16[217,640]{1,0:T(8,128)(2,1)S(1)} %collective-permute-done.refs_0_.refs_1_, bf16[217,640]{1,0:T(8,128)(2,1)S(1)} %collective-permute-done.1.refs_1_.refs_2_, ...), custom_call_target="tpu_custom_call", output_to_operand_aliasing={{}: (14, {})} | custom-call | flops 1000000 | bytes 100000 | tf_op jit(solution)/shard_map/filter_mix_mlp/pallas_call | solution.py:330
  (4 shorter events, 0.1 us)
Async XLA Ops:
  0.0 1.0 %copy-start = (bf16[640,16,16]{0,2,1:T(8,128)(2,1)S(1)}, bf16[640,16,16]{0,2,1:T(8,128)(2,1)}, u32[]{:S(2)}) copy-start(bf16[640,16,16]{0,2,1:T(8,128)(2,1)} %param.8) | copy-start | bytes 983044
  1.1 17.0 %collective-permute-start = (bf16[217,640]{1,0:T(8,128)(2,1)S(1)}, bf16[217,640]{1,0:T(8,128)(2,1)S(1)}, u32[]{:S(2)}, u32[]{:S(2)}) collective-permute-start(bf16[217,640]{1,0:T(8,128)(2,1)S(1)} %get-tuple-element.20), channel_id=1, source_target_pairs={{2,0},{4,2},{6,4},{8,6},{10,8},{12,10},{14,12},{0,14},{3,1},{5,3},... | collective-permute-start | bytes 833288 | tf_op jit(solution)/shard_map/ppermute | solution.py:372
  7.1 17.2 %collective-permute-start.1 = (bf16[217,640]{1,0:T(8,128)(2,1)S(1)}, bf16[217,640]{1,0:T(8,128)(2,1)S(1)}, u32[]{:S(2)}, u32[]{:S(2)}) collective-permute-start(bf16[217,640]{1,0:T(8,128)(2,1)S(1)} %get-tuple-element.21), channel_id=1, source_target_pairs={{14,0},{0,2},{2,4},{4,6},{6,8},{8,10},{10,12},{12,14},{15,1},{1,3}... | collective-permute-start | bytes 833288 | tf_op jit(solution)/shard_map/ppermute | solution.py:372
  7.1 10.9 %collective-permute-start.2 = (bf16[64,640]{1,0:T(8,128)(2,1)S(1)}, bf16[64,640]{1,0:T(8,128)(2,1)S(1)}, u32[]{:S(2)}, u32[]{:S(2)}) collective-permute-start(bf16[64,640]{1,0:T(8,128)(2,1)S(1)} %get-tuple-element.23), channel_id=1, source_target_pairs={{8,0},{10,2},{12,4},{14,6},{0,8},{2,10},{4,12},{6,14},{9,1},{11,3}... | collective-permute-start | bytes 245768 | tf_op jit(solution)/shard_map/ppermute | solution.py:372
  7.3 20.2 %collective-permute-start.3 = (bf16[96,640]{1,0:T(8,128)(2,1)S(1)}, bf16[96,640]{1,0:T(8,128)(2,1)S(1)}, u32[]{:S(2)}, u32[]{:S(2)}) collective-permute-start(bf16[96,640]{1,0:T(8,128)(2,1)S(1)} %get-tuple-element.27), channel_id=1, source_target_pairs={{4,0},{6,2},{8,4},{10,6},{12,8},{14,10},{0,12},{2,14},{5,1},{7,3},... | collective-permute-start | bytes 368648 | tf_op jit(solution)/shard_map/ppermute | solution.py:372
  8.6 18.9 %collective-permute-start.4 = (bf16[96,640]{1,0:T(8,128)(2,1)S(1)}, bf16[96,640]{1,0:T(8,128)(2,1)S(1)}, u32[]{:S(2)}, u32[]{:S(2)}) collective-permute-start(bf16[96,640]{1,0:T(8,128)(2,1)S(1)} %get-tuple-element.28), channel_id=1, source_target_pairs={{12,0},{14,2},{0,4},{2,6},{4,8},{6,10},{8,12},{10,14},{13,1},{15,3... | collective-permute-start | bytes 368648 | tf_op jit(solution)/shard_map/ppermute | solution.py:372
  9.3 15.1 %slice-start = ((s8[5734400]{0:T(1024)(128)(4,1)}), s8[4194304]{0:T(1024)(128)(4,1)S(1)}, s32[]{:S(2)}) async-start(s8[5734400]{0:T(1024)(128)(4,1)} %bitcast.12), calls=%async_computation | async-start | bytes 8388608
  9.3 14.9 %copy-start.1 = (bf16[640,16,16]{0,2,1:T(8,128)(2,1)S(1)}, bf16[640,16,16]{0,2,1:T(8,128)(2,1)}, u32[]{:S(2)}) copy-start(bf16[640,16,16]{0,2,1:T(8,128)(2,1)} %param.8) | copy-start | bytes 983044
  9.3 15.0 %copy-start.4 = (f32[640]{0:T(1024)S(1)}, f32[640]{0:T(1024)}, u32[]{:S(2)}) copy-start(f32[640]{0:T(1024)} %param.13) | copy-start | bytes 7684
  9.3 15.1 %slice-start.1 = ((s8[5734400]{0:T(1024)(128)(4,1)}), s8[1540096]{0:T(1024)(128)(4,1)S(1)}, s32[]{:S(2)}) async-start(s8[5734400]{0:T(1024)(128)(4,1)} %bitcast.12), calls=%async_computation.1 | async-start | bytes 3080192
  9.3 15.1 %copy-start.2 = (bf16[640,1280]{1,0:T(8,128)(2,1)S(1)}, bf16[640,1280]{1,0:T(8,128)(2,1)}, u32[]{:S(2)}) copy-start(bf16[640,1280]{1,0:T(8,128)(2,1)} %refs_12_.1) | copy-start | bytes 4915204
  9.3 15.1 %copy-start.3 = (bf16[1280,640]{1,0:T(8,128)(2,1)S(1)}, bf16[1280,640]{1,0:T(8,128)(2,1)}, u32[]{:S(2)}) copy-start(bf16[1280,640]{1,0:T(8,128)(2,1)} %refs_13_.1) | copy-start | bytes 4915204
  18.1 9.5 %collective-permute-start.5 = (bf16[64,640]{1,0:T(8,128)(2,1)S(1)}, bf16[64,640]{1,0:T(8,128)(2,1)S(1)}, u32[]{:S(2)}, u32[]{:S(2)}) collective-permute-start(bf16[64,640]{1,0:T(8,128)(2,1)S(1)} %collective-permute-done.2.refs_7_), channel_id=1, source_target_pairs={{14,0},{0,2},{2,4},{4,6},{6,8},{8,10},{10,12},{12,14},{15,1},{1,3}... | collective-permute-start | bytes 245768 | tf_op jit(solution)/shard_map/ppermute | solution.py:372
  18.1 9.5 %collective-permute-start.6 = (bf16[64,640]{1,0:T(8,128)(2,1)S(1)}, bf16[64,640]{1,0:T(8,128)(2,1)S(1)}, u32[]{:S(2)}, u32[]{:S(2)}) collective-permute-start(bf16[64,640]{1,0:T(8,128)(2,1)S(1)} %collective-permute-done.2.refs_7_), channel_id=1, source_target_pairs={{2,0},{4,2},{6,4},{8,6},{10,8},{12,10},{14,12},{0,14},{3,1},{5,3},... | collective-permute-start | bytes 245768 | tf_op jit(solution)/shard_map/ppermute | solution.py:372
  24.3 3.3 %collective-permute-start.7 = (bf16[32,640]{1,0:T(8,128)(2,1)S(1)}, bf16[32,640]{1,0:T(8,128)(2,1)S(1)}, u32[]{:S(2)}, u32[]{:S(2)}) collective-permute-start(bf16[32,640]{1,0:T(8,128)(2,1)S(1)} %pack_edge_row.1), channel_id=1, source_target_pairs={{0,1},{1,0},{2,3},{3,2},{4,5},{5,4},{6,7},{7,6},{8,9},{9,8},{10,11... | collective-permute-start | bytes 122888 | tf_op jit(solution)/shard_map/ppermute | solution.py:142

commit v6 on v5

--- a/solution.py
+++ b/solution.py
@@ -234,6 +234,9 @@
                 gap = jnp.zeros((gap, strip.shape[1]), strip.dtype)
                 strip = jnp.concatenate([gap, strip, gap], axis=0)
             start = middle - plan.margin_blocks * cols
+            users = [s for s in range(rows) if slot in plan.sources(s)]
+            if max(plan.blocks[s] for s in users) > plan.margin_blocks:
+                win[sources.index(slot)] = jnp.zeros(win.shape[1:], win.dtype)
             win[sources.index(slot), start : start + strip.shape[0]] = strip
         else:
             win[sources.index(slot), middle : middle + cols] = x_ref[row_of(plan, south, slot)]

time: 31 us -> 31 us (level)
  no operation moved by 1% of the time
where the time goes in v6:
time: 31 us; the launch traced here: 30.8 us
  starting transfers between devices  14.5 us (47%)
  Pallas kernels  10.7 us (35%)
  waiting for transfers between devices  4.46 us (14%)
  local copies, waits for them, and re-layouts  1 us (3%)
    ppermute x7, starting transfers between devices, shifted(): lax.ppermute(value, 'lon', [((i + step) % count, i) for i in range(count)])  14.4 us
    pallas_call x2, Pallas kernels, compute(): pl.pallas_call(functools.partial(compute_body, plan, slots, moves, len(ed...  6.34 us
    ppermute x7, waiting for transfers between devices, shifted(): lax.ppermute(value, 'lon', [((i + step) % count, i) for i in range(count)])  4.45 us
    pallas_call x1, Pallas kernels, make_taps(): pl.pallas_call(functools.partial(taps_body, plan, entries), out_shape=jax...  4.26 us
    unnamed x14, local copies, waits for them, and re-layouts  1 us
  transfers between devices with their start and end apart: 8, of which 1 were waited for; matrix products, arithmetic and copies ran while one was open for 0% of the time, Pallas kernels for 24%

profile of v6, /device:TPU:0, one launch (start us, length us, event | category | flops | bytes accessed | tf_op | source)
XLA Modules:
  0.0 30.8 jit_solution(1858442752611776619)
XLA Ops:
  0.0 0.0 copy-start
  0.0 1.0 %copy-done = bf16[640,16,16]{0,2,1:T(8,128)(2,1)S(1)} copy-done((bf16[640,16,16]{0,2,1:T(8,128)(2,1)S(1)}, bf16[640,16,16]{0,2,1:T(8,128)(2,1)}, u32[]{:S(2)}) %copy-start) | copy-done | bytes 327704
  1.0 0.1 pack_columns.2
  1.1 6.0 %collective-permute-start = (bf16[217,640]{1,0:T(8,128)(2,1)S(1)}, bf16[217,640]{1,0:T(8,128)(2,1)S(1)}, u32[]{:S(2)}, u32[]{:S(2)}) collective-permute-start(bf16[217,640]{1,0:T(8,128)(2,1)S(1)} %get-tuple-element.20), channel_id=1, source_target_pairs={{2,0},{4,2},{6,4},{8,6},{10,8},{12,10},{14,12},{0,14},{3,1},{5,3},... | collective-permute-start | bytes 833288 | tf_op jit(solution)/shard_map/ppermute | solution.py:375
  7.1 0.0 collective-permute-start.1
  7.1 0.1 collective-permute-start.2
  7.3 1.3 %collective-permute-start.3 = (bf16[96,640]{1,0:T(8,128)(2,1)S(1)}, bf16[96,640]{1,0:T(8,128)(2,1)S(1)}, u32[]{:S(2)}, u32[]{:S(2)}) collective-permute-start(bf16[96,640]{1,0:T(8,128)(2,1)S(1)} %get-tuple-element.27), channel_id=1, source_target_pairs={{4,0},{6,2},{8,4},{10,6},{12,8},{14,10},{0,12},{2,14},{5,1},{7,3},... | collective-permute-start | bytes 368648 | tf_op jit(solution)/shard_map/ppermute | solution.py:375
  8.6 0.7 %collective-permute-start.4 = (bf16[96,640]{1,0:T(8,128)(2,1)S(1)}, bf16[96,640]{1,0:T(8,128)(2,1)S(1)}, u32[]{:S(2)}, u32[]{:S(2)}) collective-permute-start(bf16[96,640]{1,0:T(8,128)(2,1)S(1)} %get-tuple-element.28), channel_id=1, source_target_pairs={{12,0},{14,2},{0,4},{2,6},{4,8},{6,10},{8,12},{10,14},{13,1},{15,3... | collective-permute-start | bytes 368648 | tf_op jit(solution)/shard_map/ppermute | solution.py:375
  9.3 0.0 slice-start
  9.3 0.0 copy-start.1
  9.3 0.0 copy-start.4
  9.3 0.0 slice-start.1
  9.3 0.0 copy-start.2
  9.3 0.0 copy-start.3
  9.3 4.3 %filter_taps.1.refs_3_.refs_9_ = bf16[16,112,384]{2,1,0:T(8,128)(2,1)S(1)} custom-call(s32[112,32]{1,0:T(8,128)} %bitcast.21, s32[112,32]{1,0:T(8,128)} %bitcast.22, f32[112,32]{1,0:T(8,128)} %bitcast.23), custom_call_target="tpu_custom_call" | custom-call | flops 3000000000 | bytes 10000000 | tf_op jit(solution)/shard_map/filter_taps/pallas_call | solution.py:211
  13.6 4.4 %collective-permute-done.2.refs_7_ = bf16[64,640]{1,0:T(8,128)(2,1)S(1)} collective-permute-done((bf16[64,640]{1,0:T(8,128)(2,1)S(1)}, bf16[64,640]{1,0:T(8,128)(2,1)S(1)}, u32[]{:S(2)}, u32[]{:S(2)}) %collective-permute-start.2) | collective-permute-done | bytes 81952 | tf_op jit(solution)/shard_map/ppermute | solution.py:375
  18.1 0.0 collective-permute-start.5
  18.1 0.0 collective-permute-done.refs_0_.refs_1_
  18.1 6.2 %collective-permute-start.6 = (bf16[64,640]{1,0:T(8,128)(2,1)S(1)}, bf16[64,640]{1,0:T(8,128)(2,1)S(1)}, u32[]{:S(2)}, u32[]{:S(2)}) collective-permute-start(bf16[64,640]{1,0:T(8,128)(2,1)S(1)} %collective-permute-done.2.refs_7_), channel_id=1, source_target_pairs={{2,0},{4,2},{6,4},{8,6},{10,8},{12,10},{14,12},{0,14},{3,1},{5,3},... | collective-permute-start | bytes 245768 | tf_op jit(solution)/shard_map/ppermute | solution.py:375
  24.2 0.0 collective-permute-done.1.refs_1_.refs_2_
  24.2 0.0 copy-done.1
  24.3 0.1 collective-permute-start.7
  24.4 0.0 copy-done.4
  24.4 0.0 slice-done
  24.4 0.0 slice-done.1
  24.4 0.0 copy-done.2
  24.4 0.0 copy-done.3
  24.4 3.1 %filter_mix_mlp.2.refs_14_ = bf16[16,16,640]{2,1,0:T(8,128)(2,1)} custom-call(bf16[16,16,640]{2,1,0:T(8,128)(2,1)S(1)} %bitcast.19, bf16[217,640]{1,0:T(8,128)(2,1)S(1)} %collective-permute-done.refs_0_.refs_1_, bf16[217,640]{1,0:T(8,128)(2,1)S(1)} %collective-permute-done.1.refs_1_.refs_2_, bf16[16,112,384]{2,1,0:T(8,128)(2,1)S(1)} %filter_taps.1.refs_3_.refs_9_, ...), custom_call_target="tpu_custom_call" | custom-call | flops 1000000 | bytes 100000 | tf_op jit(solution)/shard_map/filter_mix_mlp/pallas_call | solution.py:333
  27.5 0.0 collective-permute-done.3.refs_3_
  27.5 0.0 collective-permute-done.4.refs_4_
  27.5 0.0 collective-permute-done.5.refs_5_
  27.6 0.0 collective-permute-done.6.refs_6_
  27.6 0.0 collective-permute-done.7.refs_8_
  27.6 3.2 %filter_mix_mlp.3 = bf16[16,16,640]{2,1,0:T(8,128)(2,1)} custom-call(bf16[16,16,640]{2,1,0:T(8,128)(2,1)S(1)} %bitcast.20, bf16[217,640]{1,0:T(8,128)(2,1)S(1)} %collective-permute-done.refs_0_.refs_1_, bf16[217,640]{1,0:T(8,128)(2,1)S(1)} %collective-permute-done.1.refs_1_.refs_2_, ...), custom_call_target="tpu_custom_call", output_to_operand_aliasing={{}: (14, {})} | custom-call | flops 1000000 | bytes 100000 | tf_op jit(solution)/shard_map/filter_mix_mlp/pallas_call | solution.py:333
  (4 shorter events, 0.1 us)
Async XLA Ops:
  0.0 1.0 %copy-start = (bf16[640,16,16]{0,2,1:T(8,128)(2,1)S(1)}, bf16[640,16,16]{0,2,1:T(8,128)(2,1)}, u32[]{:S(2)}) copy-start(bf16[640,16,16]{0,2,1:T(8,128)(2,1)} %param.8) | copy-start | bytes 983044
  1.1 17.0 %collective-permute-start = (bf16[217,640]{1,0:T(8,128)(2,1)S(1)}, bf16[217,640]{1,0:T(8,128)(2,1)S(1)}, u32[]{:S(2)}, u32[]{:S(2)}) collective-permute-start(bf16[217,640]{1,0:T(8,128)(2,1)S(1)} %get-tuple-element.20), channel_id=1, source_target_pairs={{2,0},{4,2},{6,4},{8,6},{10,8},{12,10},{14,12},{0,14},{3,1},{5,3},... | collective-permute-start | bytes 833288 | tf_op jit(solution)/shard_map/ppermute | solution.py:375
  7.1 17.2 %collective-permute-start.1 = (bf16[217,640]{1,0:T(8,128)(2,1)S(1)}, bf16[217,640]{1,0:T(8,128)(2,1)S(1)}, u32[]{:S(2)}, u32[]{:S(2)}) collective-permute-start(bf16[217,640]{1,0:T(8,128)(2,1)S(1)} %get-tuple-element.21), channel_id=1, source_target_pairs={{14,0},{0,2},{2,4},{4,6},{6,8},{8,10},{10,12},{12,14},{15,1},{1,3}... | collective-permute-start | bytes 833288 | tf_op jit(solution)/shard_map/ppermute | solution.py:375
  7.1 10.9 %collective-permute-start.2 = (bf16[64,640]{1,0:T(8,128)(2,1)S(1)}, bf16[64,640]{1,0:T(8,128)(2,1)S(1)}, u32[]{:S(2)}, u32[]{:S(2)}) collective-permute-start(bf16[64,640]{1,0:T(8,128)(2,1)S(1)} %get-tuple-element.23), channel_id=1, source_target_pairs={{8,0},{10,2},{12,4},{14,6},{0,8},{2,10},{4,12},{6,14},{9,1},{11,3}... | collective-permute-start | bytes 245768 | tf_op jit(solution)/shard_map/ppermute | solution.py:375
  7.3 20.2 %collective-permute-start.3 = (bf16[96,640]{1,0:T(8,128)(2,1)S(1)}, bf16[96,640]{1,0:T(8,128)(2,1)S(1)}, u32[]{:S(2)}, u32[]{:S(2)}) collective-permute-start(bf16[96,640]{1,0:T(8,128)(2,1)S(1)} %get-tuple-element.27), channel_id=1, source_target_pairs={{4,0},{6,2},{8,4},{10,6},{12,8},{14,10},{0,12},{2,14},{5,1},{7,3},... | collective-permute-start | bytes 368648 | tf_op jit(solution)/shard_map/ppermute | solution.py:375
  8.6 18.9 %collective-permute-start.4 = (bf16[96,640]{1,0:T(8,128)(2,1)S(1)}, bf16[96,640]{1,0:T(8,128)(2,1)S(1)}, u32[]{:S(2)}, u32[]{:S(2)}) collective-permute-start(bf16[96,640]{1,0:T(8,128)(2,1)S(1)} %get-tuple-element.28), channel_id=1, source_target_pairs={{12,0},{14,2},{0,4},{2,6},{4,8},{6,10},{8,12},{10,14},{13,1},{15,3... | collective-permute-start | bytes 368648 | tf_op jit(solution)/shard_map/ppermute | solution.py:375
  9.3 15.1 %slice-start = ((s8[5734400]{0:T(1024)(128)(4,1)}), s8[4194304]{0:T(1024)(128)(4,1)S(1)}, s32[]{:S(2)}) async-start(s8[5734400]{0:T(1024)(128)(4,1)} %bitcast.12), calls=%async_computation | async-start | bytes 8388608
  9.3 14.9 %copy-start.1 = (bf16[640,16,16]{0,2,1:T(8,128)(2,1)S(1)}, bf16[640,16,16]{0,2,1:T(8,128)(2,1)}, u32[]{:S(2)}) copy-start(bf16[640,16,16]{0,2,1:T(8,128)(2,1)} %param.8) | copy-start | bytes 983044
  9.3 15.0 %copy-start.4 = (f32[640]{0:T(1024)S(1)}, f32[640]{0:T(1024)}, u32[]{:S(2)}) copy-start(f32[640]{0:T(1024)} %param.13) | copy-start | bytes 7684
  9.3 15.1 %slice-start.1 = ((s8[5734400]{0:T(1024)(128)(4,1)}), s8[1540096]{0:T(1024)(128)(4,1)S(1)}, s32[]{:S(2)}) async-start(s8[5734400]{0:T(1024)(128)(4,1)} %bitcast.12), calls=%async_computation.1 | async-start | bytes 3080192
  9.3 15.1 %copy-start.2 = (bf16[640,1280]{1,0:T(8,128)(2,1)S(1)}, bf16[640,1280]{1,0:T(8,128)(2,1)}, u32[]{:S(2)}) copy-start(bf16[640,1280]{1,0:T(8,128)(2,1)} %refs_12_.1) | copy-start | bytes 4915204
  9.3 15.1 %copy-start.3 = (bf16[1280,640]{1,0:T(8,128)(2,1)S(1)}, bf16[1280,640]{1,0:T(8,128)(2,1)}, u32[]{:S(2)}) copy-start(bf16[1280,640]{1,0:T(8,128)(2,1)} %refs_13_.1) | copy-start | bytes 4915204
  18.1 9.5 %collective-permute-start.5 = (bf16[64,640]{1,0:T(8,128)(2,1)S(1)}, bf16[64,640]{1,0:T(8,128)(2,1)S(1)}, u32[]{:S(2)}, u32[]{:S(2)}) collective-permute-start(bf16[64,640]{1,0:T(8,128)(2,1)S(1)} %collective-permute-done.2.refs_7_), channel_id=1, source_target_pairs={{14,0},{0,2},{2,4},{4,6},{6,8},{8,10},{10,12},{12,14},{15,1},{1,3}... | collective-permute-start | bytes 245768 | tf_op jit(solution)/shard_map/ppermute | solution.py:375
  18.1 9.5 %collective-permute-start.6 = (bf16[64,640]{1,0:T(8,128)(2,1)S(1)}, bf16[64,640]{1,0:T(8,128)(2,1)S(1)}, u32[]{:S(2)}, u32[]{:S(2)}) collective-permute-start(bf16[64,640]{1,0:T(8,128)(2,1)S(1)} %collective-permute-done.2.refs_7_), channel_id=1, source_target_pairs={{2,0},{4,2},{6,4},{8,6},{10,8},{12,10},{14,12},{0,14},{3,1},{5,3},... | collective-permute-start | bytes 245768 | tf_op jit(solution)/shard_map/ppermute | solution.py:375
  24.3 3.3 %collective-permute-start.7 = (bf16[32,640]{1,0:T(8,128)(2,1)S(1)}, bf16[32,640]{1,0:T(8,128)(2,1)S(1)}, u32[]{:S(2)}, u32[]{:S(2)}) collective-permute-start(bf16[32,640]{1,0:T(8,128)(2,1)S(1)} %pack_edge_row.1), channel_id=1, source_target_pairs={{0,1},{1,0},{2,3},{3,2},{4,5},{5,4},{6,7},{7,6},{8,9},{9,8},{10,11... | collective-permute-start | bytes 122888 | tf_op jit(solution)/shard_map/ppermute | solution.py:142

commit v7 on v6

--- a/solution.py
+++ b/solution.py
@@ -365,11 +365,15 @@
     x = jnp.transpose(fields, (1, 2, 0))
 
     direct = [m for m in plan.moves if m[0] < half - 1 or m[0] == half]
-    close = [m for m in direct if m[0] == 1]
-    wide = [m for m in direct if m[0] > 1]
-    sent = dict(zip(close, pack(plan, close, x)))
-    later, sent[1, 1], sent[1, -1] = lax.optimization_barrier((x, sent[1, 1], sent[1, -1]))
-    sent.update(zip(wide, pack(plan, wide, later)))
+    order = [[(1, 1)], [(half, 1)], [(1, -1)]]
+    order = [[m for m in group if m in direct] for group in order]
+    order.append([m for m in direct if all(m not in group for group in order)])
+    sent, later = {}, x
+    for group in order:
+        if group:
+            packed = pack(plan, group, later)
+            sent.update(zip(group, packed))
+            later, _ = lax.optimization_barrier((later, packed))
 
     def shifted(value, step):
         return lax.ppermute(value, "lon", [((i + step) % count, i) for i in range(count)])

time: 31 us -> 29.6 us (0.955)
  starting transfers between devices: 14.5 us -> 11.4 us
  waiting for transfers between devices: 4.46 us -> 6.08 us
    ppermute x7, starting transfers between devices: 14.4 us -> 11.4 us  [shifted(): lax.ppermute(value, 'lon', [((i + step) % count, i) for i in range(count)])]
    ppermute x7, waiting for transfers between devices: 4.45 us -> 6.07 us  [shifted(): lax.ppermute(value, 'lon', [((i + step) % count, i) for i in range(count)])]
  transfers between devices with their start and end apart: 8 -> 8, of which waited for: 1 -> 2; matrix products, arithmetic and copies ran while one was open for 0% -> 0% of each run, Pallas kernels for 24% -> 25%
where the time goes in v7:
time: 29.6 us; the launch traced here: 29.4 us
  starting transfers between devices  11.4 us (39%)
  Pallas kernels  10.8 us (36%)
  waiting for transfers between devices  6.08 us (21%)
  local copies, waits for them, and re-layouts  1 us (3%)
    ppermute x7, starting transfers between devices, shifted(): lax.ppermute(value, 'lon', [((i + step) % count, i) for i in range(count)])  11.4 us
    pallas_call x2, Pallas kernels, compute(): pl.pallas_call(functools.partial(compute_body, plan, slots, moves, len(ed...  6.32 us
    ppermute x7, waiting for transfers between devices, shifted(): lax.ppermute(value, 'lon', [((i + step) % count, i) for i in range(count)])  6.07 us
    pallas_call x1, Pallas kernels, make_taps(): pl.pallas_call(functools.partial(taps_body, plan, entries), out_shape=jax...  4.25 us
    unnamed x14, local copies, waits for them, and re-layouts  1 us
  transfers between devices with their start and end apart: 8, of which 2 were waited for; matrix products, arithmetic and copies ran while one was open for 0% of the time, Pallas kernels for 25%

profile of v7, /device:TPU:0, one launch (start us, length us, event | category | flops | bytes accessed | tf_op | source)
XLA Modules:
  0.0 29.4 jit_solution(6118230969529877402)
XLA Ops:
  0.0 0.0 copy-start
  0.0 1.0 %copy-done = bf16[640,16,16]{0,2,1:T(8,128)(2,1)S(1)} copy-done((bf16[640,16,16]{0,2,1:T(8,128)(2,1)S(1)}, bf16[640,16,16]{0,2,1:T(8,128)(2,1)}, u32[]{:S(2)}) %copy-start) | copy-done | bytes 327704
  1.0 0.1 pack_columns.4
  1.0 6.0 %collective-permute-start = (bf16[217,640]{1,0:T(8,128)(2,1)S(1)}, bf16[217,640]{1,0:T(8,128)(2,1)S(1)}, u32[]{:S(2)}, u32[]{:S(2)}) collective-permute-start(bf16[217,640]{1,0:T(8,128)(2,1)S(1)} %pack_columns.4), channel_id=1, source_target_pairs={{2,0},{4,2},{6,4},{8,6},{10,8},{12,10},{14,12},{0,14},{3,1},{5,3},... | collective-permute-start | bytes 833288 | tf_op jit(solution)/shard_map/ppermute | solution.py:379
  7.1 0.1 collective-permute-start.2
  7.1 0.1 pack_columns.6
  7.2 0.1 collective-permute-start.1
  7.4 1.4 %collective-permute-start.3 = (bf16[96,640]{1,0:T(8,128)(2,1)S(1)}, bf16[96,640]{1,0:T(8,128)(2,1)S(1)}, u32[]{:S(2)}, u32[]{:S(2)}) collective-permute-start(bf16[96,640]{1,0:T(8,128)(2,1)S(1)} %get-tuple-element.21), channel_id=1, source_target_pairs={{4,0},{6,2},{8,4},{10,6},{12,8},{14,10},{0,12},{2,14},{5,1},{7,3},... | collective-permute-start | bytes 368648 | tf_op jit(solution)/shard_map/ppermute | solution.py:379
  8.8 0.7 %collective-permute-start.4 = (bf16[96,640]{1,0:T(8,128)(2,1)S(1)}, bf16[96,640]{1,0:T(8,128)(2,1)S(1)}, u32[]{:S(2)}, u32[]{:S(2)}) collective-permute-start(bf16[96,640]{1,0:T(8,128)(2,1)S(1)} %get-tuple-element.22), channel_id=1, source_target_pairs={{12,0},{14,2},{0,4},{2,6},{4,8},{6,10},{8,12},{10,14},{13,1},{15,3... | collective-permute-start | bytes 368648 | tf_op jit(solution)/shard_map/ppermute | solution.py:379
  9.4 0.0 slice-start
  9.5 0.0 copy-start.1
  9.5 0.0 copy-start.4
  9.5 0.0 slice-start.1
  9.5 0.0 copy-start.2
  9.5 0.0 copy-start.3
  9.5 4.3 %filter_taps.1.refs_3_.refs_9_ = bf16[16,112,384]{2,1,0:T(8,128)(2,1)S(1)} custom-call(s32[112,32]{1,0:T(8,128)} %bitcast.23, s32[112,32]{1,0:T(8,128)} %bitcast.24, f32[112,32]{1,0:T(8,128)} %bitcast.25), custom_call_target="tpu_custom_call" | custom-call | flops 3000000000 | bytes 10000000 | tf_op jit(solution)/shard_map/filter_taps/pallas_call | solution.py:211
  13.7 4.4 %collective-permute-done.2.refs_7_ = bf16[64,640]{1,0:T(8,128)(2,1)S(1)} collective-permute-done((bf16[64,640]{1,0:T(8,128)(2,1)S(1)}, bf16[64,640]{1,0:T(8,128)(2,1)S(1)}, u32[]{:S(2)}, u32[]{:S(2)}) %collective-permute-start.2) | collective-permute-done | bytes 81952 | tf_op jit(solution)/shard_map/ppermute | solution.py:379
  18.1 0.0 collective-permute-start.5
  18.1 1.7 %collective-permute-done.1.refs_1_.refs_2_ = bf16[217,640]{1,0:T(8,128)(2,1)S(1)} collective-permute-done((bf16[217,640]{1,0:T(8,128)(2,1)S(1)}, bf16[217,640]{1,0:T(8,128)(2,1)S(1)}, u32[]{:S(2)}, u32[]{:S(2)}) %collective-permute-start.1) | collective-permute-done | bytes 277792 | tf_op jit(solution)/shard_map/ppermute | solution.py:379
  19.8 3.1 %collective-permute-start.6 = (bf16[64,640]{1,0:T(8,128)(2,1)S(1)}, bf16[64,640]{1,0:T(8,128)(2,1)S(1)}, u32[]{:S(2)}, u32[]{:S(2)}) collective-permute-start(bf16[64,640]{1,0:T(8,128)(2,1)S(1)} %collective-permute-done.2.refs_7_), channel_id=1, source_target_pairs={{2,0},{4,2},{6,4},{8,6},{10,8},{12,10},{14,12},{0,14},{3,1},{5,3},... | collective-permute-start | bytes 245768 | tf_op jit(solution)/shard_map/ppermute | solution.py:379
  22.9 0.0 collective-permute-done.refs_0_.refs_1_
  22.9 0.0 copy-done.1
  22.9 0.1 collective-permute-start.7
  23.0 0.0 copy-done.4
  23.0 0.0 slice-done
  23.0 0.0 slice-done.1
  23.0 0.0 copy-done.2
  23.0 0.0 copy-done.3
  23.0 3.1 %filter_mix_mlp.2.refs_14_ = bf16[16,16,640]{2,1,0:T(8,128)(2,1)} custom-call(bf16[16,16,640]{2,1,0:T(8,128)(2,1)S(1)} %bitcast.21, bf16[217,640]{1,0:T(8,128)(2,1)S(1)} %collective-permute-done.refs_0_.refs_1_, bf16[217,640]{1,0:T(8,128)(2,1)S(1)} %collective-permute-done.1.refs_1_.refs_2_, bf16[16,112,384]{2,1,0:T(8,128)(2,1)S(1)} %filter_taps.1.refs_3_.refs_9_, ...), custom_call_target="tpu_custom_call" | custom-call | flops 1000000 | bytes 100000 | tf_op jit(solution)/shard_map/filter_mix_mlp/pallas_call | solution.py:333
  26.1 0.0 collective-permute-done.3.refs_3_
  26.2 0.0 collective-permute-done.4.refs_4_
  26.2 0.0 collective-permute-done.5.refs_5_
  26.2 0.0 collective-permute-done.6.refs_6_
  26.2 0.0 collective-permute-done.7.refs_8_
  26.2 3.2 %filter_mix_mlp.3 = bf16[16,16,640]{2,1,0:T(8,128)(2,1)} custom-call(bf16[16,16,640]{2,1,0:T(8,128)(2,1)S(1)} %bitcast.22, bf16[217,640]{1,0:T(8,128)(2,1)S(1)} %collective-permute-done.refs_0_.refs_1_, bf16[217,640]{1,0:T(8,128)(2,1)S(1)} %collective-permute-done.1.refs_1_.refs_2_, ...), custom_call_target="tpu_custom_call", output_to_operand_aliasing={{}: (14, {})} | custom-call | flops 1000000 | bytes 100000 | tf_op jit(solution)/shard_map/filter_mix_mlp/pallas_call | solution.py:333
  (5 shorter events, 0.1 us)
Async XLA Ops:
  0.0 1.0 %copy-start = (bf16[640,16,16]{0,2,1:T(8,128)(2,1)S(1)}, bf16[640,16,16]{0,2,1:T(8,128)(2,1)}, u32[]{:S(2)}) copy-start(bf16[640,16,16]{0,2,1:T(8,128)(2,1)} %param.8) | copy-start | bytes 983044
  1.0 21.8 %collective-permute-start = (bf16[217,640]{1,0:T(8,128)(2,1)S(1)}, bf16[217,640]{1,0:T(8,128)(2,1)S(1)}, u32[]{:S(2)}, u32[]{:S(2)}) collective-permute-start(bf16[217,640]{1,0:T(8,128)(2,1)S(1)} %pack_columns.4), channel_id=1, source_target_pairs={{2,0},{4,2},{6,4},{8,6},{10,8},{12,10},{14,12},{0,14},{3,1},{5,3},... | collective-permute-start | bytes 833288 | tf_op jit(solution)/shard_map/ppermute | solution.py:379
  7.1 11.1 %collective-permute-start.2 = (bf16[64,640]{1,0:T(8,128)(2,1)S(1)}, bf16[64,640]{1,0:T(8,128)(2,1)S(1)}, u32[]{:S(2)}, u32[]{:S(2)}) collective-permute-start(bf16[64,640]{1,0:T(8,128)(2,1)S(1)} %pack_columns.5), channel_id=1, source_target_pairs={{8,0},{10,2},{12,4},{14,6},{0,8},{2,10},{4,12},{6,14},{9,1},{11,3}... | collective-permute-start | bytes 245768 | tf_op jit(solution)/shard_map/ppermute | solution.py:379
  7.2 12.6 %collective-permute-start.1 = (bf16[217,640]{1,0:T(8,128)(2,1)S(1)}, bf16[217,640]{1,0:T(8,128)(2,1)S(1)}, u32[]{:S(2)}, u32[]{:S(2)}) collective-permute-start(bf16[217,640]{1,0:T(8,128)(2,1)S(1)} %pack_columns.6), channel_id=1, source_target_pairs={{14,0},{0,2},{2,4},{4,6},{6,8},{8,10},{10,12},{12,14},{15,1},{1,3}... | collective-permute-start | bytes 833288 | tf_op jit(solution)/shard_map/ppermute | solution.py:379
  7.4 18.8 %collective-permute-start.3 = (bf16[96,640]{1,0:T(8,128)(2,1)S(1)}, bf16[96,640]{1,0:T(8,128)(2,1)S(1)}, u32[]{:S(2)}, u32[]{:S(2)}) collective-permute-start(bf16[96,640]{1,0:T(8,128)(2,1)S(1)} %get-tuple-element.21), channel_id=1, source_target_pairs={{4,0},{6,2},{8,4},{10,6},{12,8},{14,10},{0,12},{2,14},{5,1},{7,3},... | collective-permute-start | bytes 368648 | tf_op jit(solution)/shard_map/ppermute | solution.py:379
  8.8 17.4 %collective-permute-start.4 = (bf16[96,640]{1,0:T(8,128)(2,1)S(1)}, bf16[96,640]{1,0:T(8,128)(2,1)S(1)}, u32[]{:S(2)}, u32[]{:S(2)}) collective-permute-start(bf16[96,640]{1,0:T(8,128)(2,1)S(1)} %get-tuple-element.22), channel_id=1, source_target_pairs={{12,0},{14,2},{0,4},{2,6},{4,8},{6,10},{8,12},{10,14},{13,1},{15,3... | collective-permute-start | bytes 368648 | tf_op jit(solution)/shard_map/ppermute | solution.py:379
  9.4 13.6 %slice-start = ((s8[5734400]{0:T(1024)(128)(4,1)}), s8[4194304]{0:T(1024)(128)(4,1)S(1)}, s32[]{:S(2)}) async-start(s8[5734400]{0:T(1024)(128)(4,1)} %bitcast.12), calls=%async_computation | async-start | bytes 8388608
  9.5 13.4 %copy-start.1 = (bf16[640,16,16]{0,2,1:T(8,128)(2,1)S(1)}, bf16[640,16,16]{0,2,1:T(8,128)(2,1)}, u32[]{:S(2)}) copy-start(bf16[640,16,16]{0,2,1:T(8,128)(2,1)} %param.8) | copy-start | bytes 983044
  9.5 13.5 %copy-start.4 = (f32[640]{0:T(1024)S(1)}, f32[640]{0:T(1024)}, u32[]{:S(2)}) copy-start(f32[640]{0:T(1024)} %param.13) | copy-start | bytes 7684
  9.5 13.6 %slice-start.1 = ((s8[5734400]{0:T(1024)(128)(4,1)}), s8[1540096]{0:T(1024)(128)(4,1)S(1)}, s32[]{:S(2)}) async-start(s8[5734400]{0:T(1024)(128)(4,1)} %bitcast.12), calls=%async_computation.1 | async-start | bytes 3080192
  9.5 13.6 %copy-start.2 = (bf16[640,1280]{1,0:T(8,128)(2,1)S(1)}, bf16[640,1280]{1,0:T(8,128)(2,1)}, u32[]{:S(2)}) copy-start(bf16[640,1280]{1,0:T(8,128)(2,1)} %refs_12_.1) | copy-start | bytes 4915204
  9.5 13.6 %copy-start.3 = (bf16[1280,640]{1,0:T(8,128)(2,1)S(1)}, bf16[1280,640]{1,0:T(8,128)(2,1)}, u32[]{:S(2)}) copy-start(bf16[1280,640]{1,0:T(8,128)(2,1)} %refs_13_.1) | copy-start | bytes 4915204
  18.1 8.0 %collective-permute-start.5 = (bf16[64,640]{1,0:T(8,128)(2,1)S(1)}, bf16[64,640]{1,0:T(8,128)(2,1)S(1)}, u32[]{:S(2)}, u32[]{:S(2)}) collective-permute-start(bf16[64,640]{1,0:T(8,128)(2,1)S(1)} %collective-permute-done.2.refs_7_), channel_id=1, source_target_pairs={{14,0},{0,2},{2,4},{4,6},{6,8},{8,10},{10,12},{12,14},{15,1},{1,3}... | collective-permute-start | bytes 245768 | tf_op jit(solution)/shard_map/ppermute | solution.py:379
  19.8 6.4 %collective-permute-start.6 = (bf16[64,640]{1,0:T(8,128)(2,1)S(1)}, bf16[64,640]{1,0:T(8,128)(2,1)S(1)}, u32[]{:S(2)}, u32[]{:S(2)}) collective-permute-start(bf16[64,640]{1,0:T(8,128)(2,1)S(1)} %collective-permute-done.2.refs_7_), channel_id=1, source_target_pairs={{2,0},{4,2},{6,4},{8,6},{10,8},{12,10},{14,12},{0,14},{3,1},{5,3},... | collective-permute-start | bytes 245768 | tf_op jit(solution)/shard_map/ppermute | solution.py:379
  22.9 3.3 %collective-permute-start.7 = (bf16[32,640]{1,0:T(8,128)(2,1)S(1)}, bf16[32,640]{1,0:T(8,128)(2,1)S(1)}, u32[]{:S(2)}, u32[]{:S(2)}) collective-permute-start(bf16[32,640]{1,0:T(8,128)(2,1)S(1)} %pack_edge_row.1), channel_id=1, source_target_pairs={{0,1},{1,0},{2,3},{3,2},{4,5},{5,4},{6,7},{7,6},{8,9},{9,8},{10,11... | collective-permute-start | bytes 122888 | tf_op jit(solution)/shard_map/ppermute | solution.py:142

commit v8 on v7

--- a/solution.py
+++ b/solution.py
@@ -381,11 +381,11 @@
     got = {m: shifted(sent[m], m[0] * m[1]) for m in direct}
     forward = (half - 1, 1) in plan.moves and half > 2
     if forward:
-        got[half - 1, 1] = shifted(got[half, 1], -1)
+        got[half - 1, -1] = shifted(got[half, 1], 1)
     taps = make_taps(plan, (support_rows, support_lons, support_weights))
     if forward:
         opposite, taps = lax.optimization_barrier((got[half, 1], taps))
-        got[half - 1, -1] = shifted(opposite, 1)
+        got[half - 1, 1] = shifted(opposite, -1)
     first = [m for m in got if m[0] <= plan.margin_blocks]
     joined, taps = lax.optimization_barrier(([got[m] for m in first], taps))
     got.update(zip(first, joined))

time: 29.6 us -> 31.4 us (1.061)
  waiting for transfers between devices: 6.08 us -> 8.89 us
  starting transfers between devices: 11.4 us -> 10.4 us
    ppermute x7, waiting for transfers between devices: 6.07 us -> 8.89 us  [shifted(): lax.ppermute(value, 'lon', [((i + step) % count, i) for i in range(count)])]
    ppermute x7, starting transfers between devices: 11.4 us -> 10.3 us  [shifted(): lax.ppermute(value, 'lon', [((i + step) % count, i) for i in range(count)])]
  transfers between devices with their start and end apart: 8 -> 8, of which waited for: 2 -> 2; matrix products, arithmetic and copies ran while one was open for 0% -> 0% of each run, Pallas kernels for 25% -> 24%
where the time goes in v8:
time: 31.4 us; the launch traced here: 31.2 us
  Pallas kernels  10.8 us (34%)
  starting transfers between devices  10.4 us (33%)
  waiting for transfers between devices  8.89 us (28%)
  local copies, waits for them, and re-layouts  1 us (3%)
    ppermute x7, starting transfers between devices, shifted(): lax.ppermute(value, 'lon', [((i + step) % count, i) for i in range(count)])  10.3 us
    ppermute x7, waiting for transfers between devices, shifted(): lax.ppermute(value, 'lon', [((i + step) % count, i) for i in range(count)])  8.89 us
    pallas_call x2, Pallas kernels, compute(): pl.pallas_call(functools.partial(compute_body, plan, slots, moves, len(ed...  6.32 us
    pallas_call x1, Pallas kernels, make_taps(): pl.pallas_call(functools.partial(taps_body, plan, entries), out_shape=jax...  4.25 us
    unnamed x14, local copies, waits for them, and re-layouts  1 us
  transfers between devices with their start and end apart: 8, of which 2 were waited for; matrix products, arithmetic and copies ran while one was open for 0% of the time, Pallas kernels for 24%

profile of v8, /device:TPU:0, one launch (start us, length us, event | category | flops | bytes accessed | tf_op | source)
XLA Modules:
  0.0 31.2 jit_solution(13695126131183417828)
XLA Ops:
  0.0 0.0 copy-start
  0.0 1.0 %copy-done = bf16[640,16,16]{0,2,1:T(8,128)(2,1)S(1)} copy-done((bf16[640,16,16]{0,2,1:T(8,128)(2,1)S(1)}, bf16[640,16,16]{0,2,1:T(8,128)(2,1)}, u32[]{:S(2)}) %copy-start) | copy-done | bytes 327704
  1.0 0.1 pack_columns.4
  1.0 6.0 %collective-permute-start = (bf16[217,640]{1,0:T(8,128)(2,1)S(1)}, bf16[217,640]{1,0:T(8,128)(2,1)S(1)}, u32[]{:S(2)}, u32[]{:S(2)}) collective-permute-start(bf16[217,640]{1,0:T(8,128)(2,1)S(1)} %pack_columns.4), channel_id=1, source_target_pairs={{2,0},{4,2},{6,4},{8,6},{10,8},{12,10},{14,12},{0,14},{3,1},{5,3},... | collective-permute-start | bytes 833288 | tf_op jit(solution)/shard_map/ppermute | solution.py:379
  7.1 0.1 collective-permute-start.2
  7.1 0.1 pack_columns.6
  7.2 0.1 collective-permute-start.1
  7.4 1.4 %collective-permute-start.3 = (bf16[96,640]{1,0:T(8,128)(2,1)S(1)}, bf16[96,640]{1,0:T(8,128)(2,1)S(1)}, u32[]{:S(2)}, u32[]{:S(2)}) collective-permute-start(bf16[96,640]{1,0:T(8,128)(2,1)S(1)} %get-tuple-element.21), channel_id=1, source_target_pairs={{4,0},{6,2},{8,4},{10,6},{12,8},{14,10},{0,12},{2,14},{5,1},{7,3},... | collective-permute-start | bytes 368648 | tf_op jit(solution)/shard_map/ppermute | solution.py:379
  8.8 0.7 %collective-permute-start.4 = (bf16[96,640]{1,0:T(8,128)(2,1)S(1)}, bf16[96,640]{1,0:T(8,128)(2,1)S(1)}, u32[]{:S(2)}, u32[]{:S(2)}) collective-permute-start(bf16[96,640]{1,0:T(8,128)(2,1)S(1)} %get-tuple-element.22), channel_id=1, source_target_pairs={{12,0},{14,2},{0,4},{2,6},{4,8},{6,10},{8,12},{10,14},{13,1},{15,3... | collective-permute-start | bytes 368648 | tf_op jit(solution)/shard_map/ppermute | solution.py:379
  9.4 0.0 slice-start
  9.5 0.0 copy-start.1
  9.5 0.0 copy-start.4
  9.5 0.0 slice-start.1
  9.5 0.0 copy-start.2
  9.5 0.0 copy-start.3
  9.5 4.3 %filter_taps.1.refs_3_.refs_9_ = bf16[16,112,384]{2,1,0:T(8,128)(2,1)S(1)} custom-call(s32[112,32]{1,0:T(8,128)} %bitcast.23, s32[112,32]{1,0:T(8,128)} %bitcast.24, f32[112,32]{1,0:T(8,128)} %bitcast.25), custom_call_target="tpu_custom_call" | custom-call | flops 3000000000 | bytes 10000000 | tf_op jit(solution)/shard_map/filter_taps/pallas_call | solution.py:211
  13.7 4.5 %collective-permute-done.2.refs_7_ = bf16[64,640]{1,0:T(8,128)(2,1)S(1)} collective-permute-done((bf16[64,640]{1,0:T(8,128)(2,1)S(1)}, bf16[64,640]{1,0:T(8,128)(2,1)S(1)}, u32[]{:S(2)}, u32[]{:S(2)}) %collective-permute-start.2) | collective-permute-done | bytes 81952 | tf_op jit(solution)/shard_map/ppermute | solution.py:379
  18.2 2.0 %collective-permute-start.6 = (bf16[64,640]{1,0:T(8,128)(2,1)S(1)}, bf16[64,640]{1,0:T(8,128)(2,1)S(1)}, u32[]{:S(2)}, u32[]{:S(2)}) collective-permute-start(bf16[64,640]{1,0:T(8,128)(2,1)S(1)} %collective-permute-done.2.refs_7_), channel_id=1, source_target_pairs={{2,0},{4,2},{6,4},{8,6},{10,8},{12,10},{14,12},{0,14},{3,1},{5,3},... | collective-permute-start | bytes 245768 | tf_op jit(solution)/shard_map/ppermute | solution.py:379
  20.3 0.0 collective-permute-done.1.refs_1_.refs_2_
  20.3 0.0 collective-permute-start.5
  20.3 0.0 collective-permute-done.refs_0_.refs_1_
  20.3 0.0 copy-done.1
  20.3 0.1 collective-permute-start.7
  20.4 0.0 copy-done.4
  20.4 0.0 slice-done
  20.4 0.0 slice-done.1
  20.4 0.0 copy-done.2
  20.4 0.0 copy-done.3
  20.5 3.1 %filter_mix_mlp.2.refs_14_ = bf16[16,16,640]{2,1,0:T(8,128)(2,1)} custom-call(bf16[16,16,640]{2,1,0:T(8,128)(2,1)S(1)} %bitcast.21, bf16[217,640]{1,0:T(8,128)(2,1)S(1)} %collective-permute-done.refs_0_.refs_1_, bf16[217,640]{1,0:T(8,128)(2,1)S(1)} %collective-permute-done.1.refs_1_.refs_2_, bf16[16,112,384]{2,1,0:T(8,128)(2,1)S(1)} %filter_taps.1.refs_3_.refs_9_, ...), custom_call_target="tpu_custom_call" | custom-call | flops 1000000 | bytes 100000 | tf_op jit(solution)/shard_map/filter_mix_mlp/pallas_call | solution.py:333
  23.6 0.0 collective-permute-done.3.refs_3_
  23.6 0.0 collective-permute-done.4.refs_4_
  23.6 0.0 collective-permute-done.6.refs_6_
  23.6 4.4 %collective-permute-done.5.refs_5_ = bf16[64,640]{1,0:T(8,128)(2,1)S(1)} collective-permute-done((bf16[64,640]{1,0:T(8,128)(2,1)S(1)}, bf16[64,640]{1,0:T(8,128)(2,1)S(1)}, u32[]{:S(2)}, u32[]{:S(2)}) %collective-permute-start.5) | collective-permute-done | bytes 81952 | tf_op jit(solution)/shard_map/ppermute | solution.py:379
  28.0 0.0 collective-permute-done.7.refs_8_
  28.0 3.2 %filter_mix_mlp.3 = bf16[16,16,640]{2,1,0:T(8,128)(2,1)} custom-call(bf16[16,16,640]{2,1,0:T(8,128)(2,1)S(1)} %bitcast.22, bf16[217,640]{1,0:T(8,128)(2,1)S(1)} %collective-permute-done.refs_0_.refs_1_, bf16[217,640]{1,0:T(8,128)(2,1)S(1)} %collective-permute-done.1.refs_1_.refs_2_, ...), custom_call_target="tpu_custom_call", output_to_operand_aliasing={{}: (14, {})} | custom-call | flops 1000000 | bytes 100000 | tf_op jit(solution)/shard_map/filter_mix_mlp/pallas_call | solution.py:333
  (5 shorter events, 0.1 us)
Async XLA Ops:
  0.0 1.0 %copy-start = (bf16[640,16,16]{0,2,1:T(8,128)(2,1)S(1)}, bf16[640,16,16]{0,2,1:T(8,128)(2,1)}, u32[]{:S(2)}) copy-start(bf16[640,16,16]{0,2,1:T(8,128)(2,1)} %param.8) | copy-start | bytes 983044
  1.0 19.2 %collective-permute-start = (bf16[217,640]{1,0:T(8,128)(2,1)S(1)}, bf16[217,640]{1,0:T(8,128)(2,1)S(1)}, u32[]{:S(2)}, u32[]{:S(2)}) collective-permute-start(bf16[217,640]{1,0:T(8,128)(2,1)S(1)} %pack_columns.4), channel_id=1, source_target_pairs={{2,0},{4,2},{6,4},{8,6},{10,8},{12,10},{14,12},{0,14},{3,1},{5,3},... | collective-permute-start | bytes 833288 | tf_op jit(solution)/shard_map/ppermute | solution.py:379
  7.1 11.2 %collective-permute-start.2 = (bf16[64,640]{1,0:T(8,128)(2,1)S(1)}, bf16[64,640]{1,0:T(8,128)(2,1)S(1)}, u32[]{:S(2)}, u32[]{:S(2)}) collective-permute-start(bf16[64,640]{1,0:T(8,128)(2,1)S(1)} %pack_columns.5), channel_id=1, source_target_pairs={{8,0},{10,2},{12,4},{14,6},{0,8},{2,10},{4,12},{6,14},{9,1},{11,3}... | collective-permute-start | bytes 245768 | tf_op jit(solution)/shard_map/ppermute | solution.py:379
  7.2 13.0 %collective-permute-start.1 = (bf16[217,640]{1,0:T(8,128)(2,1)S(1)}, bf16[217,640]{1,0:T(8,128)(2,1)S(1)}, u32[]{:S(2)}, u32[]{:S(2)}) collective-permute-start(bf16[217,640]{1,0:T(8,128)(2,1)S(1)} %pack_columns.6), channel_id=1, source_target_pairs={{14,0},{0,2},{2,4},{4,6},{6,8},{8,10},{10,12},{12,14},{15,1},{1,3}... | collective-permute-start | bytes 833288 | tf_op jit(solution)/shard_map/ppermute | solution.py:379
  7.4 16.2 %collective-permute-start.3 = (bf16[96,640]{1,0:T(8,128)(2,1)S(1)}, bf16[96,640]{1,0:T(8,128)(2,1)S(1)}, u32[]{:S(2)}, u32[]{:S(2)}) collective-permute-start(bf16[96,640]{1,0:T(8,128)(2,1)S(1)} %get-tuple-element.21), channel_id=1, source_target_pairs={{4,0},{6,2},{8,4},{10,6},{12,8},{14,10},{0,12},{2,14},{5,1},{7,3},... | collective-permute-start | bytes 368648 | tf_op jit(solution)/shard_map/ppermute | solution.py:379
  8.8 14.8 %collective-permute-start.4 = (bf16[96,640]{1,0:T(8,128)(2,1)S(1)}, bf16[96,640]{1,0:T(8,128)(2,1)S(1)}, u32[]{:S(2)}, u32[]{:S(2)}) collective-permute-start(bf16[96,640]{1,0:T(8,128)(2,1)S(1)} %get-tuple-element.22), channel_id=1, source_target_pairs={{12,0},{14,2},{0,4},{2,6},{4,8},{6,10},{8,12},{10,14},{13,1},{15,3... | collective-permute-start | bytes 368648 | tf_op jit(solution)/shard_map/ppermute | solution.py:379
  9.4 11.0 %slice-start = ((s8[5734400]{0:T(1024)(128)(4,1)}), s8[4194304]{0:T(1024)(128)(4,1)S(1)}, s32[]{:S(2)}) async-start(s8[5734400]{0:T(1024)(128)(4,1)} %bitcast.12), calls=%async_computation | async-start | bytes 8388608
  9.5 10.8 %copy-start.1 = (bf16[640,16,16]{0,2,1:T(8,128)(2,1)S(1)}, bf16[640,16,16]{0,2,1:T(8,128)(2,1)}, u32[]{:S(2)}) copy-start(bf16[640,16,16]{0,2,1:T(8,128)(2,1)} %param.8) | copy-start | bytes 983044
  9.5 10.9 %copy-start.4 = (f32[640]{0:T(1024)S(1)}, f32[640]{0:T(1024)}, u32[]{:S(2)}) copy-start(f32[640]{0:T(1024)} %param.13) | copy-start | bytes 7684
  9.5 11.0 %slice-start.1 = ((s8[5734400]{0:T(1024)(128)(4,1)}), s8[1540096]{0:T(1024)(128)(4,1)S(1)}, s32[]{:S(2)}) async-start(s8[5734400]{0:T(1024)(128)(4,1)} %bitcast.12), calls=%async_computation.1 | async-start | bytes 3080192
  9.5 11.0 %copy-start.2 = (bf16[640,1280]{1,0:T(8,128)(2,1)S(1)}, bf16[640,1280]{1,0:T(8,128)(2,1)}, u32[]{:S(2)}) copy-start(bf16[640,1280]{1,0:T(8,128)(2,1)} %refs_12_.1) | copy-start | bytes 4915204
  9.5 11.0 %copy-start.3 = (bf16[1280,640]{1,0:T(8,128)(2,1)S(1)}, bf16[1280,640]{1,0:T(8,128)(2,1)}, u32[]{:S(2)}) copy-start(bf16[1280,640]{1,0:T(8,128)(2,1)} %refs_13_.1) | copy-start | bytes 4915204
  18.2 5.4 %collective-permute-start.6 = (bf16[64,640]{1,0:T(8,128)(2,1)S(1)}, bf16[64,640]{1,0:T(8,128)(2,1)S(1)}, u32[]{:S(2)}, u32[]{:S(2)}) collective-permute-start(bf16[64,640]{1,0:T(8,128)(2,1)S(1)} %collective-permute-done.2.refs_7_), channel_id=1, source_target_pairs={{2,0},{4,2},{6,4},{8,6},{10,8},{12,10},{14,12},{0,14},{3,1},{5,3},... | collective-permute-start | bytes 245768 | tf_op jit(solution)/shard_map/ppermute | solution.py:379
  20.3 7.7 %collective-permute-start.5 = (bf16[64,640]{1,0:T(8,128)(2,1)S(1)}, bf16[64,640]{1,0:T(8,128)(2,1)S(1)}, u32[]{:S(2)}, u32[]{:S(2)}) collective-permute-start(bf16[64,640]{1,0:T(8,128)(2,1)S(1)} %collective-permute-done.2.refs_7_), channel_id=1, source_target_pairs={{14,0},{0,2},{2,4},{4,6},{6,8},{8,10},{10,12},{12,14},{15,1},{1,3}... | collective-permute-start | bytes 245768 | tf_op jit(solution)/shard_map/ppermute | solution.py:379
  20.3 7.7 %collective-permute-start.7 = (bf16[32,640]{1,0:T(8,128)(2,1)S(1)}, bf16[32,640]{1,0:T(8,128)(2,1)S(1)}, u32[]{:S(2)}, u32[]{:S(2)}) collective-permute-start(bf16[32,640]{1,0:T(8,128)(2,1)S(1)} %pack_edge_row.1), channel_id=1, source_target_pairs={{0,1},{1,0},{2,3},{3,2},{4,5},{5,4},{6,7},{7,6},{8,9},{9,8},{10,11... | collective-permute-start | bytes 122888 | tf_op jit(solution)/shard_map/ppermute | solution.py:142
